TPU v7x, 512 devices: a whole 4x8x8 slice. The times are simulated.
512 devices in a mesh: op: 64 (over x, z, core), sec: 8 (over y).
Axes of the slice: x: 4, y: 8, z: 8, core: 2. Of those that a mesh axis runs over, the one named last changes fastest.
Arguments:
- psi: float32 [640, 8, 640], P('op', 'sec'), may hold values from -6 to 6
- left_env: float32 [64, 8, 640, 640], P('op', 'sec'), may hold values from -0.25 to 0.25
- right_env: float32 [64, 8, 640, 640], P('op', 'sec'), may hold values from -0.03125 to 0.03125
- denominators: float32 [640, 8, 640], P('op', 'sec'), may hold values from 0.5 to 4
- source_sector: int32 [64, 8], replicated, may hold values from 0 to 7
- owner: int32 [8], replicated, may hold values from 0 to 7, each once
- orders: int32 [8], replicated, may hold values from 480 to 640
Outputs:
- new_vector: float32 [640, 8, 640], P('op', 'sec')
- correction: float32 [640, 8, 640], P('op', 'sec')
Inputs may be any that keep to these rules, and one draw needn't show every extreme that they name: `source_sector`: entry (t, s) is the sector from which term t maps into sector s. `owner`: each sector's slot; every slot holds one sector. Only the first orders rows and columns of a sector's block count; the inputs may hold any values beyond them, and the mask removes those entries.
All inputs are finite; a program needn't handle non-finite values.
Results may differ from a plain program's by a relative error of at most 0.0003.
Values sent between devices are 32-bit elements; how exact they have to be, the bound alone decides.
No kernel may reach another device: no remote copies, remote signals or barrier semaphores. Data moves between devices by JAX's collectives and lax.ppermute only.
A program may use at most 64 MiB of HBM per device.

v0:
```python
import functools

import jax
import jax.numpy as jnp
from jax import lax
from jax.experimental import pallas as pl
from jax.experimental.pallas import tpu as pltpu
from jax.sharding import Mesh
from jax.sharding import PartitionSpec as P

CHIP = ("op_0", "op_1")
OP = ("op_0", "op_1", "op_2")
EPS = 1e-06
LANES = 128
VMEM = pl.BlockSpec(memory_space=pltpu.VMEM)
SMEM = pl.BlockSpec(memory_space=pltpu.SMEM)


def up8(n):
    return -(-n // 8) * 8


def op_position():
    sizes = [lax.axis_size(a) for a in OP]
    return (lax.axis_index("op_0") * sizes[1] + lax.axis_index("op_1")) * sizes[2] + lax.axis_index("op_2")


def sector_at(owner_ref, slot, nsec):
    found = jnp.int32(0)
    for s in range(nsec):
        found = found + jnp.where(owner_ref[s] == slot, s, 0)
    return found


def row_mask(order, lines, per_row, first_row):
    line = lax.broadcasted_iota(jnp.int32, (lines, LANES), 0)
    lane = lax.broadcasted_iota(jnp.int32, (lines, LANES), 1)
    row = line // per_row
    col = (line - row * per_row) * LANES + lane
    return (first_row + row < order) & (col < order)


def total(x):
    return jnp.sum(jnp.sum(x, axis=0, keepdims=True), axis=1, keepdims=True)


def lane_row(values):
    lane = lax.broadcasted_iota(jnp.int32, (1, LANES), 1)
    out = jnp.zeros((1, LANES), jnp.float32)
    for i, v in enumerate(values):
        out = jnp.where(lane == i, v, out)
    return out


def prep_kernel(per_row, nsec, pad, owner_ref, orders_ref, psi_ref, den_ref, v_ref, out_ref):
    lines = psi_ref.shape[0]
    rows = lines // per_row
    order = orders_ref[sector_at(owner_ref, lax.axis_index("sec"), nsec)]
    keep = row_mask(order, lines, per_row, op_position() * rows)
    v = jnp.where(keep, psi_ref[...], 0.0)
    d = den_ref[...]
    v_ref[...] = v
    for y in range(nsec):
        out_ref[2 * y * pad : 2 * y * pad + lines, :] = v
        out_ref[(2 * y + 1) * pad : (2 * y + 1) * pad + lines, :] = d
        if pad > lines:
            out_ref[2 * y * pad + lines : (2 * y + 1) * pad, :] = jnp.zeros((pad - lines, LANES), jnp.float32)
            out_ref[(2 * y + 1) * pad + lines : (2 * y + 2) * pad, :] = jnp.ones((pad - lines, LANES), jnp.float32)


def spread(table_ref, owner_ref, source_ref, out_ref, lines, pitch, nsec):
    sector = sector_at(owner_ref, lax.axis_index("sec"), nsec)
    for t in range(out_ref.shape[0] // lines):
        slot = owner_ref[source_ref[sector, t]]
        start = pl.multiple_of(slot * pitch, 8)
        out_ref[t * lines : (t + 1) * lines, :] = table_ref[pl.ds(start, lines), :]


def select_kernel(lines, pad, nsec, owner_ref, source_ref, vd_ref, out_ref):
    spread(vd_ref, owner_ref, source_ref, out_ref, lines, 2 * pad, nsec)


def halves(x):
    hi = x.astype(jnp.bfloat16)
    return hi, (x - hi.astype(jnp.float32)).astype(jnp.bfloat16)


def dot3(a_hi, a_lo, b_hi, b_lo):
    dot = functools.partial(jnp.dot, preferred_element_type=jnp.float32)
    return dot(a_hi, b_hi) + (dot(a_hi, b_lo) + dot(a_lo, b_hi))


def split_kernel(rows, left_ref, right_ref, lh_ref, ll_ref, rh_ref, rl_ref, order_ref):
    width = left_ref.shape[0]
    half = width // 2
    mine = lax.axis_index("op_2") == 0
    for q in range(width // (2 * rows)):
        a = left_ref[2 * q * rows : (2 * q + 1) * rows, :]
        b = left_ref[(2 * q + 1) * rows : (2 * q + 2) * rows, :]
        order_ref[q * rows : (q + 1) * rows, :] = jnp.where(mine, b, a)
        order_ref[half + q * rows : half + (q + 1) * rows, :] = jnp.where(mine, a, b)
    step = 160

    def body(m, carry):
        at = pl.ds(pl.multiple_of(m * step, step), step)
        lh_ref[at, :], ll_ref[at, :] = halves(order_ref[at, :])
        rh_ref[at, :], rl_ref[at, :] = halves(right_ref[at, :])
        return carry

    lax.fori_loop(0, width // step, body, 0)


def left_product(lh_ref, ll_ref, ih_ref, il_ref, out_ref, first, per_row):
    step = 160
    for m in range(out_ref.shape[0] // per_row // step):
        at = pl.ds(first + m * step, step)
        y = dot3(lh_ref[at, :], ll_ref[at, :], ih_ref[...], il_ref[...])
        for k in range(per_row):
            out_ref[pl.ds(m * step * per_row + k, step, stride=per_row), :] = y[:, k * LANES : (k + 1) * LANES]


def inner_kernel(per_row, x_ref, rh_ref, rl_ref, lh_ref, ll_ref, ih_ref, il_ref, out_ref):
    width = rh_ref.shape[0]
    step = 160
    for m in range(width // step):
        x = jnp.concatenate(
            [x_ref[pl.ds(m * step * per_row + k, step, stride=per_row), :] for k in range(per_row)], axis=1
        )
        x_hi, x_lo = halves(x)
        at = pl.ds(m * step, step)
        ih_ref[at, :], il_ref[at, :] = halves(dot3(x_hi, x_lo, rh_ref[...], rl_ref[...]))
    left_product(lh_ref, ll_ref, ih_ref, il_ref, out_ref, 0, per_row)


def own_kernel(per_row, lh_ref, ll_ref, ih_ref, il_ref, out_ref):
    left_product(lh_ref, ll_ref, ih_ref, il_ref, out_ref, lh_ref.shape[0] // 2, per_row)


def masked_sum(part_ref, owner_ref, orders_ref, lines, per_row, nsec):
    parts = part_ref.shape[0] // lines
    w = part_ref[0:lines, :]
    for q in range(1, parts):
        w = w + part_ref[q * lines : (q + 1) * lines, :]
    order = orders_ref[sector_at(owner_ref, lax.axis_index("sec"), nsec)]
    keep = row_mask(order, lines, per_row, op_position() * (lines // per_row))
    return jnp.where(keep, w, 0.0)


def share_kernel(lines, pad, per_row, nsec, owner_ref, orders_ref, part_ref, w_ref, out_ref):
    w = masked_sum(part_ref, owner_ref, orders_ref, lines, per_row, nsec)
    w_ref[...] = w
    for y in range(nsec):
        out_ref[y * pad : y * pad + lines, :] = w
        if pad > lines:
            out_ref[y * pad + lines : (y + 1) * pad, :] = jnp.zeros((pad - lines, LANES), jnp.float32)


def first_sums_kernel(pad, nsec, vd_ref, w8_ref, out_ref):
    vv = jnp.zeros((pad, LANES), jnp.float32)
    vw = jnp.zeros((pad, LANES), jnp.float32)
    for y in range(nsec):
        v = vd_ref[2 * y * pad : (2 * y + 1) * pad, :]
        vv = vv + v * v
        vw = vw + v * w8_ref[y * pad : (y + 1) * pad, :]
    out_ref[...] = jnp.broadcast_to(lane_row([total(vv), total(vw)]), out_ref.shape)


def update_kernel(lines, pad, nsec, count, owner_ref, source_ref, sums_ref, vd_ref, w8_ref, out_ref, t_ref, scal_ref, t8_ref):
    sums = jnp.sum(sums_ref[...], axis=0, keepdims=True) / count
    norm, product = sums[:, 0:1], sums[:, 1:2]
    scale = 1.0 / jnp.sqrt(norm + EPS)
    rayleigh = product / (norm + EPS)
    for y in range(nsec):
        v0 = scale * vd_ref[2 * y * pad : (2 * y + 1) * pad, :]
        d = vd_ref[(2 * y + 1) * pad : (2 * y + 2) * pad, :]
        w0 = scale * w8_ref[y * pad : (y + 1) * pad, :]
        t8_ref[y * pad : (y + 1) * pad, :] = (w0 - rayleigh * v0) / d
    t_ref[...] = t8_ref[pl.ds(pl.multiple_of(lax.axis_index("sec") * pad, 8), lines), :]
    scal_ref[...] = jnp.broadcast_to(lane_row([norm, product]), scal_ref.shape)
    spread(t8_ref, owner_ref, source_ref, out_ref, lines, pad, nsec)


def last_sums_kernel(lines, per_row, nsec, owner_ref, orders_ref, part_ref, scal_ref, v_ref, w_ref, t_ref, h_ref, out_ref):
    h = masked_sum(part_ref, owner_ref, orders_ref, lines, per_row, nsec)
    h_ref[...] = h
    scale = 1.0 / jnp.sqrt(scal_ref[0:1, 0:1] + EPS)
    v0 = scale * v_ref[...]
    w0 = scale * w_ref[...]
    t = t_ref[...]
    sums = [total(v0 * t), total(t * t), total(t * w0), total(t * h), total(v0 * h)]
    out_ref[...] = jnp.broadcast_to(lane_row(sums), out_ref.shape)


def relay_kernel(in_ref, out_ref):
    out_ref[...] = jnp.broadcast_to(jnp.sum(in_ref[...], axis=0, keepdims=True), out_ref.shape)


def final_kernel(count, sums_ref, scal_ref, v_ref, w_ref, t_ref, h_ref, den_ref, new_ref, corr_ref):
    norm, product = scal_ref[0:1, 0:1], scal_ref[0:1, 1:2]
    sums = jnp.sum(sums_ref[...], axis=0, keepdims=True) / count
    along, tt, tw, th, vh = (sums[:, i : i + 1] for i in range(5))
    scale = 1.0 / jnp.sqrt(norm + EPS)
    rayleigh = product / (norm + EPS)
    vv = norm / (norm + EPS)
    tail = tt - 2.0 * along * along + along * along * vv
    inv = 1.0 / jnp.sqrt(tail + EPS)
    corner = inv * inv * (th - along * (tw + vh) + along * along * rayleigh)
    couple = inv * (tw - along * rayleigh)
    y = 2.0 * couple
    x = rayleigh - corner
    big = jnp.maximum(jnp.abs(x), jnp.abs(y))
    none = big == 0.0
    big = jnp.where(none, 1.0, big)
    xs = jnp.where(none, 1.0, x / big)
    ys = y / big
    hyp = jnp.sqrt(xs * xs + ys * ys)
    major = jnp.sqrt((hyp + jnp.abs(xs)) / (2.0 * hyp))
    minor = jnp.abs(ys) / (2.0 * hyp * major)
    ahead = xs > 0.0
    cosine = jnp.where(ahead, major, minor)
    sine = jnp.where(ys < 0.0, -1.0, 1.0) * jnp.where(ahead, minor, major)
    v0 = scale * v_ref[...]
    w0 = scale * w_ref[...]
    v1 = inv * (t_ref[...] - along * v0)
    w1 = inv * (h_ref[...] - along * w0)
    new = sine * v0 - cosine * v1
    applied = sine * w0 - cosine * w1
    lam = sine * sine * rayleigh + cosine * cosine * corner - 2.0 * sine * cosine * couple
    new_ref[...] = new
    corr_ref[...] = (applied - lam * new) / den_ref[...]


def f32(*shape):
    return jax.ShapeDtypeStruct(shape, jnp.float32)


def bf16(*shape):
    return jax.ShapeDtypeStruct(shape, jnp.bfloat16)


def call(kernel, out, smem, vmem, scratch=()):
    return pl.pallas_call(
        kernel,
        out_shape=out,
        in_specs=[SMEM] * len(smem) + [VMEM] * len(vmem),
        out_specs=jax.tree.map(lambda _: VMEM, out),
        scratch_shapes=scratch,
        compiler_params=pltpu.CompilerParams(vmem_limit_bytes=32 * 1024 * 1024),
    )(*smem, *vmem)


def exchange(x, axis, parts):
    lines = x.shape[0] // parts
    y = lax.all_to_all(x.reshape(parts, lines, 1, LANES), axis, 0, 0, tiled=True)
    return y.reshape(x.shape)


def per_device(psi, left_env, right_env, denominators, source_sector, owner, orders):
    rows = psi.shape[0]
    width = psi.shape[2]
    per_row = width // LANES
    lines = rows * per_row
    pad = up8(lines)
    nop = lax.axis_size(OP)
    nchip = lax.axis_size(CHIP)
    nsec = lax.axis_size("sec")
    count = float(width * nsec * width)
    left = left_env.reshape(width, width)
    right = right_env.reshape(width, width)
    source = source_sector.T
    psi_l = psi.reshape(lines, LANES)
    den_l = denominators.reshape(lines, LANES)
    part = functools.partial
    swap = [(0, 1), (1, 0)]

    v, vd = call(
        part(prep_kernel, per_row, nsec, pad),
        (f32(lines, LANES), f32(2 * nsec * pad, LANES)),
        (owner, orders),
        (psi_l, den_l),
    )
    vd8 = exchange(vd, "sec", nsec)
    lh, ll, rh, rl = call(
        part(split_kernel, rows),
        (bf16(width, width),) * 4,
        (),
        (left, right),
        scratch=[pltpu.VMEM((width, width), jnp.float32)],
    )

    def products(x):
        ih, il, other = call(
            part(inner_kernel, per_row),
            (bf16(width, width), bf16(width, width), f32(width * per_row // 2, LANES)),
            (),
            (x, rh, rl, lh, ll),
        )
        came = lax.ppermute(other, "op_2", swap)
        own = call(part(own_kernel, per_row), f32(width * per_row // 2, LANES), (), (lh, ll, ih, il))
        return exchange(own + came, CHIP, nchip)

    chosen = call(part(select_kernel, lines, pad, nsec), f32(nop * lines, LANES), (owner, source), (vd8,))
    parts = products(exchange(chosen, OP, nop))
    w, w_out = call(
        part(share_kernel, lines, pad, per_row, nsec),
        (f32(lines, LANES), f32(nsec * pad, LANES)),
        (owner, orders),
        (parts,),
    )
    w8 = exchange(w_out, "sec", nsec)
    sums = call(part(first_sums_kernel, pad, nsec), f32(nop, LANES), (), (vd8, w8))
    sums = exchange(sums, OP, nop)
    chosen, t, scal = call(
        part(update_kernel, lines, pad, nsec, count),
        (f32(nop * lines, LANES), f32(lines, LANES), f32(8, LANES)),
        (owner, source),
        (sums, vd8, w8),
        scratch=[pltpu.VMEM((nsec * pad, LANES), jnp.float32)],
    )
    parts = products(exchange(chosen, OP, nop))
    h, sums = call(
        part(last_sums_kernel, lines, per_row, nsec),
        (f32(lines, LANES), f32(nsec, LANES)),
        (owner, orders),
        (parts, scal, v, w, t),
    )
    sums = exchange(sums, "sec", nsec)
    sums = call(relay_kernel, f32(nop, LANES), (), (sums,))
    sums = exchange(sums, OP, nop)
    new, corr = call(
        part(final_kernel, count),
        (f32(lines, LANES), f32(lines, LANES)),
        (),
        (sums, scal, v, w, t, h, den_l),
    )
    return new.reshape(psi.shape), corr.reshape(psi.shape)


def solution(mesh):
    sec = mesh.shape["sec"]
    torus = Mesh(mesh.devices.reshape(4, 8, 2, sec), (*OP, "sec"))
    specs = (
        P(OP, "sec", None),
        P(OP, "sec", None, None),
        P(OP, "sec", None, None),
        P(OP, "sec", None),
        P(),
        P(),
        P(),
    )
    outs = (P(OP, "sec", None), P(OP, "sec", None))
    return jax.shard_map(per_device, mesh=torus, in_specs=specs, out_specs=outs, check_vma=False)
```

profile of v0, /device:TPU:1, one launch (start us, length us, event | category | flops | bytes accessed | tf_op | source)
XLA Modules:
  0.0 265.4 jit_solution(8064447449193348347)
XLA Ops:
  0.6 0.8 reduce
  1.5 0.8 reduce.1
  2.3 0.0 copy-start.7
  2.3 0.6 copy-done.7
  2.9 0.0 copy-start.9
  2.9 0.7 copy-done.9
  3.6 0.6 shard_map.87
  4.2 21.5 %all_to_all.45 = f32[8,112,1,128]{3,1,2,0:T(8,128)S(1)} all-to-all(f32[8,112,1,128]{3,1,2,0:T(8,128)S(1)} %bitcast.42), channel_id=1, replica_groups=mesh['op_0'=4,'op_1'=8,'op_2'=2,'sec'=8] {'sec'}, dimensions={0} | all-to-all | bytes 917504 | tf_op jit(solution)/shard_map/all_to_all | solution.py:254
  25.7 0.0 copy-start.5
  25.7 0.7 copy-done.5
  26.4 1.9 shard_map.88
  28.3 16.5 %all-to-all-start.1 = ((f32[64,50,1,128]{3,2,1,0:T(1,128)}), f32[64,50,1,128]{3,2,1,0:T(1,128)}, u32[]{:S(2)}, u32[]{:S(2)}) async-start(f32[64,50,1,128]{3,2,1,0:T(1,128)} %bitcast.6), calls=%async_computation.1 | async-start | bytes 3276800 | tf_op jit(solution)/shard_map/all_to_all | solution.py:254
  44.8 0.0 copy-start.3
  44.8 1.4 copy-done.3
  46.2 0.0 copy-start.4
  46.2 1.4 copy-done.4
  47.6 0.9 shard_map.86
  48.6 0.0 copy-start
  48.6 0.9 copy-done
  49.5 36.4 %all-to-all-done.1 = f32[64,50,1,128]{3,2,1,0:T(1,128)} async-done(((f32[64,50,1,128]{3,2,1,0:T(1,128)}), f32[64,50,1,128]{3,2,1,0:T(1,128)}, u32[]{:S(2)}, u32[]{:S(2)}) %all-to-all-start.1) | async-done | bytes 1638432 | tf_op jit(solution)/shard_map/all_to_all | solution.py:254
  85.9 0.0 copy-start.1
  85.9 1.1 copy-done.1
  87.0 5.0 %shard_map.89 = (bf16[640,640]{1,0:T(8,128)(2,1)S(1)}, bf16[640,640]{1,0:T(8,128)(2,1)S(1)}, f32[1600,128]{1,0:T(8,128)S(1)}) custom-call(f32[3200,128]{1,0:T(8,128)} %bitcast.7.x_ref, bf16[640,640]{1,0:T(8,128)(2,1)S(1)} %get-tuple-element.26.rh_ref, bf16[640,640]{1,0:T(8,128)(2,1)S(1)} %copy-done.1, bf16[640,640]{1,0:T(8,128)(2,1)S(1)} %get-tuple-element.23.lh_ref, ...), custom_call_target="tpu_custom_call" | custom-call | tf_op jit(solution)/shard_map/pallas_call | solution.py:242
  92.0 1.9 collective-permute-start
  94.0 1.3 shard_map.90
  95.3 0.0 copy-start.8
  95.3 0.0 copy-start.10
  95.3 0.9 collective-permute-done
  96.2 0.1 add.6
  96.3 0.0 copy-start.6
  96.4 24.5 %all_to_all.46 = f32[32,50,1,128]{3,2,1,0:T(1,128)S(1)} all-to-all(f32[32,50,1,128]{3,2,1,0:T(1,128)S(1)} %bitcast.52), channel_id=1, replica_groups=mesh['op_0'=4,'op_1'=8,'op_2'=2,'sec'=8] {'op_0','op_1'}, dimensions={0} | all-to-all | bytes 1638400 | tf_op jit(solution)/shard_map/all_to_all | solution.py:254
  120.9 0.0 copy-done.8
  120.9 0.0 copy-done.10
  120.9 0.6 shard_map.91
  121.5 11.4 %all_to_all.47 = f32[8,56,1,128]{3,1,2,0:T(8,128)S(1)} all-to-all(f32[8,56,1,128]{3,1,2,0:T(8,128)S(1)} %bitcast.43), channel_id=1, replica_groups=mesh['op_0'=4,'op_1'=8,'op_2'=2,'sec'=8] {'sec'}, dimensions={0} | all-to-all | bytes 458752 | tf_op jit(solution)/shard_map/all_to_all | solution.py:254
  132.9 0.1 shard_map.92
  133.0 21.6 %all_to_all.48 = f32[64,1,1,128]{3,2,1,0:T(1,128)S(1)} all-to-all(f32[64,1,1,128]{3,2,1,0:T(1,128)S(1)} %bitcast.45), channel_id=1, replica_groups=mesh['op_0'=4,'op_1'=8,'op_2'=2,'sec'=8] {'op_0','op_1','op_2'}, dimensions={0} | all-to-all | bytes 65536 | tf_op jit(solution)/shard_map/all_to_all | solution.py:254
  154.6 0.0 copy-done.6
  154.6 0.9 shard_map.93
  155.6 0.0 copy-start.2
  155.6 45.3 %all_to_all.49 = f32[64,50,1,128]{3,2,1,0:T(1,128)S(1)} all-to-all(f32[64,50,1,128]{3,2,1,0:T(1,128)S(1)} %bitcast.41), channel_id=1, replica_groups=mesh['op_0'=4,'op_1'=8,'op_2'=2,'sec'=8] {'op_0','op_1','op_2'}, dimensions={0} | all-to-all | bytes 3276800 | tf_op jit(solution)/shard_map/all_to_all | solution.py:254
  200.9 0.0 copy-done.2
  200.9 3.6 %shard_map.94 = (bf16[640,640]{1,0:T(8,128)(2,1)S(1)}, bf16[640,640]{1,0:T(8,128)(2,1)S(1)}, f32[1600,128]{1,0:T(8,128)S(1)}) custom-call(f32[3200,128]{1,0:T(8,128)S(1)} %bitcast.34, bf16[640,640]{1,0:T(8,128)(2,1)S(1)} %get-tuple-element.26.rh_ref, bf16[640,640]{1,0:T(8,128)(2,1)S(1)} %copy-done.2, bf16[640,640]{1,0:T(8,128)(2,1)S(1)} %get-tuple-element.23.lh_ref, ...), custom_call_target="tpu_custom_call" | custom-call | tf_op jit(solution)/shard_map/pallas_call | solution.py:242
  204.4 2.0 collective-permute-start.1
  206.5 1.3 shard_map.95
  207.8 0.9 collective-permute-done.1
  208.7 0.1 add.7
  208.8 24.6 %all_to_all.50 = f32[32,50,1,128]{3,2,1,0:T(1,128)S(1)} all-to-all(f32[32,50,1,128]{3,2,1,0:T(1,128)S(1)} %bitcast.53), channel_id=1, replica_groups=mesh['op_0'=4,'op_1'=8,'op_2'=2,'sec'=8] {'op_0','op_1'}, dimensions={0} | all-to-all | bytes 1638400 | tf_op jit(solution)/shard_map/all_to_all | solution.py:254
  233.3 0.7 shard_map.96
  234.1 8.9 %all_to_all.51 = f32[8,1,1,128]{3,2,1,0:T(1,128)S(1)} all-to-all(f32[8,1,1,128]{3,2,1,0:T(1,128)S(1)} %bitcast.51), channel_id=1, replica_groups=mesh['op_0'=4,'op_1'=8,'op_2'=2,'sec'=8] {'sec'}, dimensions={0} | all-to-all | bytes 8192 | tf_op jit(solution)/shard_map/all_to_all | solution.py:254
  243.0 20.7 %all_to_all.52 = f32[64,1,1,128]{3,2,1,0:T(1,128)S(1)} all-to-all(f32[64,1,1,128]{3,2,1,0:T(1,128)S(1)} %bitcast.46), channel_id=1, replica_groups=mesh['op_0'=4,'op_1'=8,'op_2'=2,'sec'=8] {'op_0','op_1','op_2'}, dimensions={0} | all-to-all | bytes 65536 | tf_op jit(solution)/shard_map/all_to_all | solution.py:254
  263.7 0.5 shard_map.98
  264.2 0.6 reshape.100
  264.8 0.6 reshape.101
  (3 shorter events, 0.0 us)
Async XLA Ops:
  2.3 0.7 copy-start.7
  2.9 0.7 copy-start.9
  25.7 0.7 copy-start.5
  28.3 57.6 %all-to-all-start.1 = ((f32[64,50,1,128]{3,2,1,0:T(1,128)}), f32[64,50,1,128]{3,2,1,0:T(1,128)}, u32[]{:S(2)}, u32[]{:S(2)}) async-start(f32[64,50,1,128]{3,2,1,0:T(1,128)} %bitcast.6), calls=%async_computation.1 | async-start | bytes 3276800 | tf_op jit(solution)/shard_map/all_to_all | solution.py:254
  44.8 1.4 copy-start.3
  46.2 1.4 copy-start.4
  48.6 0.9 copy-start
  85.9 1.1 copy-start.1
  92.0 4.2 %collective-permute-start = (f32[1600,128]{1,0:T(8,128)S(1)}, f32[1600,128]{1,0:T(8,128)S(1)}, u32[]{:S(2)}, u32[]{:S(2)}) collective-permute-start(f32[1600,128]{1,0:T(8,128)S(1)} %get-tuple-element.30), channel_id=1, source_target_pairs={{0,8},{8,0},{1,9},{9,1},{2,10},{10,2},{3,11},{11,3},{4,12},{12,4},... | collective-permute-start | bytes 2457608 | tf_op jit(solution)/shard_map/ppermute | solution.py:298
  95.3 25.6 %copy-start.8 = (s32[8]{0:T(128)S(1)}, s32[8]{0:T(128)}, u32[]{:S(2)}) copy-start(s32[8]{0:T(128)} %owner_ref.9) | copy-start | bytes 100
  95.3 25.6 %copy-start.10 = (s32[8]{0:T(128)S(1)}, s32[8]{0:T(128)}, u32[]{:S(2)}) copy-start(s32[8]{0:T(128)} %orders_ref.5) | copy-start | bytes 100
  96.3 58.3 %copy-start.6 = (s32[64,8]{0,1:T(8,128)S(1)}, s32[64,8]{0,1:T(8,128)}, u32[]{:S(2)}) copy-start(s32[64,8]{0,1:T(8,128)} %param.11) | copy-start | bytes 6148
  155.6 45.3 %copy-start.2 = (bf16[640,640]{1,0:T(8,128)(2,1)S(1)}, bf16[640,640]{1,0:T(8,128)(2,1)}, u32[]{:S(2)}) copy-start(bf16[640,640]{1,0:T(8,128)(2,1)} %copy-done) | copy-start | bytes 2457604
  204.4 4.2 %collective-permute-start.1 = (f32[1600,128]{1,0:T(8,128)S(1)}, f32[1600,128]{1,0:T(8,128)S(1)}, u32[]{:S(2)}, u32[]{:S(2)}) collective-permute-start(f32[1600,128]{1,0:T(8,128)S(1)} %get-tuple-element.35), channel_id=1, source_target_pairs={{0,8},{8,0},{1,9},{9,1},{2,10},{10,2},{3,11},{11,3},{4,12},{12,4},... | collective-permute-start | bytes 2457608 | tf_op jit(solution)/shard_map/ppermute | solution.py:298
where the time goes:
time: 266 us; the launch traced here: 265 us
  blocking collectives  179 us (67%)
  waiting for transfers between devices  38.3 us (14%)
  starting transfers between devices  20.4 us (8%)
  Pallas kernels  17.4 us (7%)
  local copies, waits for them, and re-layouts  8.2 us (3%)
    all_to_all x8, blocking collectives, exchange(): lax.all_to_all(x.reshape(parts, lines, 1, LANES), axis, 0, 0, tiled=True)  179 us
    all_to_all x1, waiting for transfers between devices, exchange(): lax.all_to_all(x.reshape(parts, lines, 1, LANES), axis, 0, 0, tiled=True)  36.4 us
    pallas_call x13, Pallas kernels, call(): pl.pallas_call(kernel, out_shape=out, in_specs=[SMEM] * len(smem) + [VMEM...  17.4 us
    all_to_all x1, starting transfers between devices, exchange(): lax.all_to_all(x.reshape(parts, lines, 1, LANES), axis, 0, 0, tiled=True)  16.5 us
    unnamed x22, local copies, waits for them, and re-layouts  6.92 us
  transfers between devices with their start and end apart: 3, of which 3 were waited for; matrix products, arithmetic and copies ran while one was open for 0% of the time, Pallas kernels for 1%

commit v1 on v0

--- a/solution.py
+++ b/solution.py
@@ -52,20 +52,26 @@
     return out
 
 
-def prep_kernel(per_row, nsec, pad, owner_ref, orders_ref, psi_ref, den_ref, v_ref, out_ref):
-    lines = psi_ref.shape[0]
-    rows = lines // per_row
+def prep_kernel(per_row, nsec, pad, owner_ref, orders_ref, psi_ref, den_ref, v_ref, v_out_ref, d_out_ref):
+    rows, width = psi_ref.shape[0], psi_ref.shape[2]
+    lines = rows * per_row
     order = orders_ref[sector_at(owner_ref, lax.axis_index("sec"), nsec)]
-    keep = row_mask(order, lines, per_row, op_position() * rows)
-    v = jnp.where(keep, psi_ref[...], 0.0)
-    d = den_ref[...]
-    v_ref[...] = v
-    for y in range(nsec):
-        out_ref[2 * y * pad : 2 * y * pad + lines, :] = v
-        out_ref[(2 * y + 1) * pad : (2 * y + 1) * pad + lines, :] = d
-        if pad > lines:
-            out_ref[2 * y * pad + lines : (2 * y + 1) * pad, :] = jnp.zeros((pad - lines, LANES), jnp.float32)
-            out_ref[(2 * y + 1) * pad + lines : (2 * y + 2) * pad, :] = jnp.ones((pad - lines, LANES), jnp.float32)
+    row = lax.broadcasted_iota(jnp.int32, (rows, width), 0) + op_position() * rows
+    col = lax.broadcasted_iota(jnp.int32, (rows, width), 1)
+    v = jnp.where((row < order) & (col < order), psi_ref[:, 0, :], 0.0)
+    d = den_ref[:, 0, :]
+    for k in range(per_row):
+        part = slice(k * LANES, (k + 1) * LANES)
+        at = pl.ds(k, rows, stride=per_row)
+        v_ref[at, :] = v[:, part]
+        d_out_ref[at, :] = d[:, part]
+        for y in range(nsec):
+            at = pl.ds(y * pad + k, rows, stride=per_row)
+            v_out_ref[at, :] = v[:, part]
+    if pad > lines:
+        for y in range(nsec):
+            v_out_ref[y * pad + lines : (y + 1) * pad, :] = jnp.zeros((pad - lines, LANES), jnp.float32)
+        d_out_ref[lines:pad, :] = jnp.ones((pad - lines, LANES), jnp.float32)
 
 
 def spread(table_ref, owner_ref, source_ref, out_ref, lines, pitch, nsec):
@@ -76,8 +82,9 @@
         out_ref[t * lines : (t + 1) * lines, :] = table_ref[pl.ds(start, lines), :]
 
 
-def select_kernel(lines, pad, nsec, owner_ref, source_ref, vd_ref, out_ref):
-    spread(vd_ref, owner_ref, source_ref, out_ref, lines, 2 * pad, nsec)
+def select_kernel(lines, pad, nsec, owner_ref, source_ref, v8_ref, d_ref, out_ref, d_out_ref):
+    d_out_ref[...] = d_ref[...]
+    spread(v8_ref, owner_ref, source_ref, out_ref, lines, pad, nsec)
 
 
 def halves(x):
@@ -90,7 +97,18 @@
     return dot(a_hi, b_hi) + (dot(a_hi, b_lo) + dot(a_lo, b_hi))
 
 
-def split_kernel(rows, left_ref, right_ref, lh_ref, ll_ref, rh_ref, rl_ref, order_ref):
+def split_rows(x_ref, hi_ref, lo_ref):
+    step = 160
+
+    def body(m, carry):
+        at = pl.ds(pl.multiple_of(m * step, step), step)
+        hi_ref[at, :], lo_ref[at, :] = halves(x_ref[at, :])
+        return carry
+
+    lax.fori_loop(0, x_ref.shape[0] // step, body, 0)
+
+
+def split_kernel(rows, left_ref, right_ref, mats_ref, order_ref):
     width = left_ref.shape[0]
     half = width // 2
     mine = lax.axis_index("op_2") == 0
@@ -99,28 +117,21 @@
         b = left_ref[(2 * q + 1) * rows : (2 * q + 2) * rows, :]
         order_ref[q * rows : (q + 1) * rows, :] = jnp.where(mine, b, a)
         order_ref[half + q * rows : half + (q + 1) * rows, :] = jnp.where(mine, a, b)
-    step = 160
-
-    def body(m, carry):
-        at = pl.ds(pl.multiple_of(m * step, step), step)
-        lh_ref[at, :], ll_ref[at, :] = halves(order_ref[at, :])
-        rh_ref[at, :], rl_ref[at, :] = halves(right_ref[at, :])
-        return carry
-
-    lax.fori_loop(0, width // step, body, 0)
-
-
-def left_product(lh_ref, ll_ref, ih_ref, il_ref, out_ref, first, per_row):
+    split_rows(order_ref, mats_ref.at[0], mats_ref.at[1])
+    split_rows(right_ref, mats_ref.at[2], mats_ref.at[3])
+
+
+def left_product(mats_ref, ih_ref, il_ref, out_ref, first, per_row):
     step = 160
     for m in range(out_ref.shape[0] // per_row // step):
         at = pl.ds(first + m * step, step)
-        y = dot3(lh_ref[at, :], ll_ref[at, :], ih_ref[...], il_ref[...])
+        y = dot3(mats_ref[0, at, :], mats_ref[1, at, :], ih_ref[...], il_ref[...])
         for k in range(per_row):
             out_ref[pl.ds(m * step * per_row + k, step, stride=per_row), :] = y[:, k * LANES : (k + 1) * LANES]
 
 
-def inner_kernel(per_row, x_ref, rh_ref, rl_ref, lh_ref, ll_ref, ih_ref, il_ref, out_ref):
-    width = rh_ref.shape[0]
+def inner_kernel(per_row, x_ref, mats_ref, ih_ref, il_ref, out_ref):
+    width = mats_ref.shape[1]
     step = 160
     for m in range(width // step):
         x = jnp.concatenate(
@@ -128,12 +139,12 @@
         )
         x_hi, x_lo = halves(x)
         at = pl.ds(m * step, step)
-        ih_ref[at, :], il_ref[at, :] = halves(dot3(x_hi, x_lo, rh_ref[...], rl_ref[...]))
-    left_product(lh_ref, ll_ref, ih_ref, il_ref, out_ref, 0, per_row)
-
-
-def own_kernel(per_row, lh_ref, ll_ref, ih_ref, il_ref, out_ref):
-    left_product(lh_ref, ll_ref, ih_ref, il_ref, out_ref, lh_ref.shape[0] // 2, per_row)
+        ih_ref[at, :], il_ref[at, :] = halves(dot3(x_hi, x_lo, mats_ref[2], mats_ref[3]))
+    left_product(mats_ref, ih_ref, il_ref, out_ref, 0, per_row)
+
+
+def own_kernel(per_row, mats_ref, ih_ref, il_ref, out_ref):
+    left_product(mats_ref, ih_ref, il_ref, out_ref, mats_ref.shape[1] // 2, per_row)
 
 
 def masked_sum(part_ref, owner_ref, orders_ref, lines, per_row, nsec):
@@ -155,27 +166,27 @@
             out_ref[y * pad + lines : (y + 1) * pad, :] = jnp.zeros((pad - lines, LANES), jnp.float32)
 
 
-def first_sums_kernel(pad, nsec, vd_ref, w8_ref, out_ref):
+def first_sums_kernel(pad, nsec, v8_ref, w8_ref, out_ref):
     vv = jnp.zeros((pad, LANES), jnp.float32)
     vw = jnp.zeros((pad, LANES), jnp.float32)
     for y in range(nsec):
-        v = vd_ref[2 * y * pad : (2 * y + 1) * pad, :]
+        v = v8_ref[y * pad : (y + 1) * pad, :]
         vv = vv + v * v
         vw = vw + v * w8_ref[y * pad : (y + 1) * pad, :]
     out_ref[...] = jnp.broadcast_to(lane_row([total(vv), total(vw)]), out_ref.shape)
 
 
-def update_kernel(lines, pad, nsec, count, owner_ref, source_ref, sums_ref, vd_ref, w8_ref, out_ref, t_ref, scal_ref, t8_ref):
+def update_kernel(lines, pad, nsec, count, owner_ref, source_ref, sums_ref, v8_ref, d8_ref, w8_ref, out_ref, t_ref, scal_ref, t8_ref):
     sums = jnp.sum(sums_ref[...], axis=0, keepdims=True) / count
     norm, product = sums[:, 0:1], sums[:, 1:2]
     scale = 1.0 / jnp.sqrt(norm + EPS)
     rayleigh = product / (norm + EPS)
-    for y in range(nsec):
-        v0 = scale * vd_ref[2 * y * pad : (2 * y + 1) * pad, :]
-        d = vd_ref[(2 * y + 1) * pad : (2 * y + 2) * pad, :]
-        w0 = scale * w8_ref[y * pad : (y + 1) * pad, :]
-        t8_ref[y * pad : (y + 1) * pad, :] = (w0 - rayleigh * v0) / d
-    t_ref[...] = t8_ref[pl.ds(pl.multiple_of(lax.axis_index("sec") * pad, 8), lines), :]
+    me = lax.axis_index("sec")
+    for k in range(nsec):
+        slot = lax.rem(me + nsec - k, nsec)
+        at = pl.ds(pl.multiple_of(slot * pad, 8), pad)
+        t8_ref[at, :] = (scale * w8_ref[at, :] - rayleigh * (scale * v8_ref[at, :])) / d8_ref[k * pad : (k + 1) * pad, :]
+    t_ref[...] = t8_ref[pl.ds(pl.multiple_of(me * pad, 8), lines), :]
     scal_ref[...] = jnp.broadcast_to(lane_row([norm, product]), scal_ref.shape)
     spread(t8_ref, owner_ref, source_ref, out_ref, lines, pad, nsec)
 
@@ -191,11 +202,7 @@
     out_ref[...] = jnp.broadcast_to(lane_row(sums), out_ref.shape)
 
 
-def relay_kernel(in_ref, out_ref):
-    out_ref[...] = jnp.broadcast_to(jnp.sum(in_ref[...], axis=0, keepdims=True), out_ref.shape)
-
-
-def final_kernel(count, sums_ref, scal_ref, v_ref, w_ref, t_ref, h_ref, den_ref, new_ref, corr_ref):
+def final_kernel(count, per_row, sums_ref, scal_ref, v_ref, w_ref, t_ref, h_ref, d_ref, new_ref, corr_ref, new_lines, corr_lines):
     norm, product = scal_ref[0:1, 0:1], scal_ref[0:1, 1:2]
     sums = jnp.sum(sums_ref[...], axis=0, keepdims=True) / count
     along, tt, tw, th, vh = (sums[:, i : i + 1] for i in range(5))
@@ -226,8 +233,13 @@
     new = sine * v0 - cosine * v1
     applied = sine * w0 - cosine * w1
     lam = sine * sine * rayleigh + cosine * cosine * corner - 2.0 * sine * cosine * couple
-    new_ref[...] = new
-    corr_ref[...] = (applied - lam * new) / den_ref[...]
+    new_lines[...] = new
+    corr_lines[...] = (applied - lam * new) / d_ref[0 : new.shape[0], :]
+    rows = new_ref.shape[0]
+    for k in range(per_row):
+        at, part = pl.ds(k, rows, stride=per_row), slice(k * LANES, (k + 1) * LANES)
+        new_ref[:, 0, part] = new_lines[at, :]
+        corr_ref[:, 0, part] = corr_lines[at, :]
 
 
 def f32(*shape):
@@ -268,39 +280,46 @@
     left = left_env.reshape(width, width)
     right = right_env.reshape(width, width)
     source = source_sector.T
-    psi_l = psi.reshape(lines, LANES)
-    den_l = denominators.reshape(lines, LANES)
     part = functools.partial
     swap = [(0, 1), (1, 0)]
 
-    v, vd = call(
+    v, v_out, d_out = call(
         part(prep_kernel, per_row, nsec, pad),
-        (f32(lines, LANES), f32(2 * nsec * pad, LANES)),
+        (f32(lines, LANES), f32(nsec * pad, LANES), f32(pad, LANES)),
         (owner, orders),
-        (psi_l, den_l),
-    )
-    vd8 = exchange(vd, "sec", nsec)
-    lh, ll, rh, rl = call(
+        (psi, denominators),
+    )
+    v8 = exchange(v_out, "sec", nsec)
+    square = bf16(width, width)
+    half = f32(width * per_row // 2, LANES)
+    mats = call(
         part(split_kernel, rows),
-        (bf16(width, width),) * 4,
+        bf16(4, width, width),
         (),
         (left, right),
         scratch=[pltpu.VMEM((width, width), jnp.float32)],
     )
 
     def products(x):
-        ih, il, other = call(
-            part(inner_kernel, per_row),
-            (bf16(width, width), bf16(width, width), f32(width * per_row // 2, LANES)),
-            (),
-            (x, rh, rl, lh, ll),
-        )
+        ih, il, other = call(part(inner_kernel, per_row), (square, square, half), (), (x, mats))
         came = lax.ppermute(other, "op_2", swap)
-        own = call(part(own_kernel, per_row), f32(width * per_row // 2, LANES), (), (lh, ll, ih, il))
+        own = call(part(own_kernel, per_row), half, (), (mats, ih, il))
         return exchange(own + came, CHIP, nchip)
 
-    chosen = call(part(select_kernel, lines, pad, nsec), f32(nop * lines, LANES), (owner, source), (vd8,))
-    parts = products(exchange(chosen, OP, nop))
+    chosen, d8 = call(
+        part(select_kernel, lines, pad, nsec),
+        (f32(nop * lines, LANES), f32(pad, LANES)),
+        (owner, source),
+        (v8, d_out),
+    )
+    chosen = exchange(chosen, OP, nop)
+    reach = 1
+    while reach < nsec:
+        came = lax.ppermute(d8, "sec", [(i, (i + reach) % nsec) for i in range(nsec)])
+        d8 = jnp.concatenate([d8, came], axis=0)
+        reach *= 2
+    chosen, d8 = lax.optimization_barrier((chosen, d8))
+    parts = products(chosen)
     w, w_out = call(
         part(share_kernel, lines, pad, per_row, nsec),
         (f32(lines, LANES), f32(nsec * pad, LANES)),
@@ -308,32 +327,32 @@
         (parts,),
     )
     w8 = exchange(w_out, "sec", nsec)
-    sums = call(part(first_sums_kernel, pad, nsec), f32(nop, LANES), (), (vd8, w8))
+    sums = call(part(first_sums_kernel, pad, nsec), f32(nop, LANES), (), (v8, w8))
     sums = exchange(sums, OP, nop)
     chosen, t, scal = call(
         part(update_kernel, lines, pad, nsec, count),
         (f32(nop * lines, LANES), f32(lines, LANES), f32(8, LANES)),
         (owner, source),
-        (sums, vd8, w8),
+        (sums, v8, d8, w8),
         scratch=[pltpu.VMEM((nsec * pad, LANES), jnp.float32)],
     )
     parts = products(exchange(chosen, OP, nop))
     h, sums = call(
         part(last_sums_kernel, lines, per_row, nsec),
-        (f32(lines, LANES), f32(nsec, LANES)),
+        (f32(lines, LANES), f32(1, LANES)),
         (owner, orders),
         (parts, scal, v, w, t),
     )
-    sums = exchange(sums, "sec", nsec)
-    sums = call(relay_kernel, f32(nop, LANES), (), (sums,))
-    sums = exchange(sums, OP, nop)
-    new, corr = call(
-        part(final_kernel, count),
-        (f32(lines, LANES), f32(lines, LANES)),
+    chips = nchip * nsec
+    sums = jnp.broadcast_to(lax.psum(sums, "op_2"), (chips, LANES))
+    sums = exchange(sums, (*CHIP, "sec"), chips)
+    return call(
+        part(final_kernel, count, per_row),
+        (f32(*psi.shape), f32(*psi.shape)),
         (),
-        (sums, scal, v, w, t, h, den_l),
-    )
-    return new.reshape(psi.shape), corr.reshape(psi.shape)
+        (sums, scal, v, w, t, h, d_out),
+        scratch=[pltpu.VMEM((lines, LANES), jnp.float32)] * 2,
+    )
 
 
 def solution(mesh):

time: 266 us -> 259 us (0.974)
  blocking collectives: 179 us -> 172 us
  starting transfers between devices: 20.4 us -> 26.7 us
  waiting for transfers between devices: 38.3 us -> 32.4 us
    all_to_all x1, waiting for transfers between devices: 36.4 us -> 15 us  [exchange(): lax.all_to_all(x.reshape(parts, lines, 1, LANES), axis, 0, 0, tiled=True)]
    ppermute x0 -> x3, waiting for transfers between devices: none -> 15.6 us  [per_device(): lax.ppermute(d8, 'sec', [(i, (i + reach) % nsec) for i in range(nsec)])]
    all_to_all x8 -> x7, blocking collectives: 179 us -> 165 us  [exchange(): lax.all_to_all(x.reshape(parts, lines, 1, LANES), axis, 0, 0, tiled=True)]
    psum x0 -> x1, blocking collectives: none -> 6.75 us  [per_device(): sums = jnp.broadcast_to(lax.psum(sums, 'op_2'), (chips, LANES))]
    ppermute x0 -> x3, starting transfers between devices: none -> 6.02 us  [per_device(): lax.ppermute(d8, 'sec', [(i, (i + reach) % nsec) for i in range(nsec)])]
    pallas_call x13 -> x12, Pallas kernels: 17.4 us -> 18.1 us  [call(): pl.pallas_call(kernel, out_shape=out, in_specs=[SMEM] * len(smem) + [VMEM...]
    unnamed x22 -> x34, local copies, waits for them, and re-layouts: 6.92 us -> 7.12 us
  transfers between devices with their start and end apart: 3 -> 6, of which waited for: 3 -> 6; matrix products, arithmetic and copies ran while one was open for 0% -> 0% of each run, Pallas kernels for 1% -> 1%
where the time goes in v1:
time: 259 us; the launch traced here: 258 us
  blocking collectives  172 us (66%)
  waiting for transfers between devices  32.4 us (13%)
  starting transfers between devices  26.7 us (10%)
  Pallas kernels  18.1 us (7%)
  local copies, waits for them, and re-layouts  7.19 us (3%)
    all_to_all x7, blocking collectives, exchange(): lax.all_to_all(x.reshape(parts, lines, 1, LANES), axis, 0, 0, tiled=True)  165 us
    pallas_call x12, Pallas kernels, call(): pl.pallas_call(kernel, out_shape=out, in_specs=[SMEM] * len(smem) + [VMEM...  18.1 us
    all_to_all x1, starting transfers between devices, exchange(): lax.all_to_all(x.reshape(parts, lines, 1, LANES), axis, 0, 0, tiled=True)  16.7 us
    ppermute x3, waiting for transfers between devices, per_device(): lax.ppermute(d8, 'sec', [(i, (i + reach) % nsec) for i in range(nsec)])  15.6 us
    all_to_all x1, waiting for transfers between devices, exchange(): lax.all_to_all(x.reshape(parts, lines, 1, LANES), axis, 0, 0, tiled=True)  15 us
    unnamed x34, local copies, waits for them, and re-layouts  7.12 us
    psum x1, blocking collectives, per_device(): sums = jnp.broadcast_to(lax.psum(sums, 'op_2'), (chips, LANES))  6.75 us
    ppermute x3, starting transfers between devices, per_device(): lax.ppermute(d8, 'sec', [(i, (i + reach) % nsec) for i in range(nsec)])  6.02 us
  transfers between devices with their start and end apart: 6, of which 6 were waited for; matrix products, arithmetic and copies ran while one was open for 0% of the time, Pallas kernels for 1%

profile of v1, /device:TPU:1, one launch (start us, length us, event | category | flops | bytes accessed | tf_op | source)
XLA Modules:
  0.0 257.9 jit_solution(6988759171444945804)
XLA Ops:
  0.6 0.0 copy-start.9
  0.6 0.7 copy-done.9
  1.4 0.7 copy-done.10
  2.1 0.7 copy-done.13
  2.8 0.7 copy-done.15
  3.4 0.6 shard_map.87
  4.0 0.0 copy-start.3
  4.0 0.0 copy-start.5
  4.0 16.3 %all_to_all.40 = f32[8,56,1,128]{3,1,2,0:T(8,128)S(1)} all-to-all(f32[8,56,1,128]{3,1,2,0:T(8,128)S(1)} %bitcast.37), channel_id=1, replica_groups=mesh['op_0'=4,'op_1'=8,'op_2'=2,'sec'=8] {'sec'}, dimensions={0} | all-to-all | bytes 458752 | tf_op jit(solution)/shard_map/all_to_all | solution.py:266
  20.4 0.0 copy-done.3
  20.4 0.0 copy-done.5
  20.4 0.7 copy-done.11
  21.1 1.9 shard_map.88
  23.0 16.7 %all-to-all-start.1 = ((f32[64,50,1,128]{3,2,1,0:T(1,128)}), f32[64,50,1,128]{3,2,1,0:T(1,128)}, u32[]{:S(2)}, u32[]{:S(2)}) async-start(f32[64,50,1,128]{3,2,1,0:T(1,128)} %bitcast.6), calls=%async_computation.1 | async-start | bytes 3276800 | tf_op jit(solution)/shard_map/all_to_all | solution.py:266
  39.7 2.2 collective-permute-start
  41.9 4.0 %collective-permute-done = f32[56,128]{1,0:T(8,128)S(1)} collective-permute-done((f32[56,128]{1,0:T(8,128)S(1)}, f32[56,128]{1,0:T(8,128)S(1)}, u32[]{:S(2)}, u32[]{:S(2)}) %collective-permute-start) | collective-permute-done | bytes 28704 | tf_op jit(solution)/shard_map/ppermute | solution.py:318
  46.0 1.9 collective-permute-start.1
  47.9 6.1 %collective-permute-done.1 = f32[112,128]{1,0:T(8,128)S(1)} collective-permute-done((f32[112,128]{1,0:T(8,128)S(1)}, f32[112,128]{1,0:T(8,128)S(1)}, u32[]{:S(2)}, u32[]{:S(2)}) %collective-permute-start.1) | collective-permute-done | bytes 57376 | tf_op jit(solution)/shard_map/ppermute | solution.py:318
  54.0 1.9 collective-permute-start.2
  55.9 0.0 copy-start
  55.9 1.4 copy-done
  57.3 1.4 copy-done.1
  58.8 0.9 shard_map.86.mats_ref
  59.7 5.5 %collective-permute-done.2 = f32[224,128]{1,0:T(8,128)S(1)} collective-permute-done((f32[224,128]{1,0:T(8,128)S(1)}, f32[224,128]{1,0:T(8,128)S(1)}, u32[]{:S(2)}, u32[]{:S(2)}) %collective-permute-start.2) | collective-permute-done | bytes 114720 | tf_op jit(solution)/shard_map/ppermute | solution.py:318
  65.2 0.7 pad_maximum_fusion.d8_ref
  65.9 15.0 %all-to-all-done.1 = f32[64,50,1,128]{3,2,1,0:T(1,128)} async-done(((f32[64,50,1,128]{3,2,1,0:T(1,128)}), f32[64,50,1,128]{3,2,1,0:T(1,128)}, u32[]{:S(2)}, u32[]{:S(2)}) %all-to-all-start.1) | async-done | bytes 1638432 | tf_op jit(solution)/shard_map/all_to_all | solution.py:266
  80.8 5.0 %shard_map.89 = (bf16[640,640]{1,0:T(8,128)(2,1)S(1)}, bf16[640,640]{1,0:T(8,128)(2,1)S(1)}, f32[1600,128]{1,0:T(8,128)S(1)}) custom-call(f32[3200,128]{1,0:T(8,128)} %bitcast.7.x_ref, bf16[4,640,640]{2,1,0:T(8,128)(2,1)S(1)} %shard_map.86.mats_ref), custom_call_target="tpu_custom_call" | custom-call | tf_op jit(solution)/shard_map/pallas_call | solution.py:254
  85.8 1.9 collective-permute-start.3
  87.8 1.3 shard_map.90
  89.1 0.0 copy-start.14
  89.1 0.0 copy-start.16
  89.1 0.9 collective-permute-done.3
  90.0 0.1 add.8
  90.2 0.0 copy-start.2
  90.2 0.0 copy-start.12
  90.2 24.7 %all_to_all.41 = f32[32,50,1,128]{3,2,1,0:T(1,128)S(1)} all-to-all(f32[32,50,1,128]{3,2,1,0:T(1,128)S(1)} %bitcast.44), channel_id=1, replica_groups=mesh['op_0'=4,'op_1'=8,'op_2'=2,'sec'=8] {'op_0','op_1'}, dimensions={0} | all-to-all | bytes 1638400 | tf_op jit(solution)/shard_map/all_to_all | solution.py:266
  114.8 0.0 copy-done.14
  114.9 0.0 copy-done.16
  114.9 0.6 shard_map.91
  115.5 11.4 %all_to_all.42 = f32[8,56,1,128]{3,1,2,0:T(8,128)S(1)} all-to-all(f32[8,56,1,128]{3,1,2,0:T(8,128)S(1)} %bitcast.38), channel_id=1, replica_groups=mesh['op_0'=4,'op_1'=8,'op_2'=2,'sec'=8] {'sec'}, dimensions={0} | all-to-all | bytes 458752 | tf_op jit(solution)/shard_map/all_to_all | solution.py:266
  126.9 0.1 shard_map.92
  127.0 21.6 %all_to_all.43 = f32[64,1,1,128]{3,2,1,0:T(1,128)S(1)} all-to-all(f32[64,1,1,128]{3,2,1,0:T(1,128)S(1)} %bitcast.40), channel_id=1, replica_groups=mesh['op_0'=4,'op_1'=8,'op_2'=2,'sec'=8] {'op_0','op_1','op_2'}, dimensions={0} | all-to-all | bytes 65536 | tf_op jit(solution)/shard_map/all_to_all | solution.py:266
  148.6 0.0 copy-done.2
  148.6 0.0 copy-done.12
  148.6 1.0 shard_map.93
  149.5 0.0 copy-start.7
  149.6 45.2 %all_to_all.44 = f32[64,50,1,128]{3,2,1,0:T(1,128)S(1)} all-to-all(f32[64,50,1,128]{3,2,1,0:T(1,128)S(1)} %bitcast.35), channel_id=1, replica_groups=mesh['op_0'=4,'op_1'=8,'op_2'=2,'sec'=8] {'op_0','op_1','op_2'}, dimensions={0} | all-to-all | bytes 3276800 | tf_op jit(solution)/shard_map/all_to_all | solution.py:266
  194.7 3.6 %shard_map.94 = (bf16[640,640]{1,0:T(8,128)(2,1)S(1)}, bf16[640,640]{1,0:T(8,128)(2,1)S(1)}, f32[1600,128]{1,0:T(8,128)S(1)}) custom-call(f32[3200,128]{1,0:T(8,128)S(1)} %bitcast.25, bf16[4,640,640]{2,1,0:T(8,128)(2,1)S(1)} %shard_map.86.mats_ref), custom_call_target="tpu_custom_call" | custom-call | tf_op jit(solution)/shard_map/pallas_call | solution.py:254
  198.3 2.0 collective-permute-start.4
  200.3 1.3 shard_map.95
  201.6 0.0 copy-start.4
  201.6 0.9 collective-permute-done.4
  202.5 0.1 add.9
  202.6 0.0 copy-start.6
  202.6 24.6 %all_to_all.45 = f32[32,50,1,128]{3,2,1,0:T(1,128)S(1)} all-to-all(f32[32,50,1,128]{3,2,1,0:T(1,128)S(1)} %bitcast.45), channel_id=1, replica_groups=mesh['op_0'=4,'op_1'=8,'op_2'=2,'sec'=8] {'op_0','op_1'}, dimensions={0} | all-to-all | bytes 1638400 | tf_op jit(solution)/shard_map/all_to_all | solution.py:266
  227.2 0.0 copy-done.7
  227.2 0.0 copy-done.4
  227.2 0.7 shard_map.96
  227.9 6.7 %psum.7 = f32[128]{0:T(128)S(1)} all-reduce(f32[128]{0:T(128)S(1)} %bitcast.43), channel_id=1, replica_groups=mesh['op_0'=4,'op_1'=8,'op_2'=2,'sec'=8] {'op_2'}, use_global_device_ids=true, to_apply=%region_0.0 | all-reduce | flops 128 | bytes 1024 | tf_op jit(solution)/shard_map/psum | solution.py:347
  234.7 0.1 reshape.74
  234.7 21.3 %all_to_all.46 = f32[256,1,1,128]{3,2,1,0:T(1,128)S(1)} all-to-all(f32[256,1,1,128]{3,2,1,0:T(1,128)S(1)} %reshape.74), channel_id=1, replica_groups=mesh['op_0'=4,'op_1'=8,'op_2'=2,'sec'=8] {'op_0','op_1','sec'}, dimensions={0} | all-to-all | bytes 262144 | tf_op jit(solution)/shard_map/all_to_all | solution.py:266
  256.0 0.0 copy-done.6
  256.0 0.7 copy-done.8
  256.7 1.1 shard_map.97
  (8 shorter events, 0.0 us)
Async XLA Ops:
  0.6 0.7 copy-start.9
  1.4 0.7 copy-start.10
  2.1 0.7 copy-start.13
  2.8 0.7 copy-start.15
  4.0 16.3 %copy-start.3 = (f32[50,128]{1,0:T(8,128)}, f32[50,128]{1,0:T(8,128)S(1)}, u32[]{:S(2)}) copy-start(f32[50,128]{1,0:T(8,128)S(1)} %get-tuple-element.37.v_ref) | copy-start | bytes 76804
  4.0 16.3 %copy-start.5 = (f32[56,128]{1,0:T(8,128)}, f32[56,128]{1,0:T(8,128)S(1)}, u32[]{:S(2)}) copy-start(f32[56,128]{1,0:T(8,128)S(1)} %get-tuple-element.23.d_ref) | copy-start | bytes 86020
  20.4 0.7 copy-start.11
  23.0 57.9 %all-to-all-start.1 = ((f32[64,50,1,128]{3,2,1,0:T(1,128)}), f32[64,50,1,128]{3,2,1,0:T(1,128)}, u32[]{:S(2)}, u32[]{:S(2)}) async-start(f32[64,50,1,128]{3,2,1,0:T(1,128)} %bitcast.6), calls=%async_computation.1 | async-start | bytes 3276800 | tf_op jit(solution)/shard_map/all_to_all | solution.py:266
  39.7 6.2 %collective-permute-start = (f32[56,128]{1,0:T(8,128)S(1)}, f32[56,128]{1,0:T(8,128)S(1)}, u32[]{:S(2)}, u32[]{:S(2)}) collective-permute-start(f32[56,128]{1,0:T(8,128)S(1)} %get-tuple-element.25), channel_id=1, source_target_pairs={{0,1},{1,2},{2,3},{3,4},{4,5},{5,6},{6,7},{7,0},{8,9},{9,10},{10,1... | collective-permute-start | bytes 86024 | tf_op jit(solution)/shard_map/ppermute | solution.py:318
  46.0 8.0 %collective-permute-start.1 = (f32[112,128]{1,0:T(8,128)S(1)}, f32[112,128]{1,0:T(8,128)S(1)}, u32[]{:S(2)}, u32[]{:S(2)}) collective-permute-start(f32[112,128]{1,0:T(8,128)S(1)} %pad_maximum_fusion.2), channel_id=1, source_target_pairs={{0,2},{1,3},{2,4},{3,5},{4,6},{5,7},{6,0},{7,1},{8,10},{9,11},{10,... | collective-permute-start | bytes 172040 | tf_op jit(solution)/shard_map/ppermute | solution.py:318
  54.0 11.2 %collective-permute-start.2 = (f32[224,128]{1,0:T(8,128)S(1)}, f32[224,128]{1,0:T(8,128)S(1)}, u32[]{:S(2)}, u32[]{:S(2)}) collective-permute-start(f32[224,128]{1,0:T(8,128)S(1)} %pad_maximum_fusion.1), channel_id=1, source_target_pairs={{0,4},{1,5},{2,6},{3,7},{4,0},{5,1},{6,2},{7,3},{8,12},{9,13},{10,... | collective-permute-start | bytes 344072 | tf_op jit(solution)/shard_map/ppermute | solution.py:318
  55.9 1.4 copy-start
  57.3 1.4 copy-start.1
  85.8 4.2 %collective-permute-start.3 = (f32[1600,128]{1,0:T(8,128)S(1)}, f32[1600,128]{1,0:T(8,128)S(1)}, u32[]{:S(2)}, u32[]{:S(2)}) collective-permute-start(f32[1600,128]{1,0:T(8,128)S(1)} %get-tuple-element.29), channel_id=1, source_target_pairs={{0,8},{8,0},{1,9},{9,1},{2,10},{10,2},{3,11},{11,3},{4,12},{12,4},... | collective-permute-start | bytes 2457608 | tf_op jit(solution)/shard_map/ppermute | solution.py:305
  89.1 25.8 %copy-start.14 = (s32[8]{0:T(128)S(1)}, s32[8]{0:T(128)}, u32[]{:S(2)}) copy-start(s32[8]{0:T(128)} %owner_ref.9) | copy-start | bytes 100
  89.1 25.8 %copy-start.16 = (s32[8]{0:T(128)S(1)}, s32[8]{0:T(128)}, u32[]{:S(2)}) copy-start(s32[8]{0:T(128)} %orders_ref.5) | copy-start | bytes 100
  90.2 58.4 %copy-start.2 = (f32[448,128]{1,0:T(8,128)S(1)}, f32[448,128]{1,0:T(8,128)}, u32[]{:S(2)}) copy-start(f32[448,128]{1,0:T(8,128)} %pad_maximum_fusion.d8_ref) | copy-start | bytes 688132
  90.2 58.4 %copy-start.12 = (s32[64,8]{0,1:T(8,128)S(1)}, s32[64,8]{0,1:T(8,128)}, u32[]{:S(2)}) copy-start(s32[64,8]{0,1:T(8,128)} %param.11) | copy-start | bytes 6148
  149.5 77.6 %copy-start.7 = (f32[50,128]{1,0:T(8,128)}, f32[50,128]{1,0:T(8,128)S(1)}, u32[]{:S(2)}) copy-start(f32[50,128]{1,0:T(8,128)S(1)} %get-tuple-element.39.t_ref) | copy-start | bytes 76804
  198.3 4.2 %collective-permute-start.4 = (f32[1600,128]{1,0:T(8,128)S(1)}, f32[1600,128]{1,0:T(8,128)S(1)}, u32[]{:S(2)}, u32[]{:S(2)}) collective-permute-start(f32[1600,128]{1,0:T(8,128)S(1)} %get-tuple-element.35), channel_id=1, source_target_pairs={{0,8},{8,0},{1,9},{9,1},{2,10},{10,2},{3,11},{11,3},{4,12},{12,4},... | collective-permute-start | bytes 2457608 | tf_op jit(solution)/shard_map/ppermute | solution.py:305
  201.6 25.6 %copy-start.4 = (f32[50,128]{1,0:T(8,128)S(1)}, f32[50,128]{1,0:T(8,128)}, u32[]{:S(2)}) copy-start(f32[50,128]{1,0:T(8,128)} %copy-done.3) | copy-start | bytes 76804
  202.6 53.4 %copy-start.6 = (f32[56,128]{1,0:T(8,128)S(1)}, f32[56,128]{1,0:T(8,128)}, u32[]{:S(2)}) copy-start(f32[56,128]{1,0:T(8,128)} %copy-done.5) | copy-start | bytes 86020
  256.0 0.7 copy-start.8

commit v2 on v1

--- a/solution.py
+++ b/solution.py
@@ -14,6 +14,7 @@
 LANES = 128
 VMEM = pl.BlockSpec(memory_space=pltpu.VMEM)
 SMEM = pl.BlockSpec(memory_space=pltpu.SMEM)
+ANY = pl.BlockSpec(memory_space=pl.ANY)
 
 
 def up8(n):
@@ -52,12 +53,26 @@
     return out
 
 
-def prep_kernel(per_row, nsec, pad, owner_ref, orders_ref, psi_ref, den_ref, v_ref, v_out_ref, d_out_ref):
+def prep_kernel(per_row, nsec, pad, owner_in, orders_in, source_in, psi_in, den_in, v_ref, v_out_ref, d_out_ref, slots_ref, owner_ref, orders_ref, source_ref, psi_ref, den_ref, sems):
+    ends = ((owner_in, owner_ref), (orders_in, orders_ref), (source_in, source_ref), (psi_in, psi_ref), (den_in, den_ref))
+    copies = [pltpu.make_async_copy(src, dst, sems.at[i]) for i, (src, dst) in enumerate(ends)]
+    for c in copies:
+        c.start()
     rows, width = psi_ref.shape[0], psi_ref.shape[2]
     lines = rows * per_row
-    order = orders_ref[sector_at(owner_ref, lax.axis_index("sec"), nsec)]
+    if pad > lines:
+        for y in range(nsec):
+            v_out_ref[y * pad + lines : (y + 1) * pad, :] = jnp.zeros((pad - lines, LANES), jnp.float32)
+        d_out_ref[lines:pad, :] = jnp.ones((pad - lines, LANES), jnp.float32)
     row = lax.broadcasted_iota(jnp.int32, (rows, width), 0) + op_position() * rows
     col = lax.broadcasted_iota(jnp.int32, (rows, width), 1)
+    for c in copies:
+        c.wait()
+    sector = sector_at(owner_ref, lax.axis_index("sec"), nsec)
+    order = orders_ref[sector]
+    for t in range(slots_ref.shape[0] - 1):
+        slots_ref[t] = owner_ref[source_ref[sector, t]]
+    slots_ref[slots_ref.shape[0] - 1] = order
     v = jnp.where((row < order) & (col < order), psi_ref[:, 0, :], 0.0)
     d = den_ref[:, 0, :]
     for k in range(per_row):
@@ -66,25 +81,28 @@
         v_ref[at, :] = v[:, part]
         d_out_ref[at, :] = d[:, part]
         for y in range(nsec):
-            at = pl.ds(y * pad + k, rows, stride=per_row)
-            v_out_ref[at, :] = v[:, part]
-    if pad > lines:
-        for y in range(nsec):
-            v_out_ref[y * pad + lines : (y + 1) * pad, :] = jnp.zeros((pad - lines, LANES), jnp.float32)
-        d_out_ref[lines:pad, :] = jnp.ones((pad - lines, LANES), jnp.float32)
-
-
-def spread(table_ref, owner_ref, source_ref, out_ref, lines, pitch, nsec):
-    sector = sector_at(owner_ref, lax.axis_index("sec"), nsec)
-    for t in range(out_ref.shape[0] // lines):
-        slot = owner_ref[source_ref[sector, t]]
-        start = pl.multiple_of(slot * pitch, 8)
-        out_ref[t * lines : (t + 1) * lines, :] = table_ref[pl.ds(start, lines), :]
-
-
-def select_kernel(lines, pad, nsec, owner_ref, source_ref, v8_ref, d_ref, out_ref, d_out_ref):
-    d_out_ref[...] = d_ref[...]
-    spread(v8_ref, owner_ref, source_ref, out_ref, lines, pad, nsec)
+            v_out_ref[pl.ds(y * pad + k, rows, stride=per_row), :] = v[:, part]
+
+
+PIECES = 4
+
+
+def spread(table_ref, slots_ref, out_ref, lines, pitch, buf_ref, sems):
+    terms = out_ref.shape[0] // lines
+    copies = []
+    for c in range(PIECES):
+        for t in range(c * terms // PIECES, (c + 1) * terms // PIECES):
+            start = pl.multiple_of(slots_ref[t] * pitch, 8)
+            buf_ref[t * lines : (t + 1) * lines, :] = table_ref[pl.ds(start, lines), :]
+        at = pl.ds(c * (terms * lines // PIECES), terms * lines // PIECES)
+        copies.append(pltpu.make_async_copy(buf_ref.at[at], out_ref.at[at], sems.at[c]))
+        copies[-1].start()
+    for c in copies:
+        c.wait()
+
+
+def select_kernel(lines, pad, slots_ref, v8_ref, out_ref, buf_ref, sems):
+    spread(v8_ref, slots_ref, out_ref, lines, pad, buf_ref, sems)
 
 
 def halves(x):
@@ -130,10 +148,16 @@
             out_ref[pl.ds(m * step * per_row + k, step, stride=per_row), :] = y[:, k * LANES : (k + 1) * LANES]
 
 
-def inner_kernel(per_row, x_ref, mats_ref, ih_ref, il_ref, out_ref):
+def inner_kernel(per_row, x_in, mats_ref, ih_ref, il_ref, out_ref, x_ref, sems):
     width = mats_ref.shape[1]
-    step = 160
-    for m in range(width // step):
+    step = width // PIECES
+    copies = []
+    for m in range(PIECES):
+        at = pl.ds(m * step * per_row, step * per_row)
+        copies.append(pltpu.make_async_copy(x_in.at[at], x_ref.at[at], sems.at[m]))
+        copies[-1].start()
+    for m in range(PIECES):
+        copies[m].wait()
         x = jnp.concatenate(
             [x_ref[pl.ds(m * step * per_row + k, step, stride=per_row), :] for k in range(per_row)], axis=1
         )
@@ -147,18 +171,17 @@
     left_product(mats_ref, ih_ref, il_ref, out_ref, mats_ref.shape[1] // 2, per_row)
 
 
-def masked_sum(part_ref, owner_ref, orders_ref, lines, per_row, nsec):
+def masked_sum(part_ref, slots_ref, lines, per_row):
     parts = part_ref.shape[0] // lines
     w = part_ref[0:lines, :]
     for q in range(1, parts):
         w = w + part_ref[q * lines : (q + 1) * lines, :]
-    order = orders_ref[sector_at(owner_ref, lax.axis_index("sec"), nsec)]
-    keep = row_mask(order, lines, per_row, op_position() * (lines // per_row))
+    keep = row_mask(slots_ref[slots_ref.shape[0] - 1], lines, per_row, op_position() * (lines // per_row))
     return jnp.where(keep, w, 0.0)
 
 
-def share_kernel(lines, pad, per_row, nsec, owner_ref, orders_ref, part_ref, w_ref, out_ref):
-    w = masked_sum(part_ref, owner_ref, orders_ref, lines, per_row, nsec)
+def share_kernel(lines, pad, per_row, nsec, slots_ref, part_ref, w_ref, out_ref):
+    w = masked_sum(part_ref, slots_ref, lines, per_row)
     w_ref[...] = w
     for y in range(nsec):
         out_ref[y * pad : y * pad + lines, :] = w
@@ -176,7 +199,7 @@
     out_ref[...] = jnp.broadcast_to(lane_row([total(vv), total(vw)]), out_ref.shape)
 
 
-def update_kernel(lines, pad, nsec, count, owner_ref, source_ref, sums_ref, v8_ref, d8_ref, w8_ref, out_ref, t_ref, scal_ref, t8_ref):
+def update_kernel(lines, pad, nsec, count, slots_ref, sums_ref, v8_ref, d8_ref, w8_ref, out_ref, t_ref, scal_ref, t8_ref, buf_ref, sems):
     sums = jnp.sum(sums_ref[...], axis=0, keepdims=True) / count
     norm, product = sums[:, 0:1], sums[:, 1:2]
     scale = 1.0 / jnp.sqrt(norm + EPS)
@@ -188,25 +211,26 @@
         t8_ref[at, :] = (scale * w8_ref[at, :] - rayleigh * (scale * v8_ref[at, :])) / d8_ref[k * pad : (k + 1) * pad, :]
     t_ref[...] = t8_ref[pl.ds(pl.multiple_of(me * pad, 8), lines), :]
     scal_ref[...] = jnp.broadcast_to(lane_row([norm, product]), scal_ref.shape)
-    spread(t8_ref, owner_ref, source_ref, out_ref, lines, pad, nsec)
-
-
-def last_sums_kernel(lines, per_row, nsec, owner_ref, orders_ref, part_ref, scal_ref, v_ref, w_ref, t_ref, h_ref, out_ref):
-    h = masked_sum(part_ref, owner_ref, orders_ref, lines, per_row, nsec)
-    h_ref[...] = h
+    spread(t8_ref, slots_ref, out_ref, lines, pad, buf_ref, sems)
+
+
+def last_sums_kernel(lines, per_row, pad, slots_ref, part_ref, scal_ref, v_ref, w_ref, t_ref, d_ref, out_ref, keep_ref):
+    h = masked_sum(part_ref, slots_ref, lines, per_row)
     scale = 1.0 / jnp.sqrt(scal_ref[0:1, 0:1] + EPS)
     v0 = scale * v_ref[...]
     w0 = scale * w_ref[...]
     t = t_ref[...]
-    sums = [total(v0 * t), total(t * t), total(t * w0), total(t * h), total(v0 * h)]
-    out_ref[...] = jnp.broadcast_to(lane_row(sums), out_ref.shape)
-
-
-def final_kernel(count, per_row, sums_ref, scal_ref, v_ref, w_ref, t_ref, h_ref, d_ref, new_ref, corr_ref, new_lines, corr_lines):
-    norm, product = scal_ref[0:1, 0:1], scal_ref[0:1, 1:2]
+    for i, x in enumerate((v0, w0, t, h, d_ref[0:lines, :])):
+        keep_ref[i * pad : i * pad + lines, :] = x
+    keep_ref[5 * pad : 5 * pad + 8, :] = scal_ref[...]
+    out_ref[...] = lane_row([total(v0 * t), total(t * t), total(t * w0), total(t * h), total(v0 * h)])
+
+
+def final_kernel(count, per_row, lines, pad, sums_ref, keep_ref, new_ref, corr_ref, new_lines, corr_lines):
+    norm, product = keep_ref[5 * pad : 5 * pad + 1, 0:1], keep_ref[5 * pad : 5 * pad + 1, 1:2]
+    v0, w0, t, h, d = (keep_ref[i * pad : i * pad + lines, :] for i in range(5))
     sums = jnp.sum(sums_ref[...], axis=0, keepdims=True) / count
     along, tt, tw, th, vh = (sums[:, i : i + 1] for i in range(5))
-    scale = 1.0 / jnp.sqrt(norm + EPS)
     rayleigh = product / (norm + EPS)
     vv = norm / (norm + EPS)
     tail = tt - 2.0 * along * along + along * along * vv
@@ -226,15 +250,13 @@
     ahead = xs > 0.0
     cosine = jnp.where(ahead, major, minor)
     sine = jnp.where(ys < 0.0, -1.0, 1.0) * jnp.where(ahead, minor, major)
-    v0 = scale * v_ref[...]
-    w0 = scale * w_ref[...]
-    v1 = inv * (t_ref[...] - along * v0)
-    w1 = inv * (h_ref[...] - along * w0)
+    v1 = inv * (t - along * v0)
+    w1 = inv * (h - along * w0)
     new = sine * v0 - cosine * v1
     applied = sine * w0 - cosine * w1
     lam = sine * sine * rayleigh + cosine * cosine * corner - 2.0 * sine * cosine * couple
     new_lines[...] = new
-    corr_lines[...] = (applied - lam * new) / d_ref[0 : new.shape[0], :]
+    corr_lines[...] = (applied - lam * new) / d
     rows = new_ref.shape[0]
     for k in range(per_row):
         at, part = pl.ds(k, rows, stride=per_row), slice(k * LANES, (k + 1) * LANES)
@@ -250,15 +272,17 @@
     return jax.ShapeDtypeStruct(shape, jnp.bfloat16)
 
 
-def call(kernel, out, smem, vmem, scratch=()):
+def call(kernel, out, smem, vmem, scratch=(), anywhere=(), out_anywhere=0, out_smem=0, limit=32 * 1024 * 1024):
+    outs = out if isinstance(out, tuple) else (out,)
+    specs = [ANY] * out_anywhere + [VMEM] * (len(outs) - out_anywhere - out_smem) + [SMEM] * out_smem
     return pl.pallas_call(
         kernel,
         out_shape=out,
-        in_specs=[SMEM] * len(smem) + [VMEM] * len(vmem),
-        out_specs=jax.tree.map(lambda _: VMEM, out),
+        in_specs=[SMEM] * len(smem) + [ANY] * len(anywhere) + [VMEM] * len(vmem),
+        out_specs=tuple(specs) if isinstance(out, tuple) else specs[0],
         scratch_shapes=scratch,
-        compiler_params=pltpu.CompilerParams(vmem_limit_bytes=32 * 1024 * 1024),
-    )(*smem, *vmem)
+        compiler_params=pltpu.CompilerParams(vmem_limit_bytes=limit),
+    )(*smem, *anywhere, *vmem)
 
 
 def exchange(x, axis, parts):
@@ -283,11 +307,27 @@
     part = functools.partial
     swap = [(0, 1), (1, 0)]
 
-    v, v_out, d_out = call(
+    v, v_out, d_out, slots = call(
         part(prep_kernel, per_row, nsec, pad),
-        (f32(lines, LANES), f32(nsec * pad, LANES), f32(pad, LANES)),
-        (owner, orders),
-        (psi, denominators),
+        (
+            f32(lines, LANES),
+            f32(nsec * pad, LANES),
+            f32(pad, LANES),
+            jax.ShapeDtypeStruct((nop + 1,), jnp.int32),
+        ),
+        (),
+        (),
+        limit=None,
+        out_smem=1,
+        anywhere=(owner, orders, source, psi, denominators),
+        scratch=[
+            pltpu.SMEM((nsec,), jnp.int32),
+            pltpu.SMEM((nsec,), jnp.int32),
+            pltpu.SMEM(source.shape, jnp.int32),
+            pltpu.VMEM(psi.shape, jnp.float32),
+            pltpu.VMEM(psi.shape, jnp.float32),
+            pltpu.SemaphoreType.DMA((5,)),
+        ],
     )
     v8 = exchange(v_out, "sec", nsec)
     square = bf16(width, width)
@@ -300,18 +340,25 @@
         scratch=[pltpu.VMEM((width, width), jnp.float32)],
     )
 
+    whole = [pltpu.VMEM((nop * lines, LANES), jnp.float32), pltpu.SemaphoreType.DMA((PIECES,))]
+
     def products(x):
-        ih, il, other = call(part(inner_kernel, per_row), (square, square, half), (), (x, mats))
+        ih, il, other = call(
+            part(inner_kernel, per_row), (square, square, half), (), (mats,), anywhere=(x,), scratch=whole
+        )
         came = lax.ppermute(other, "op_2", swap)
         own = call(part(own_kernel, per_row), half, (), (mats, ih, il))
         return exchange(own + came, CHIP, nchip)
 
-    chosen, d8 = call(
-        part(select_kernel, lines, pad, nsec),
-        (f32(nop * lines, LANES), f32(pad, LANES)),
-        (owner, source),
-        (v8, d_out),
-    )
+    chosen = call(
+        part(select_kernel, lines, pad),
+        f32(nop * lines, LANES),
+        (slots,),
+        (v8,),
+        scratch=whole,
+        out_anywhere=1,
+    )
+    chosen, d8 = lax.optimization_barrier((chosen, d_out))
     chosen = exchange(chosen, OP, nop)
     reach = 1
     while reach < nsec:
@@ -323,7 +370,7 @@
     w, w_out = call(
         part(share_kernel, lines, pad, per_row, nsec),
         (f32(lines, LANES), f32(nsec * pad, LANES)),
-        (owner, orders),
+        (slots,),
         (parts,),
     )
     w8 = exchange(w_out, "sec", nsec)
@@ -332,25 +379,26 @@
     chosen, t, scal = call(
         part(update_kernel, lines, pad, nsec, count),
         (f32(nop * lines, LANES), f32(lines, LANES), f32(8, LANES)),
-        (owner, source),
+        (slots,),
         (sums, v8, d8, w8),
-        scratch=[pltpu.VMEM((nsec * pad, LANES), jnp.float32)],
+        scratch=[pltpu.VMEM((nsec * pad, LANES), jnp.float32), *whole],
+        out_anywhere=1,
     )
     parts = products(exchange(chosen, OP, nop))
-    h, sums = call(
-        part(last_sums_kernel, lines, per_row, nsec),
-        (f32(lines, LANES), f32(1, LANES)),
-        (owner, orders),
-        (parts, scal, v, w, t),
+    sums, keep = call(
+        part(last_sums_kernel, lines, per_row, pad),
+        (f32(1, LANES), f32(5 * pad + 8, LANES)),
+        (slots,),
+        (parts, scal, v, w, t, d_out),
     )
     chips = nchip * nsec
     sums = jnp.broadcast_to(lax.psum(sums, "op_2"), (chips, LANES))
     sums = exchange(sums, (*CHIP, "sec"), chips)
     return call(
-        part(final_kernel, count, per_row),
+        part(final_kernel, count, per_row, lines, pad),
         (f32(*psi.shape), f32(*psi.shape)),
         (),
-        (sums, scal, v, w, t, h, d_out),
+        (sums, keep),
         scratch=[pltpu.VMEM((lines, LANES), jnp.float32)] * 2,
     )
 

time: 259 us -> 259 us (level)
  local copies, waits for them, and re-layouts: 7.19 us -> 3.6 us
  Pallas kernels: 18.1 us -> 21.3 us
    unnamed x34 -> x14, local copies, waits for them, and re-layouts: 7.12 us -> 3.53 us
    pallas_call x12, Pallas kernels: 18.1 us -> 21.3 us  [call(): pl.pallas_call(kernel, out_shape=out, in_specs=[SMEM] * len(smem) + [ANY]...]
where the time goes in v2:
time: 259 us; the launch traced here: 258 us
  blocking collectives  172 us (66%)
  waiting for transfers between devices  32.4 us (13%)
  starting transfers between devices  26.6 us (10%)
  Pallas kernels  21.3 us (8%)
  local copies, waits for them, and re-layouts  3.6 us (1%)
    all_to_all x7, blocking collectives, exchange(): lax.all_to_all(x.reshape(parts, lines, 1, LANES), axis, 0, 0, tiled=True)  165 us
    pallas_call x12, Pallas kernels, call(): pl.pallas_call(kernel, out_shape=out, in_specs=[SMEM] * len(smem) + [ANY]...  21.3 us
    all_to_all x1, starting transfers between devices, exchange(): lax.all_to_all(x.reshape(parts, lines, 1, LANES), axis, 0, 0, tiled=True)  16.6 us
    ppermute x3, waiting for transfers between devices, per_device(): lax.ppermute(d8, 'sec', [(i, (i + reach) % nsec) for i in range(nsec)])  15.6 us
    all_to_all x1, waiting for transfers between devices, exchange(): lax.all_to_all(x.reshape(parts, lines, 1, LANES), axis, 0, 0, tiled=True)  15 us
    psum x1, blocking collectives, per_device(): sums = jnp.broadcast_to(lax.psum(sums, 'op_2'), (chips, LANES))  6.75 us
    ppermute x3, starting transfers between devices, per_device(): lax.ppermute(d8, 'sec', [(i, (i + reach) % nsec) for i in range(nsec)])  6.02 us
  transfers between devices with their start and end apart: 6, of which 6 were waited for; matrix products, arithmetic and copies ran while one was open for 0% of the time, Pallas kernels for 1%

profile of v2, /device:TPU:1, one launch (start us, length us, event | category | flops | bytes accessed | tf_op | source)
XLA Modules:
  0.0 257.7 jit_solution(4813621885013090130)
XLA Ops:
  0.6 1.6 shard_map.86
  2.2 16.7 %all_to_all.40 = f32[8,56,1,128]{3,1,2,0:T(8,128)S(1)} all-to-all(f32[8,56,1,128]{3,1,2,0:T(8,128)} %bitcast.43), channel_id=1, replica_groups=mesh['op_0'=4,'op_1'=8,'op_2'=2,'sec'=8] {'sec'}, dimensions={0} | all-to-all | bytes 458752 | tf_op jit(solution)/shard_map/all_to_all | solution.py:290
  18.9 0.0 copy-start.5
  18.9 0.7 copy-done.5
  19.5 1.8 shard_map.88
  21.3 0.0 copy-start.3
  21.3 16.6 %all-to-all-start.1 = ((f32[64,50,1,128]{3,2,1,0:T(1,128)}), f32[64,50,1,128]{3,2,1,0:T(1,128)}, u32[]{:S(2)}, u32[]{:S(2)}) async-start(f32[64,50,1,128]{3,2,1,0:T(1,128)} %bitcast.6), calls=%async_computation.1 | async-start | bytes 3276800 | tf_op jit(solution)/shard_map/all_to_all | solution.py:290
  37.9 0.0 copy-done.3
  38.0 2.2 collective-permute-start
  40.2 4.0 %collective-permute-done = f32[56,128]{1,0:T(8,128)S(1)} collective-permute-done((f32[56,128]{1,0:T(8,128)S(1)}, f32[56,128]{1,0:T(8,128)S(1)}, u32[]{:S(2)}, u32[]{:S(2)}) %collective-permute-start) | collective-permute-done | bytes 28704 | tf_op jit(solution)/shard_map/ppermute | solution.py:365
  44.2 1.9 collective-permute-start.1
  46.1 6.1 %collective-permute-done.1 = f32[112,128]{1,0:T(8,128)S(1)} collective-permute-done((f32[112,128]{1,0:T(8,128)S(1)}, f32[112,128]{1,0:T(8,128)S(1)}, u32[]{:S(2)}, u32[]{:S(2)}) %collective-permute-start.1) | collective-permute-done | bytes 57376 | tf_op jit(solution)/shard_map/ppermute | solution.py:365
  52.2 1.9 collective-permute-start.2
  54.1 0.0 copy-start
  54.1 1.4 copy-done
  55.6 0.0 copy-start.1
  55.6 1.4 copy-done.1
  57.0 0.9 shard_map.87.mats_ref
  57.9 5.5 %collective-permute-done.2 = f32[224,128]{1,0:T(8,128)S(1)} collective-permute-done((f32[224,128]{1,0:T(8,128)S(1)}, f32[224,128]{1,0:T(8,128)S(1)}, u32[]{:S(2)}, u32[]{:S(2)}) %collective-permute-start.2) | collective-permute-done | bytes 114720 | tf_op jit(solution)/shard_map/ppermute | solution.py:365
  63.4 0.7 pad_maximum_fusion.d8_ref
  64.1 15.0 %all-to-all-done.1 = f32[64,50,1,128]{3,2,1,0:T(1,128)} async-done(((f32[64,50,1,128]{3,2,1,0:T(1,128)}), f32[64,50,1,128]{3,2,1,0:T(1,128)}, u32[]{:S(2)}, u32[]{:S(2)}) %all-to-all-start.1) | async-done | bytes 1638432 | tf_op jit(solution)/shard_map/all_to_all | solution.py:290
  79.0 5.1 %shard_map.89 = (bf16[640,640]{1,0:T(8,128)(2,1)S(1)}, bf16[640,640]{1,0:T(8,128)(2,1)S(1)}, f32[1600,128]{1,0:T(8,128)S(1)}) custom-call(f32[3200,128]{1,0:T(8,128)} %bitcast.7.x_in, bf16[4,640,640]{2,1,0:T(8,128)(2,1)S(1)} %shard_map.87.mats_ref), custom_call_target="tpu_custom_call" | custom-call | tf_op jit(solution)/shard_map/pallas_call | solution.py:278
  84.2 1.9 collective-permute-start.3
  86.1 1.3 shard_map.90
  87.4 0.0 copy-start.6
  87.5 1.0 collective-permute-done.3
  88.4 0.1 add.8
  88.5 0.0 copy-start.2
  88.5 24.7 %all_to_all.41 = f32[32,50,1,128]{3,2,1,0:T(1,128)S(1)} all-to-all(f32[32,50,1,128]{3,2,1,0:T(1,128)S(1)} %bitcast.41), channel_id=1, replica_groups=mesh['op_0'=4,'op_1'=8,'op_2'=2,'sec'=8] {'op_0','op_1'}, dimensions={0} | all-to-all | bytes 1638400 | tf_op jit(solution)/shard_map/all_to_all | solution.py:290
  113.2 0.0 copy-done.6
  113.2 0.6 shard_map.91
  113.8 11.4 %all_to_all.42 = f32[8,56,1,128]{3,1,2,0:T(8,128)S(1)} all-to-all(f32[8,56,1,128]{3,1,2,0:T(8,128)S(1)} %bitcast.37), channel_id=1, replica_groups=mesh['op_0'=4,'op_1'=8,'op_2'=2,'sec'=8] {'sec'}, dimensions={0} | all-to-all | bytes 458752 | tf_op jit(solution)/shard_map/all_to_all | solution.py:290
  125.2 0.1 shard_map.92
  125.3 21.6 %all_to_all.43 = f32[64,1,1,128]{3,2,1,0:T(1,128)S(1)} all-to-all(f32[64,1,1,128]{3,2,1,0:T(1,128)S(1)} %bitcast.39), channel_id=1, replica_groups=mesh['op_0'=4,'op_1'=8,'op_2'=2,'sec'=8] {'op_0','op_1','op_2'}, dimensions={0} | all-to-all | bytes 65536 | tf_op jit(solution)/shard_map/all_to_all | solution.py:290
  146.9 0.0 copy-done.2
  146.9 1.8 shard_map.93
  148.7 45.2 %all_to_all.44 = f32[64,50,1,128]{3,2,1,0:T(1,128)S(1)} all-to-all(f32[64,50,1,128]{3,2,1,0:T(1,128)S(1)} %bitcast.35), channel_id=1, replica_groups=mesh['op_0'=4,'op_1'=8,'op_2'=2,'sec'=8] {'op_0','op_1','op_2'}, dimensions={0} | all-to-all | bytes 3276800 | tf_op jit(solution)/shard_map/all_to_all | solution.py:290
  193.9 5.0 %shard_map.94 = (bf16[640,640]{1,0:T(8,128)(2,1)S(1)}, bf16[640,640]{1,0:T(8,128)(2,1)S(1)}, f32[1600,128]{1,0:T(8,128)S(1)}) custom-call(f32[3200,128]{1,0:T(8,128)S(1)} %bitcast.25, bf16[4,640,640]{2,1,0:T(8,128)(2,1)S(1)} %shard_map.87.mats_ref), custom_call_target="tpu_custom_call" | custom-call | tf_op jit(solution)/shard_map/pallas_call | solution.py:278
  198.8 2.0 collective-permute-start.4
  200.8 1.3 shard_map.95
  202.1 0.0 copy-start.4
  202.2 0.9 collective-permute-done.4
  203.1 0.1 add.9
  203.1 24.6 %all_to_all.45 = f32[32,50,1,128]{3,2,1,0:T(1,128)S(1)} all-to-all(f32[32,50,1,128]{3,2,1,0:T(1,128)S(1)} %bitcast.42), channel_id=1, replica_groups=mesh['op_0'=4,'op_1'=8,'op_2'=2,'sec'=8] {'op_0','op_1'}, dimensions={0} | all-to-all | bytes 1638400 | tf_op jit(solution)/shard_map/all_to_all | solution.py:290
  227.7 0.0 copy-done.4
  227.7 0.7 shard_map.96
  228.4 6.7 %psum.7 = f32[128]{0:T(128)S(1)} all-reduce(f32[128]{0:T(128)S(1)} %bitcast.40), channel_id=1, replica_groups=mesh['op_0'=4,'op_1'=8,'op_2'=2,'sec'=8] {'op_2'}, use_global_device_ids=true, to_apply=%region_0.0 | all-reduce | flops 128 | bytes 1024 | tf_op jit(solution)/shard_map/psum | solution.py:395
  235.2 0.1 reshape.74
  235.3 21.3 %all_to_all.46 = f32[256,1,1,128]{3,2,1,0:T(1,128)S(1)} all-to-all(f32[256,1,1,128]{3,2,1,0:T(1,128)S(1)} %reshape.74), channel_id=1, replica_groups=mesh['op_0'=4,'op_1'=8,'op_2'=2,'sec'=8] {'op_0','op_1','sec'}, dimensions={0} | all-to-all | bytes 262144 | tf_op jit(solution)/shard_map/all_to_all | solution.py:290
  256.5 1.1 shard_map.97
  (2 shorter events, 0.0 us)
Async XLA Ops:
  18.9 0.7 copy-start.5
  21.3 16.6 %copy-start.3 = (f32[56,128]{1,0:T(8,128)S(1)}, f32[56,128]{1,0:T(8,128)}, u32[]{:S(2)}) copy-start(f32[56,128]{1,0:T(8,128)} %get-tuple-element.27.d_ref) | copy-start | bytes 86020
  21.3 57.7 %all-to-all-start.1 = ((f32[64,50,1,128]{3,2,1,0:T(1,128)}), f32[64,50,1,128]{3,2,1,0:T(1,128)}, u32[]{:S(2)}, u32[]{:S(2)}) async-start(f32[64,50,1,128]{3,2,1,0:T(1,128)} %bitcast.6), calls=%async_computation.1 | async-start | bytes 3276800 | tf_op jit(solution)/shard_map/all_to_all | solution.py:290
  38.0 6.2 %collective-permute-start = (f32[56,128]{1,0:T(8,128)S(1)}, f32[56,128]{1,0:T(8,128)S(1)}, u32[]{:S(2)}, u32[]{:S(2)}) collective-permute-start(f32[56,128]{1,0:T(8,128)S(1)} %copy-done.3), channel_id=1, source_target_pairs={{0,1},{1,2},{2,3},{3,4},{4,5},{5,6},{6,7},{7,0},{8,9},{9,10},{10,1... | collective-permute-start | bytes 86024 | tf_op jit(solution)/shard_map/ppermute | solution.py:365
  44.2 8.0 %collective-permute-start.1 = (f32[112,128]{1,0:T(8,128)S(1)}, f32[112,128]{1,0:T(8,128)S(1)}, u32[]{:S(2)}, u32[]{:S(2)}) collective-permute-start(f32[112,128]{1,0:T(8,128)S(1)} %pad_maximum_fusion.2), channel_id=1, source_target_pairs={{0,2},{1,3},{2,4},{3,5},{4,6},{5,7},{6,0},{7,1},{8,10},{9,11},{10,... | collective-permute-start | bytes 172040 | tf_op jit(solution)/shard_map/ppermute | solution.py:365
  52.2 11.2 %collective-permute-start.2 = (f32[224,128]{1,0:T(8,128)S(1)}, f32[224,128]{1,0:T(8,128)S(1)}, u32[]{:S(2)}, u32[]{:S(2)}) collective-permute-start(f32[224,128]{1,0:T(8,128)S(1)} %pad_maximum_fusion.1), channel_id=1, source_target_pairs={{0,4},{1,5},{2,6},{3,7},{4,0},{5,1},{6,2},{7,3},{8,12},{9,13},{10,... | collective-permute-start | bytes 344072 | tf_op jit(solution)/shard_map/ppermute | solution.py:365
  54.1 1.4 copy-start
  55.6 1.4 copy-start.1
  84.2 4.2 %collective-permute-start.3 = (f32[1600,128]{1,0:T(8,128)S(1)}, f32[1600,128]{1,0:T(8,128)S(1)}, u32[]{:S(2)}, u32[]{:S(2)}) collective-permute-start(f32[1600,128]{1,0:T(8,128)S(1)} %get-tuple-element.31), channel_id=1, source_target_pairs={{0,8},{8,0},{1,9},{9,1},{2,10},{10,2},{3,11},{11,3},{4,12},{12,4},... | collective-permute-start | bytes 2457608 | tf_op jit(solution)/shard_map/ppermute | solution.py:349
  87.4 25.7 %copy-start.6 = (s32[65]{0:T(128)S(1)}, s32[65]{0:T(128)}, u32[]{:S(2)}) copy-start(s32[65]{0:T(128)} %get-tuple-element.23.slots_ref) | copy-start | bytes 784
  88.5 58.4 %copy-start.2 = (f32[448,128]{1,0:T(8,128)S(1)}, f32[448,128]{1,0:T(8,128)}, u32[]{:S(2)}) copy-start(f32[448,128]{1,0:T(8,128)} %pad_maximum_fusion.d8_ref) | copy-start | bytes 688132
  198.8 4.2 %collective-permute-start.4 = (f32[1600,128]{1,0:T(8,128)S(1)}, f32[1600,128]{1,0:T(8,128)S(1)}, u32[]{:S(2)}, u32[]{:S(2)}) collective-permute-start(f32[1600,128]{1,0:T(8,128)S(1)} %get-tuple-element.37), channel_id=1, source_target_pairs={{0,8},{8,0},{1,9},{9,1},{2,10},{10,2},{3,11},{11,3},{4,12},{12,4},... | collective-permute-start | bytes 2457608 | tf_op jit(solution)/shard_map/ppermute | solution.py:349
  202.1 25.6 %copy-start.4 = (f32[50,128]{1,0:T(8,128)S(1)}, f32[50,128]{1,0:T(8,128)}, u32[]{:S(2)}) copy-start(f32[50,128]{1,0:T(8,128)} %get-tuple-element.39.v_ref) | copy-start | bytes 76804

commit v3 on v2

--- a/solution.py
+++ b/solution.py
@@ -8,7 +8,6 @@
 from jax.sharding import Mesh
 from jax.sharding import PartitionSpec as P
 
-CHIP = ("op_0", "op_1")
 OP = ("op_0", "op_1", "op_2")
 EPS = 1e-06
 LANES = 128
@@ -64,6 +63,7 @@
         for y in range(nsec):
             v_out_ref[y * pad + lines : (y + 1) * pad, :] = jnp.zeros((pad - lines, LANES), jnp.float32)
         d_out_ref[lines:pad, :] = jnp.ones((pad - lines, LANES), jnp.float32)
+        v_ref[lines:pad, :] = jnp.zeros((pad - lines, LANES), jnp.float32)
     row = lax.broadcasted_iota(jnp.int32, (rows, width), 0) + op_position() * rows
     col = lax.broadcasted_iota(jnp.int32, (rows, width), 1)
     for c in copies:
@@ -148,16 +148,10 @@
             out_ref[pl.ds(m * step * per_row + k, step, stride=per_row), :] = y[:, k * LANES : (k + 1) * LANES]
 
 
-def inner_kernel(per_row, x_in, mats_ref, ih_ref, il_ref, out_ref, x_ref, sems):
+def inner_kernel(per_row, x_ref, mats_ref, ih_ref, il_ref, out_ref):
     width = mats_ref.shape[1]
-    step = width // PIECES
-    copies = []
-    for m in range(PIECES):
-        at = pl.ds(m * step * per_row, step * per_row)
-        copies.append(pltpu.make_async_copy(x_in.at[at], x_ref.at[at], sems.at[m]))
-        copies[-1].start()
-    for m in range(PIECES):
-        copies[m].wait()
+    step = 160
+    for m in range(width // step):
         x = jnp.concatenate(
             [x_ref[pl.ds(m * step * per_row + k, step, stride=per_row), :] for k in range(per_row)], axis=1
         )
@@ -171,32 +165,64 @@
     left_product(mats_ref, ih_ref, il_ref, out_ref, mats_ref.shape[1] // 2, per_row)
 
 
-def masked_sum(part_ref, slots_ref, lines, per_row):
-    parts = part_ref.shape[0] // lines
-    w = part_ref[0:lines, :]
-    for q in range(1, parts):
-        w = w + part_ref[q * lines : (q + 1) * lines, :]
+def ring_slot(k, count):
+    ahead = count // 2
+    shift = -k if k <= ahead else k - ahead
+    return lax.rem(lax.axis_index("op_1") + shift + count, count)
+
+
+def fold(part_ref, out_ref, lines, pad, nz):
+    nx = part_ref.shape[0] // (nz * lines)
+    for z in range(nz):
+        x = part_ref[z * lines : (z + 1) * lines, :]
+        for i in range(1, nx):
+            x = x + part_ref[(i * nz + z) * lines : (i * nz + z + 1) * lines, :]
+        out_ref[z * pad : z * pad + lines, :] = x
+        out_ref[z * pad + lines : (z + 1) * pad, :] = jnp.zeros((pad - lines, LANES), jnp.float32)
+
+
+def ring_dot(ring, out_ref, lines, pad):
+    acc = jnp.zeros((lines, LANES), jnp.float32)
+    for k, ref in enumerate(ring):
+        at = pl.ds(pl.multiple_of(ring_slot(k, len(ring)) * pad, 8), lines)
+        acc = acc + ref[0:lines, :] * out_ref[at, :]
+    return total(acc)
+
+
+def put_line(out_ref, row, lines, pad):
+    for b in range(out_ref.shape[0] // pad):
+        out_ref[b * pad + lines : b * pad + lines + 1, :] = row
+
+
+def first_fold_kernel(lines, pad, nz, part_ref, *refs):
+    ring, out_ref = refs[:nz], refs[nz]
+    fold(part_ref, out_ref, lines, pad, nz)
+    own = ring[0][...]
+    put_line(out_ref, lane_row([total(own * own), ring_dot(ring, out_ref, lines, pad)]), lines, pad)
+
+
+def masked_sum(msg_ref, slots_ref, lines, pad, per_row):
+    w = msg_ref[0:pad, :]
+    for q in range(1, msg_ref.shape[0] // pad):
+        w = w + msg_ref[q * pad : (q + 1) * pad, :]
     keep = row_mask(slots_ref[slots_ref.shape[0] - 1], lines, per_row, op_position() * (lines // per_row))
-    return jnp.where(keep, w, 0.0)
-
-
-def share_kernel(lines, pad, per_row, nsec, slots_ref, part_ref, w_ref, out_ref):
-    w = masked_sum(part_ref, slots_ref, lines, per_row)
+    return jnp.where(keep, w[0:lines, :], 0.0), w[lines : lines + 1, :]
+
+
+def share_kernel(lines, pad, per_row, nsec, slots_ref, msg_ref, w_ref, out_ref):
+    w, row = masked_sum(msg_ref, slots_ref, lines, pad, per_row)
     w_ref[...] = w
     for y in range(nsec):
         out_ref[y * pad : y * pad + lines, :] = w
-        if pad > lines:
-            out_ref[y * pad + lines : (y + 1) * pad, :] = jnp.zeros((pad - lines, LANES), jnp.float32)
-
-
-def first_sums_kernel(pad, nsec, v8_ref, w8_ref, out_ref):
-    vv = jnp.zeros((pad, LANES), jnp.float32)
-    vw = jnp.zeros((pad, LANES), jnp.float32)
-    for y in range(nsec):
-        v = v8_ref[y * pad : (y + 1) * pad, :]
-        vv = vv + v * v
-        vw = vw + v * w8_ref[y * pad : (y + 1) * pad, :]
-    out_ref[...] = jnp.broadcast_to(lane_row([total(vv), total(vw)]), out_ref.shape)
+        out_ref[y * pad + lines : (y + 1) * pad, :] = jnp.zeros((pad - lines, LANES), jnp.float32)
+    put_line(out_ref, row, lines, pad)
+
+
+def first_sums_kernel(lines, pad, w8_ref, out_ref):
+    row = w8_ref[lines : lines + 1, :]
+    for y in range(1, w8_ref.shape[0] // pad):
+        row = row + w8_ref[y * pad + lines : y * pad + lines + 1, :]
+    out_ref[...] = jnp.broadcast_to(row, out_ref.shape)
 
 
 def update_kernel(lines, pad, nsec, count, slots_ref, sums_ref, v8_ref, d8_ref, w8_ref, out_ref, t_ref, scal_ref, t8_ref, buf_ref, sems):
@@ -209,21 +235,30 @@
         slot = lax.rem(me + nsec - k, nsec)
         at = pl.ds(pl.multiple_of(slot * pad, 8), pad)
         t8_ref[at, :] = (scale * w8_ref[at, :] - rayleigh * (scale * v8_ref[at, :])) / d8_ref[k * pad : (k + 1) * pad, :]
-    t_ref[...] = t8_ref[pl.ds(pl.multiple_of(me * pad, 8), lines), :]
+    t_ref[...] = t8_ref[pl.ds(pl.multiple_of(me * pad, 8), pad), :]
     scal_ref[...] = jnp.broadcast_to(lane_row([norm, product]), scal_ref.shape)
     spread(t8_ref, slots_ref, out_ref, lines, pad, buf_ref, sems)
 
 
-def last_sums_kernel(lines, per_row, pad, slots_ref, part_ref, scal_ref, v_ref, w_ref, t_ref, d_ref, out_ref, keep_ref):
-    h = masked_sum(part_ref, slots_ref, lines, per_row)
+def last_fold_kernel(lines, pad, nz, part_ref, scal_ref, w_ref, *refs):
+    v_ring, t_ring, out_ref = refs[:nz], refs[nz : 2 * nz], refs[2 * nz]
+    fold(part_ref, out_ref, lines, pad, nz)
     scale = 1.0 / jnp.sqrt(scal_ref[0:1, 0:1] + EPS)
-    v0 = scale * v_ref[...]
+    v0 = scale * v_ring[0][0:lines, :]
     w0 = scale * w_ref[...]
-    t = t_ref[...]
-    for i, x in enumerate((v0, w0, t, h, d_ref[0:lines, :])):
+    t = t_ring[0][0:lines, :]
+    th = ring_dot(t_ring, out_ref, lines, pad)
+    vh = scale * ring_dot(v_ring, out_ref, lines, pad)
+    put_line(out_ref, lane_row([total(v0 * t), total(t * t), total(t * w0), th, vh]), lines, pad)
+
+
+def last_sums_kernel(lines, per_row, pad, slots_ref, msg_ref, scal_ref, v_ref, w_ref, t_ref, d_ref, out_ref, keep_ref):
+    h, row = masked_sum(msg_ref, slots_ref, lines, pad, per_row)
+    scale = 1.0 / jnp.sqrt(scal_ref[0:1, 0:1] + EPS)
+    for i, x in enumerate((scale * v_ref[0:lines, :], scale * w_ref[...], t_ref[0:lines, :], h, d_ref[0:lines, :])):
         keep_ref[i * pad : i * pad + lines, :] = x
     keep_ref[5 * pad : 5 * pad + 8, :] = scal_ref[...]
-    out_ref[...] = lane_row([total(v0 * t), total(t * t), total(t * w0), total(t * h), total(v0 * h)])
+    out_ref[...] = jnp.broadcast_to(row, out_ref.shape)
 
 
 def final_kernel(count, per_row, lines, pad, sums_ref, keep_ref, new_ref, corr_ref, new_lines, corr_lines):
@@ -296,9 +331,10 @@
     width = psi.shape[2]
     per_row = width // LANES
     lines = rows * per_row
-    pad = up8(lines)
+    pad = up8(lines + 1)
     nop = lax.axis_size(OP)
-    nchip = lax.axis_size(CHIP)
+    nx = lax.axis_size("op_0")
+    nz = lax.axis_size("op_1")
     nsec = lax.axis_size("sec")
     count = float(width * nsec * width)
     left = left_env.reshape(width, width)
@@ -310,7 +346,7 @@
     v, v_out, d_out, slots = call(
         part(prep_kernel, per_row, nsec, pad),
         (
-            f32(lines, LANES),
+            f32(pad, LANES),
             f32(nsec * pad, LANES),
             f32(pad, LANES),
             jax.ShapeDtypeStruct((nop + 1,), jnp.int32),
@@ -343,12 +379,18 @@
     whole = [pltpu.VMEM((nop * lines, LANES), jnp.float32), pltpu.SemaphoreType.DMA((PIECES,))]
 
     def products(x):
-        ih, il, other = call(
-            part(inner_kernel, per_row), (square, square, half), (), (mats,), anywhere=(x,), scratch=whole
-        )
+        ih, il, other = call(part(inner_kernel, per_row), (square, square, half), (), (x, mats))
         came = lax.ppermute(other, "op_2", swap)
         own = call(part(own_kernel, per_row), half, (), (mats, ih, il))
-        return exchange(own + came, CHIP, nchip)
+        return exchange(own + came, "op_0", nx)
+
+    def round_z(x):
+        ahead, behind = [x], [x]
+        for _ in range(nz // 2):
+            ahead.append(lax.ppermute(ahead[-1], "op_1", [(i, (i + 1) % nz) for i in range(nz)]))
+        for _ in range((nz - 1) // 2):
+            behind.append(lax.ppermute(behind[-1], "op_1", [(i, (i - 1) % nz) for i in range(nz)]))
+        return ahead + behind[1:]
 
     chosen = call(
         part(select_kernel, lines, pad),
@@ -358,47 +400,57 @@
         scratch=whole,
         out_anywhere=1,
     )
-    chosen, d8 = lax.optimization_barrier((chosen, d_out))
+    chosen, d8, v = lax.optimization_barrier((chosen, d_out, v))
     chosen = exchange(chosen, OP, nop)
     reach = 1
     while reach < nsec:
         came = lax.ppermute(d8, "sec", [(i, (i + reach) % nsec) for i in range(nsec)])
         d8 = jnp.concatenate([d8, came], axis=0)
         reach *= 2
-    chosen, d8 = lax.optimization_barrier((chosen, d8))
+    chosen, d8, *v_ring = lax.optimization_barrier((chosen, d8, *round_z(v)))
     parts = products(chosen)
+    sums = call(part(first_fold_kernel, lines, pad, nz), f32(nz * pad, LANES), (), (parts, *v_ring))
     w, w_out = call(
         part(share_kernel, lines, pad, per_row, nsec),
         (f32(lines, LANES), f32(nsec * pad, LANES)),
         (slots,),
-        (parts,),
+        (exchange(sums, "op_1", nz),),
     )
     w8 = exchange(w_out, "sec", nsec)
-    sums = call(part(first_sums_kernel, pad, nsec), f32(nop, LANES), (), (v8, w8))
-    sums = exchange(sums, OP, nop)
+    near = ("op_0", "op_2")
+    count_near = lax.axis_size(near)
+    sums = call(part(first_sums_kernel, lines, pad), f32(count_near, LANES), (), (w8,))
+    sums = exchange(sums, near, count_near)
     chosen, t, scal = call(
         part(update_kernel, lines, pad, nsec, count),
-        (f32(nop * lines, LANES), f32(lines, LANES), f32(8, LANES)),
+        (f32(nop * lines, LANES), f32(pad, LANES), f32(8, LANES)),
         (slots,),
         (sums, v8, d8, w8),
+        limit=52 * 1024 * 1024,
         scratch=[pltpu.VMEM((nsec * pad, LANES), jnp.float32), *whole],
         out_anywhere=1,
     )
-    parts = products(exchange(chosen, OP, nop))
+    chosen, *t_ring = lax.optimization_barrier((exchange(chosen, OP, nop), *round_z(t)))
+    parts = products(chosen)
+    sums = call(
+        part(last_fold_kernel, lines, pad, nz),
+        f32(nz * pad, LANES),
+        (),
+        (parts, scal, w, *v_ring, *t_ring),
+    )
+    near = ("op_0", "op_2", "sec")
+    count_near = lax.axis_size(near)
     sums, keep = call(
         part(last_sums_kernel, lines, per_row, pad),
-        (f32(1, LANES), f32(5 * pad + 8, LANES)),
+        (f32(count_near, LANES), f32(5 * pad + 8, LANES)),
         (slots,),
-        (parts, scal, v, w, t, d_out),
-    )
-    chips = nchip * nsec
-    sums = jnp.broadcast_to(lax.psum(sums, "op_2"), (chips, LANES))
-    sums = exchange(sums, (*CHIP, "sec"), chips)
+        (exchange(sums, "op_1", nz), scal, v, w, t, d_out),
+    )
     return call(
         part(final_kernel, count, per_row, lines, pad),
         (f32(*psi.shape), f32(*psi.shape)),
         (),
-        (sums, keep),
+        (exchange(sums, near, count_near), keep),
         scratch=[pltpu.VMEM((lines, LANES), jnp.float32)] * 2,
     )
 

time: 259 us -> 292 us (1.13)
  starting transfers between devices: 26.6 us -> 83.8 us
  blocking collectives: 172 us -> 115 us
  waiting for transfers between devices: 32.4 us -> 62 us
  local copies, waits for them, and re-layouts: 3.6 us -> 6.66 us
    ppermute x0 -> x14, waiting for transfers between devices: none -> 50.8 us  [the longest x8 50.8 us: round_z(): lax.ppermute(ahead[-1], 'op_1', [(i, (i + 1) % nz) for i in range(nz)])]
    all_to_all x7 -> x8, blocking collectives: 165 us -> 115 us  [exchange(): lax.all_to_all(x.reshape(parts, lines, 1, LANES), axis, 0, 0, tiled=True)]
    ppermute x0 -> x14, starting transfers between devices: none -> 42.9 us  [the longest x6 24.7 us: round_z(): lax.ppermute(behind[-1], 'op_1', [(i, (i - 1) % nz) for i in range(nz)])]
    all_to_all x1 -> x2, waiting for transfers between devices: 15 us -> 0.01 us  [exchange(): lax.all_to_all(x.reshape(parts, lines, 1, LANES), axis, 0, 0, tiled=True)]
    ppermute x2, starting transfers between devices: 3.95 us -> 12.4 us  [products(): came = lax.ppermute(other, 'op_2', swap)]
    psum x1 -> x0, blocking collectives: 6.75 us -> none  [per_device(): sums = jnp.broadcast_to(lax.psum(sums, 'op_2'), (chips, LANES))]
    all_to_all x1 -> x2, starting transfers between devices: 16.6 us -> 22.5 us  [exchange(): lax.all_to_all(x.reshape(parts, lines, 1, LANES), axis, 0, 0, tiled=True)]
    ppermute x3, waiting for transfers between devices: 15.6 us -> 10.1 us  [per_device(): lax.ppermute(d8, 'sec', [(i, (i + reach) % nsec) for i in range(nsec)])]
  transfers between devices with their start and end apart: 6 -> 21, of which waited for: 6 -> 8; matrix products, arithmetic and copies ran while one was open for 0% -> 0% of each run, Pallas kernels for 1% -> 1%
where the time goes in v3:
time: 292 us; the launch traced here: 291 us
  blocking collectives  115 us (39%)
  starting transfers between devices  83.8 us (29%)
  waiting for transfers between devices  62 us (21%)
  Pallas kernels  21.7 us (7%)
  local copies, waits for them, and re-layouts  6.66 us (2%)
    all_to_all x8, blocking collectives, exchange(): lax.all_to_all(x.reshape(parts, lines, 1, LANES), axis, 0, 0, tiled=True)  115 us
    ppermute x8, waiting for transfers between devices, round_z(): lax.ppermute(ahead[-1], 'op_1', [(i, (i + 1) % nz) for i in range(nz)])  50.8 us
    ppermute x6, starting transfers between devices, round_z(): lax.ppermute(behind[-1], 'op_1', [(i, (i - 1) % nz) for i in range(nz)])  24.7 us
    all_to_all x2, starting transfers between devices, exchange(): lax.all_to_all(x.reshape(parts, lines, 1, LANES), axis, 0, 0, tiled=True)  22.5 us
    pallas_call x14, Pallas kernels, call(): pl.pallas_call(kernel, out_shape=out, in_specs=[SMEM] * len(smem) + [ANY]...  21.7 us
    ppermute x8, starting transfers between devices, round_z(): lax.ppermute(ahead[-1], 'op_1', [(i, (i + 1) % nz) for i in range(nz)])  18.2 us
    ppermute x2, starting transfers between devices, products(): came = lax.ppermute(other, 'op_2', swap)  12.4 us
    ppermute x3, waiting for transfers between devices, per_device(): lax.ppermute(d8, 'sec', [(i, (i + reach) % nsec) for i in range(nsec)])  10.1 us
  transfers between devices with their start and end apart: 21, of which 8 were waited for; matrix products, arithmetic and copies ran while one was open for 0% of the time, Pallas kernels for 1%

profile of v3, /device:TPU:1, one launch (start us, length us, event | category | flops | bytes accessed | tf_op | source)
XLA Modules:
  0.0 290.9 jit_solution(2831554194235514940)
XLA Ops:
  0.6 1.6 shard_map.86
  2.2 16.7 %all_to_all.50 = f32[8,56,1,128]{3,1,2,0:T(8,128)S(1)} all-to-all(f32[8,56,1,128]{3,1,2,0:T(8,128)} %bitcast.59), channel_id=1, replica_groups=mesh['op_0'=4,'op_1'=8,'op_2'=2,'sec'=8] {'sec'}, dimensions={0} | all-to-all | bytes 458752 | tf_op jit(solution)/shard_map/all_to_all | solution.py:325
  18.9 0.7 copy-done.32
  19.5 1.8 shard_map.88
  21.3 16.7 %all-to-all-start.1 = ((f32[64,50,1,128]{3,2,1,0:T(1,128)}), f32[64,50,1,128]{3,2,1,0:T(1,128)}, u32[]{:S(2)}, u32[]{:S(2)}) async-start(f32[64,50,1,128]{3,2,1,0:T(1,128)} %bitcast.6), calls=%async_computation.1 | async-start | bytes 3276800 | tf_op jit(solution)/shard_map/all_to_all | solution.py:325
  38.1 2.2 collective-permute-start
  40.3 4.0 %collective-permute-done = f32[56,128]{1,0:T(8,128)S(1)} collective-permute-done((f32[56,128]{1,0:T(8,128)S(1)}, f32[56,128]{1,0:T(8,128)S(1)}, u32[]{:S(2)}, u32[]{:S(2)}) %collective-permute-start) | collective-permute-done | bytes 28704 | tf_op jit(solution)/shard_map/ppermute | solution.py:407
  44.3 1.9 collective-permute-start.1
  46.3 6.1 %collective-permute-done.1 = f32[112,128]{1,0:T(8,128)S(1)} collective-permute-done((f32[112,128]{1,0:T(8,128)S(1)}, f32[112,128]{1,0:T(8,128)S(1)}, u32[]{:S(2)}, u32[]{:S(2)}) %collective-permute-start.1) | collective-permute-done | bytes 57376 | tf_op jit(solution)/shard_map/ppermute | solution.py:407
  52.4 1.9 collective-permute-start.2
  54.3 3.2 %collective-permute-start.3 = (f32[56,128]{1,0:T(8,128)S(1)}, f32[56,128]{1,0:T(8,128)S(1)}, u32[]{:S(2)}, u32[]{:S(2)}) collective-permute-start(f32[56,128]{1,0:T(8,128)S(1)} %copy-done.4), channel_id=1, source_target_pairs={{0,16},{16,32},{32,48},{48,64},{64,80},{80,96},{96,112},{112,0},{1... | collective-permute-start | bytes 86024 | tf_op jit(solution)/shard_map/ppermute | solution.py:390
  57.6 3.2 %collective-permute-start.7 = (f32[56,128]{1,0:T(8,128)S(1)}, f32[56,128]{1,0:T(8,128)S(1)}, u32[]{:S(2)}, u32[]{:S(2)}) collective-permute-start(f32[56,128]{1,0:T(8,128)S(1)} %copy-done.4), channel_id=1, source_target_pairs={{0,112},{16,0},{32,16},{48,32},{64,48},{80,64},{96,80},{112,96},{1... | collective-permute-start | bytes 86024 | tf_op jit(solution)/shard_map/ppermute | solution.py:392
  60.8 14.1 %collective-permute-done.3.refs_1_ = f32[56,128]{1,0:T(8,128)S(1)} collective-permute-done((f32[56,128]{1,0:T(8,128)S(1)}, f32[56,128]{1,0:T(8,128)S(1)}, u32[]{:S(2)}, u32[]{:S(2)}) %collective-permute-start.3) | collective-permute-done | bytes 28704 | tf_op jit(solution)/shard_map/ppermute | solution.py:390
  74.9 1.9 collective-permute-start.4
  76.9 0.6 copy-done.7
  77.5 4.6 %collective-permute-start.8 = (f32[56,128]{1,0:T(8,128)S(1)}, f32[56,128]{1,0:T(8,128)S(1)}, u32[]{:S(2)}, u32[]{:S(2)}) collective-permute-start(f32[56,128]{1,0:T(8,128)S(1)} %collective-permute-done.7.refs_5_), channel_id=1, source_target_pairs={{0,112},{16,0},{32,16},{48,32},{64,48},{80,64},{96,80},{112,96},{1... | collective-permute-start | bytes 86024 | tf_op jit(solution)/shard_map/ppermute | solution.py:392
  82.1 1.9 collective-permute-start.5
  84.0 0.0 copy-start
  84.0 1.4 copy-done
  85.4 1.4 copy-done.1
  86.9 0.9 shard_map.87.mats_ref
  87.8 4.6 %collective-permute-start.9 = (f32[56,128]{1,0:T(8,128)S(1)}, f32[56,128]{1,0:T(8,128)S(1)}, u32[]{:S(2)}, u32[]{:S(2)}) collective-permute-start(f32[56,128]{1,0:T(8,128)S(1)} %collective-permute-done.8.refs_6_), channel_id=1, source_target_pairs={{0,112},{16,0},{32,16},{48,32},{64,48},{80,64},{96,80},{112,96},{1... | collective-permute-start | bytes 86024 | tf_op jit(solution)/shard_map/ppermute | solution.py:392
  92.4 0.6 copy-done.16
  93.0 0.0 collective-permute-done.5.refs_3_
  93.0 1.9 collective-permute-start.6
  94.9 0.7 pad_maximum_fusion.d8_ref
  95.7 0.6 copy-done.22
  96.3 2.5 collective-permute-done.6.refs_4_
  98.8 0.6 copy-done.25
  99.4 5.0 %shard_map.89 = (bf16[640,640]{1,0:T(8,128)(2,1)S(1)}, bf16[640,640]{1,0:T(8,128)(2,1)S(1)}, f32[1600,128]{1,0:T(8,128)S(1)}) custom-call(f32[3200,128]{1,0:T(8,128)} %bitcast.7.x_ref, bf16[4,640,640]{2,1,0:T(8,128)(2,1)S(1)} %shard_map.87.mats_ref), custom_call_target="tpu_custom_call" | custom-call | tf_op jit(solution)/shard_map/pallas_call | solution.py:313
  104.5 6.2 %collective-permute-start.10 = (f32[1600,128]{1,0:T(8,128)S(1)}, f32[1600,128]{1,0:T(8,128)S(1)}, u32[]{:S(2)}, u32[]{:S(2)}) collective-permute-start(f32[1600,128]{1,0:T(8,128)S(1)} %get-tuple-element.51), channel_id=1, source_target_pairs={{0,8},{8,0},{1,9},{9,1},{2,10},{10,2},{3,11},{11,3},{4,12},{12,4},... | collective-permute-start | bytes 2457608 | tf_op jit(solution)/shard_map/ppermute | solution.py:383
  110.7 1.3 shard_map.90
  112.1 0.6 collective-permute-done.10
  112.6 0.1 add.6
  112.7 0.0 copy-start.33
  112.7 16.1 %all_to_all.51 = f32[4,400,1,128]{3,1,2,0:T(8,128)S(1)} all-to-all(f32[4,400,1,128]{3,1,2,0:T(8,128)S(1)} %bitcast.56), channel_id=1, replica_groups=mesh['op_0'=4,'op_1'=8,'op_2'=2,'sec'=8] {'op_0'}, dimensions={0} | all-to-all | bytes 1638400 | tf_op jit(solution)/shard_map/all_to_all | solution.py:325
  128.9 0.2 shard_map.91
  129.0 13.5 %all_to_all.52 = f32[8,56,1,128]{3,1,2,0:T(8,128)S(1)} all-to-all(f32[8,56,1,128]{3,1,2,0:T(8,128)S(1)} %bitcast.47), channel_id=1, replica_groups=mesh['op_0'=4,'op_1'=8,'op_2'=2,'sec'=8] {'op_1'}, dimensions={0} | all-to-all | bytes 458752 | tf_op jit(solution)/shard_map/all_to_all | solution.py:325
  142.6 0.6 shard_map.92
  143.2 11.5 %all_to_all.53 = f32[8,56,1,128]{3,1,2,0:T(8,128)S(1)} all-to-all(f32[8,56,1,128]{3,1,2,0:T(8,128)S(1)} %bitcast.51), channel_id=1, replica_groups=mesh['op_0'=4,'op_1'=8,'op_2'=2,'sec'=8] {'sec'}, dimensions={0} | all-to-all | bytes 458752 | tf_op jit(solution)/shard_map/all_to_all | solution.py:325
  154.7 11.2 %all_to_all.54 = f32[8,1,1,128]{3,2,1,0:T(1,128)S(1)} all-to-all(f32[8,1,1,128]{3,2,1,0:T(1,128)S(1)} %bitcast.55), channel_id=1, replica_groups=mesh['op_0'=4,'op_1'=8,'op_2'=2,'sec'=8] {'op_0','op_2'}, dimensions={0} | all-to-all | bytes 8192 | tf_op jit(solution)/shard_map/all_to_all | solution.py:325
  165.9 2.0 shard_map.94
  168.0 0.6 copy-done.30
  168.6 5.7 %all-to-all-start.6 = ((f32[64,50,1,128]{3,2,1,0:T(1,128)}), f32[64,50,1,128]{3,2,1,0:T(1,128)}, u32[]{:S(2)}, u32[]{:S(2)}) async-start(f32[64,50,1,128]{3,2,1,0:T(1,128)} %bitcast.58), calls=%async_computation.6 | async-start | bytes 3276800 | tf_op jit(solution)/shard_map/all_to_all | solution.py:325
  174.3 3.3 %collective-permute-start.11 = (f32[56,128]{1,0:T(8,128)S(1)}, f32[56,128]{1,0:T(8,128)S(1)}, u32[]{:S(2)}, u32[]{:S(2)}) collective-permute-start(f32[56,128]{1,0:T(8,128)S(1)} %copy-done.31), channel_id=1, source_target_pairs={{0,16},{16,32},{32,48},{48,64},{64,80},{80,96},{96,112},{112,0},{1... | collective-permute-start | bytes 86024 | tf_op jit(solution)/shard_map/ppermute | solution.py:390
  177.6 3.2 %collective-permute-start.15 = (f32[56,128]{1,0:T(8,128)S(1)}, f32[56,128]{1,0:T(8,128)S(1)}, u32[]{:S(2)}, u32[]{:S(2)}) collective-permute-start(f32[56,128]{1,0:T(8,128)S(1)} %copy-done.31), channel_id=1, source_target_pairs={{0,112},{16,0},{32,16},{48,32},{64,48},{80,64},{96,80},{112,96},{1... | collective-permute-start | bytes 86024 | tf_op jit(solution)/shard_map/ppermute | solution.py:392
  180.8 30.4 %collective-permute-done.11.refs_9_ = f32[56,128]{1,0:T(8,128)S(1)} collective-permute-done((f32[56,128]{1,0:T(8,128)S(1)}, f32[56,128]{1,0:T(8,128)S(1)}, u32[]{:S(2)}, u32[]{:S(2)}) %collective-permute-start.11) | collective-permute-done | bytes 28704 | tf_op jit(solution)/shard_map/ppermute | solution.py:390
  211.2 1.9 collective-permute-start.12
  213.2 4.6 %collective-permute-start.16 = (f32[56,128]{1,0:T(8,128)S(1)}, f32[56,128]{1,0:T(8,128)S(1)}, u32[]{:S(2)}, u32[]{:S(2)}) collective-permute-start(f32[56,128]{1,0:T(8,128)S(1)} %collective-permute-done.15.refs_13_), channel_id=1, source_target_pairs={{0,112},{16,0},{32,16},{48,32},{64,48},{80,64},{96,80},{112,96},{1... | collective-permute-start | bytes 86024 | tf_op jit(solution)/shard_map/ppermute | solution.py:392
  217.7 1.9 collective-permute-start.13
  219.7 4.6 %collective-permute-start.17 = (f32[56,128]{1,0:T(8,128)S(1)}, f32[56,128]{1,0:T(8,128)S(1)}, u32[]{:S(2)}, u32[]{:S(2)}) collective-permute-start(f32[56,128]{1,0:T(8,128)S(1)} %collective-permute-done.16.refs_14_), channel_id=1, source_target_pairs={{0,112},{16,0},{32,16},{48,32},{64,48},{80,64},{96,80},{112,96},{1... | collective-permute-start | bytes 86024 | tf_op jit(solution)/shard_map/ppermute | solution.py:392
  224.3 2.1 collective-permute-start.14
  226.4 3.7 %collective-permute-done.14.refs_12_ = f32[56,128]{1,0:T(8,128)S(1)} collective-permute-done((f32[56,128]{1,0:T(8,128)S(1)}, f32[56,128]{1,0:T(8,128)S(1)}, u32[]{:S(2)}, u32[]{:S(2)}) %collective-permute-start.14) | collective-permute-done | bytes 28704 | tf_op jit(solution)/shard_map/ppermute | solution.py:390
  230.1 5.0 %shard_map.95 = (bf16[640,640]{1,0:T(8,128)(2,1)S(1)}, bf16[640,640]{1,0:T(8,128)(2,1)S(1)}, f32[1600,128]{1,0:T(8,128)S(1)}) custom-call(f32[3200,128]{1,0:T(8,128)} %bitcast.21.x_ref, bf16[4,640,640]{2,1,0:T(8,128)(2,1)S(1)} %shard_map.87.mats_ref), custom_call_target="tpu_custom_call" | custom-call | tf_op jit(solution)/shard_map/pallas_call | solution.py:313
  235.2 6.2 %collective-permute-start.18 = (f32[1600,128]{1,0:T(8,128)S(1)}, f32[1600,128]{1,0:T(8,128)S(1)}, u32[]{:S(2)}, u32[]{:S(2)}) collective-permute-start(f32[1600,128]{1,0:T(8,128)S(1)} %get-tuple-element.67), channel_id=1, source_target_pairs={{0,8},{8,0},{1,9},{9,1},{2,10},{10,2},{3,11},{11,3},{4,12},{12,4},... | collective-permute-start | bytes 2457608 | tf_op jit(solution)/shard_map/ppermute | solution.py:383
  241.4 1.3 shard_map.96
  242.8 0.5 collective-permute-done.18
  243.3 0.1 add.7
  243.4 16.1 %all_to_all.55 = f32[4,400,1,128]{3,1,2,0:T(8,128)S(1)} all-to-all(f32[4,400,1,128]{3,1,2,0:T(8,128)S(1)} %bitcast.57), channel_id=1, replica_groups=mesh['op_0'=4,'op_1'=8,'op_2'=2,'sec'=8] {'op_0'}, dimensions={0} | all-to-all | bytes 1638400 | tf_op jit(solution)/shard_map/all_to_all | solution.py:325
  259.5 0.2 shard_map.97
  259.8 13.5 %all_to_all.56 = f32[8,56,1,128]{3,1,2,0:T(8,128)S(1)} all-to-all(f32[8,56,1,128]{3,1,2,0:T(8,128)S(1)} %bitcast.50), channel_id=1, replica_groups=mesh['op_0'=4,'op_1'=8,'op_2'=2,'sec'=8] {'op_1'}, dimensions={0} | all-to-all | bytes 458752 | tf_op jit(solution)/shard_map/all_to_all | solution.py:325
  273.3 0.6 shard_map.98
  273.9 15.9 %all_to_all.57 = f32[64,1,1,128]{3,2,1,0:T(1,128)S(1)} all-to-all(f32[64,1,1,128]{3,2,1,0:T(1,128)S(1)} %bitcast.53), channel_id=1, replica_groups=mesh['op_0'=4,'op_1'=8,'op_2'=2,'sec'=8] {'op_0','op_2','sec'}, dimensions={0} | all-to-all | bytes 65536 | tf_op jit(solution)/shard_map/all_to_all | solution.py:325
  289.8 1.1 shard_map.99
  (73 shorter events, 0.2 us)
Async XLA Ops:
  18.9 0.7 copy-start.32
  21.3 16.8 %copy-start.3 = (f32[56,128]{1,0:T(8,128)S(1)}, f32[56,128]{1,0:T(8,128)}, u32[]{:S(2)}) copy-start(f32[56,128]{1,0:T(8,128)} %get-tuple-element.46.d_ref) | copy-start | bytes 86020
  21.3 33.0 %copy-start.4 = (f32[56,128]{1,0:T(8,128)S(1)}, f32[56,128]{1,0:T(8,128)}, u32[]{:S(2)}) copy-start(f32[56,128]{1,0:T(8,128)} %get-tuple-element.52.refs_0_.v_ref) | copy-start | bytes 86020
  21.3 78.1 %all-to-all-start.1 = ((f32[64,50,1,128]{3,2,1,0:T(1,128)}), f32[64,50,1,128]{3,2,1,0:T(1,128)}, u32[]{:S(2)}, u32[]{:S(2)}) async-start(f32[64,50,1,128]{3,2,1,0:T(1,128)} %bitcast.6), calls=%async_computation.1 | async-start | bytes 3276800 | tf_op jit(solution)/shard_map/all_to_all | solution.py:325
  38.1 6.2 %collective-permute-start = (f32[56,128]{1,0:T(8,128)S(1)}, f32[56,128]{1,0:T(8,128)S(1)}, u32[]{:S(2)}, u32[]{:S(2)}) collective-permute-start(f32[56,128]{1,0:T(8,128)S(1)} %copy-done.3), channel_id=1, source_target_pairs={{0,1},{1,2},{2,3},{3,4},{4,5},{5,6},{6,7},{7,0},{8,9},{9,10},{10,1... | collective-permute-start | bytes 86024 | tf_op jit(solution)/shard_map/ppermute | solution.py:407
  44.3 8.0 %collective-permute-start.1 = (f32[112,128]{1,0:T(8,128)S(1)}, f32[112,128]{1,0:T(8,128)S(1)}, u32[]{:S(2)}, u32[]{:S(2)}) collective-permute-start(f32[112,128]{1,0:T(8,128)S(1)} %pad_maximum_fusion.2), channel_id=1, source_target_pairs={{0,2},{1,3},{2,4},{3,5},{4,6},{5,7},{6,0},{7,1},{8,10},{9,11},{10,... | collective-permute-start | bytes 172040 | tf_op jit(solution)/shard_map/ppermute | solution.py:407
  52.4 42.6 %collective-permute-start.2 = (f32[224,128]{1,0:T(8,128)S(1)}, f32[224,128]{1,0:T(8,128)S(1)}, u32[]{:S(2)}, u32[]{:S(2)}) collective-permute-start(f32[224,128]{1,0:T(8,128)S(1)} %pad_maximum_fusion.1), channel_id=1, source_target_pairs={{0,4},{1,5},{2,6},{3,7},{4,0},{5,1},{6,2},{7,3},{8,12},{9,13},{10,... | collective-permute-start | bytes 344072 | tf_op jit(solution)/shard_map/ppermute | solution.py:407
  54.3 20.6 %collective-permute-start.3 = (f32[56,128]{1,0:T(8,128)S(1)}, f32[56,128]{1,0:T(8,128)S(1)}, u32[]{:S(2)}, u32[]{:S(2)}) collective-permute-start(f32[56,128]{1,0:T(8,128)S(1)} %copy-done.4), channel_id=1, source_target_pairs={{0,16},{16,32},{32,48},{48,64},{64,80},{80,96},{96,112},{112,0},{1... | collective-permute-start | bytes 86024 | tf_op jit(solution)/shard_map/ppermute | solution.py:390
  57.6 19.9 %collective-permute-start.7 = (f32[56,128]{1,0:T(8,128)S(1)}, f32[56,128]{1,0:T(8,128)S(1)}, u32[]{:S(2)}, u32[]{:S(2)}) collective-permute-start(f32[56,128]{1,0:T(8,128)S(1)} %copy-done.4), channel_id=1, source_target_pairs={{0,112},{16,0},{32,16},{48,32},{64,48},{80,64},{96,80},{112,96},{1... | collective-permute-start | bytes 86024 | tf_op jit(solution)/shard_map/ppermute | solution.py:392
  74.9 7.1 %collective-permute-start.4 = (f32[56,128]{1,0:T(8,128)S(1)}, f32[56,128]{1,0:T(8,128)S(1)}, u32[]{:S(2)}, u32[]{:S(2)}) collective-permute-start(f32[56,128]{1,0:T(8,128)S(1)} %collective-permute-done.3.refs_1_), channel_id=1, source_target_pairs={{0,16},{16,32},{32,48},{48,64},{64,80},{80,96},{96,112},{112,0},{1... | collective-permute-start | bytes 86024 | tf_op jit(solution)/shard_map/ppermute | solution.py:390
  76.9 0.6 copy-start.7
  77.5 10.3 %copy-start.10 = (f32[56,128]{1,0:T(8,128)}, f32[56,128]{1,0:T(8,128)S(1)}, u32[]{:S(2)}) copy-start(f32[56,128]{1,0:T(8,128)S(1)} %collective-permute-done.7.refs_5_) | copy-start | bytes 86020
  77.5 10.3 %collective-permute-start.8 = (f32[56,128]{1,0:T(8,128)S(1)}, f32[56,128]{1,0:T(8,128)S(1)}, u32[]{:S(2)}, u32[]{:S(2)}) collective-permute-start(f32[56,128]{1,0:T(8,128)S(1)} %collective-permute-done.7.refs_5_), channel_id=1, source_target_pairs={{0,112},{16,0},{32,16},{48,32},{64,48},{80,64},{96,80},{112,96},{1... | collective-permute-start | bytes 86024 | tf_op jit(solution)/shard_map/ppermute | solution.py:392
  82.1 5.7 %copy-start.13 = (f32[56,128]{1,0:T(8,128)}, f32[56,128]{1,0:T(8,128)S(1)}, u32[]{:S(2)}) copy-start(f32[56,128]{1,0:T(8,128)S(1)} %collective-permute-done.4.refs_2_) | copy-start | bytes 86020
  82.1 10.9 %collective-permute-start.5 = (f32[56,128]{1,0:T(8,128)S(1)}, f32[56,128]{1,0:T(8,128)S(1)}, u32[]{:S(2)}, u32[]{:S(2)}) collective-permute-start(f32[56,128]{1,0:T(8,128)S(1)} %collective-permute-done.4.refs_2_), channel_id=1, source_target_pairs={{0,16},{16,32},{32,48},{48,64},{64,80},{80,96},{96,112},{112,0},{1... | collective-permute-start | bytes 86024 | tf_op jit(solution)/shard_map/ppermute | solution.py:390
  84.0 1.4 copy-start
  85.4 1.4 copy-start.1
  87.8 7.9 %collective-permute-start.9 = (f32[56,128]{1,0:T(8,128)S(1)}, f32[56,128]{1,0:T(8,128)S(1)}, u32[]{:S(2)}, u32[]{:S(2)}) collective-permute-start(f32[56,128]{1,0:T(8,128)S(1)} %collective-permute-done.8.refs_6_), channel_id=1, source_target_pairs={{0,112},{16,0},{32,16},{48,32},{64,48},{80,64},{96,80},{112,96},{1... | collective-permute-start | bytes 86024 | tf_op jit(solution)/shard_map/ppermute | solution.py:392
  92.4 0.6 copy-start.16
  93.0 2.7 copy-start.19
  93.0 5.8 %collective-permute-start.6 = (f32[56,128]{1,0:T(8,128)S(1)}, f32[56,128]{1,0:T(8,128)S(1)}, u32[]{:S(2)}, u32[]{:S(2)}) collective-permute-start(f32[56,128]{1,0:T(8,128)S(1)} %collective-permute-done.5.refs_3_), channel_id=1, source_target_pairs={{0,16},{16,32},{32,48},{48,64},{64,80},{80,96},{96,112},{112,0},{1... | collective-permute-start | bytes 86024 | tf_op jit(solution)/shard_map/ppermute | solution.py:390
  95.7 0.6 copy-start.22
  98.8 0.6 copy-start.25
  104.5 8.1 %collective-permute-start.10 = (f32[1600,128]{1,0:T(8,128)S(1)}, f32[1600,128]{1,0:T(8,128)S(1)}, u32[]{:S(2)}, u32[]{:S(2)}) collective-permute-start(f32[1600,128]{1,0:T(8,128)S(1)} %get-tuple-element.51), channel_id=1, source_target_pairs={{0,8},{8,0},{1,9},{9,1},{2,10},{10,2},{3,11},{11,3},{4,12},{12,4},... | collective-permute-start | bytes 2457608 | tf_op jit(solution)/shard_map/ppermute | solution.py:383
  112.0 16.9 %copy-start.5 = (f32[56,128]{1,0:T(8,128)S(1)}, f32[56,128]{1,0:T(8,128)}, u32[]{:S(2)}) copy-start(f32[56,128]{1,0:T(8,128)} %get-tuple-element.52.refs_0_.v_ref) | copy-start | bytes 86020
  112.0 16.8 %copy-start.8 = (f32[56,128]{1,0:T(8,128)S(1)}, f32[56,128]{1,0:T(8,128)}, u32[]{:S(2)}) copy-start(f32[56,128]{1,0:T(8,128)} %copy-done.7) | copy-start | bytes 86020
  112.0 16.8 %copy-start.11 = (f32[56,128]{1,0:T(8,128)S(1)}, f32[56,128]{1,0:T(8,128)}, u32[]{:S(2)}) copy-start(f32[56,128]{1,0:T(8,128)} %copy-done.10) | copy-start | bytes 86020
  112.0 16.8 %copy-start.14 = (f32[56,128]{1,0:T(8,128)S(1)}, f32[56,128]{1,0:T(8,128)}, u32[]{:S(2)}) copy-start(f32[56,128]{1,0:T(8,128)} %copy-done.13) | copy-start | bytes 86020
  112.0 16.8 %copy-start.17 = (f32[56,128]{1,0:T(8,128)S(1)}, f32[56,128]{1,0:T(8,128)}, u32[]{:S(2)}) copy-start(f32[56,128]{1,0:T(8,128)} %copy-done.16) | copy-start | bytes 86020
  112.0 16.8 %copy-start.20 = (f32[56,128]{1,0:T(8,128)S(1)}, f32[56,128]{1,0:T(8,128)}, u32[]{:S(2)}) copy-start(f32[56,128]{1,0:T(8,128)} %copy-done.19) | copy-start | bytes 86020
  112.0 16.8 %copy-start.23 = (f32[56,128]{1,0:T(8,128)S(1)}, f32[56,128]{1,0:T(8,128)}, u32[]{:S(2)}) copy-start(f32[56,128]{1,0:T(8,128)} %copy-done.22) | copy-start | bytes 86020
  112.0 16.8 %copy-start.26 = (f32[56,128]{1,0:T(8,128)S(1)}, f32[56,128]{1,0:T(8,128)}, u32[]{:S(2)}) copy-start(f32[56,128]{1,0:T(8,128)} %copy-done.25) | copy-start | bytes 86020
  112.7 29.9 %copy-start.33 = (s32[65]{0:T(128)S(1)}, s32[65]{0:T(128)}, u32[]{:S(2)}) copy-start(s32[65]{0:T(128)} %get-tuple-element.41.slots_ref) | copy-start | bytes 784
  128.8 37.1 %copy-start.2 = (f32[448,128]{1,0:T(8,128)S(1)}, f32[448,128]{1,0:T(8,128)}, u32[]{:S(2)}) copy-start(f32[448,128]{1,0:T(8,128)} %pad_maximum_fusion.d8_ref) | copy-start | bytes 688132
  143.2 11.6 %copy-start.28 = (f32[50,128]{1,0:T(8,128)}, f32[50,128]{1,0:T(8,128)S(1)}, u32[]{:S(2)}) copy-start(f32[50,128]{1,0:T(8,128)S(1)} %get-tuple-element.69.w_ref) | copy-start | bytes 76804
  167.9 0.6 copy-start.30
  168.6 5.7 %copy-start.31 = (f32[56,128]{1,0:T(8,128)S(1)}, f32[56,128]{1,0:T(8,128)}, u32[]{:S(2)}) copy-start(f32[56,128]{1,0:T(8,128)} %copy-done.30) | copy-start | bytes 86020
  168.6 61.5 %all-to-all-start.6 = ((f32[64,50,1,128]{3,2,1,0:T(1,128)}), f32[64,50,1,128]{3,2,1,0:T(1,128)}, u32[]{:S(2)}, u32[]{:S(2)}) async-start(f32[64,50,1,128]{3,2,1,0:T(1,128)} %bitcast.58), calls=%async_computation.6 | async-start | bytes 3276800 | tf_op jit(solution)/shard_map/all_to_all | solution.py:325
  174.3 36.9 %collective-permute-start.11 = (f32[56,128]{1,0:T(8,128)S(1)}, f32[56,128]{1,0:T(8,128)S(1)}, u32[]{:S(2)}, u32[]{:S(2)}) collective-permute-start(f32[56,128]{1,0:T(8,128)S(1)} %copy-done.31), channel_id=1, source_target_pairs={{0,16},{16,32},{32,48},{48,64},{64,80},{80,96},{96,112},{112,0},{1... | collective-permute-start | bytes 86024 | tf_op jit(solution)/shard_map/ppermute | solution.py:390
  177.6 35.6 %collective-permute-start.15 = (f32[56,128]{1,0:T(8,128)S(1)}, f32[56,128]{1,0:T(8,128)S(1)}, u32[]{:S(2)}, u32[]{:S(2)}) collective-permute-start(f32[56,128]{1,0:T(8,128)S(1)} %copy-done.31), channel_id=1, source_target_pairs={{0,112},{16,0},{32,16},{48,32},{64,48},{80,64},{96,80},{112,96},{1... | collective-permute-start | bytes 86024 | tf_op jit(solution)/shard_map/ppermute | solution.py:392
  211.2 6.5 %collective-permute-start.12 = (f32[56,128]{1,0:T(8,128)S(1)}, f32[56,128]{1,0:T(8,128)S(1)}, u32[]{:S(2)}, u32[]{:S(2)}) collective-permute-start(f32[56,128]{1,0:T(8,128)S(1)} %collective-permute-done.11.refs_9_), channel_id=1, source_target_pairs={{0,16},{16,32},{32,48},{48,64},{64,80},{80,96},{96,112},{112,0},{1... | collective-permute-start | bytes 86024 | tf_op jit(solution)/shard_map/ppermute | solution.py:390
  213.2 6.5 %collective-permute-start.16 = (f32[56,128]{1,0:T(8,128)S(1)}, f32[56,128]{1,0:T(8,128)S(1)}, u32[]{:S(2)}, u32[]{:S(2)}) collective-permute-start(f32[56,128]{1,0:T(8,128)S(1)} %collective-permute-done.15.refs_13_), channel_id=1, source_target_pairs={{0,112},{16,0},{32,16},{48,32},{64,48},{80,64},{96,80},{112,96},{1... | collective-permute-start | bytes 86024 | tf_op jit(solution)/shard_map/ppermute | solution.py:392
  217.7 6.5 %collective-permute-start.13 = (f32[56,128]{1,0:T(8,128)S(1)}, f32[56,128]{1,0:T(8,128)S(1)}, u32[]{:S(2)}, u32[]{:S(2)}) collective-permute-start(f32[56,128]{1,0:T(8,128)S(1)} %collective-permute-done.12.refs_10_), channel_id=1, source_target_pairs={{0,16},{16,32},{32,48},{48,64},{64,80},{80,96},{96,112},{112,0},{1... | collective-permute-start | bytes 86024 | tf_op jit(solution)/shard_map/ppermute | solution.py:390
  219.7 6.7 %collective-permute-start.17 = (f32[56,128]{1,0:T(8,128)S(1)}, f32[56,128]{1,0:T(8,128)S(1)}, u32[]{:S(2)}, u32[]{:S(2)}) collective-permute-start(f32[56,128]{1,0:T(8,128)S(1)} %collective-permute-done.16.refs_14_), channel_id=1, source_target_pairs={{0,112},{16,0},{32,16},{48,32},{64,48},{80,64},{96,80},{112,96},{1... | collective-permute-start | bytes 86024 | tf_op jit(solution)/shard_map/ppermute | solution.py:392
  224.3 5.8 %collective-permute-start.14 = (f32[56,128]{1,0:T(8,128)S(1)}, f32[56,128]{1,0:T(8,128)S(1)}, u32[]{:S(2)}, u32[]{:S(2)}) collective-permute-start(f32[56,128]{1,0:T(8,128)S(1)} %collective-permute-done.13.refs_11_), channel_id=1, source_target_pairs={{0,16},{16,32},{32,48},{48,64},{64,80},{80,96},{96,112},{112,0},{1... | collective-permute-start | bytes 86024 | tf_op jit(solution)/shard_map/ppermute | solution.py:390
  235.2 8.1 %collective-permute-start.18 = (f32[1600,128]{1,0:T(8,128)S(1)}, f32[1600,128]{1,0:T(8,128)S(1)}, u32[]{:S(2)}, u32[]{:S(2)}) collective-permute-start(f32[1600,128]{1,0:T(8,128)S(1)} %get-tuple-element.67), channel_id=1, source_target_pairs={{0,8},{8,0},{1,9},{9,1},{2,10},{10,2},{3,11},{11,3},{4,12},{12,4},... | collective-permute-start | bytes 2457608 | tf_op jit(solution)/shard_map/ppermute | solution.py:383
  242.7 16.8 %copy-start.6 = (f32[56,128]{1,0:T(8,128)S(1)}, f32[56,128]{1,0:T(8,128)}, u32[]{:S(2)}) copy-start(f32[56,128]{1,0:T(8,128)} %get-tuple-element.52.refs_0_.v_ref) | copy-start | bytes 86020
  242.7 16.8 %copy-start.9 = (f32[56,128]{1,0:T(8,128)S(1)}, f32[56,128]{1,0:T(8,128)}, u32[]{:S(2)}) copy-start(f32[56,128]{1,0:T(8,128)} %copy-done.7) | copy-start | bytes 86020
  242.7 16.8 %copy-start.12 = (f32[56,128]{1,0:T(8,128)S(1)}, f32[56,128]{1,0:T(8,128)}, u32[]{:S(2)}) copy-start(f32[56,128]{1,0:T(8,128)} %copy-done.10) | copy-start | bytes 86020
  242.7 16.8 %copy-start.15 = (f32[56,128]{1,0:T(8,128)S(1)}, f32[56,128]{1,0:T(8,128)}, u32[]{:S(2)}) copy-start(f32[56,128]{1,0:T(8,128)} %copy-done.13) | copy-start | bytes 86020
  242.7 16.8 %copy-start.18 = (f32[56,128]{1,0:T(8,128)S(1)}, f32[56,128]{1,0:T(8,128)}, u32[]{:S(2)}) copy-start(f32[56,128]{1,0:T(8,128)} %copy-done.16) | copy-start | bytes 86020
  242.7 16.8 %copy-start.21 = (f32[56,128]{1,0:T(8,128)S(1)}, f32[56,128]{1,0:T(8,128)}, u32[]{:S(2)}) copy-start(f32[56,128]{1,0:T(8,128)} %copy-done.19) | copy-start | bytes 86020
  242.7 16.8 %copy-start.24 = (f32[56,128]{1,0:T(8,128)S(1)}, f32[56,128]{1,0:T(8,128)}, u32[]{:S(2)}) copy-start(f32[56,128]{1,0:T(8,128)} %copy-done.22) | copy-start | bytes 86020
  242.7 16.8 %copy-start.27 = (f32[56,128]{1,0:T(8,128)S(1)}, f32[56,128]{1,0:T(8,128)}, u32[]{:S(2)}) copy-start(f32[56,128]{1,0:T(8,128)} %copy-done.25) | copy-start | bytes 86020
  242.7 16.8 %copy-start.29 = (f32[50,128]{1,0:T(8,128)S(1)}, f32[50,128]{1,0:T(8,128)}, u32[]{:S(2)}) copy-start(f32[50,128]{1,0:T(8,128)} %copy-done.28) | copy-start | bytes 76804

commit v4 on v2

--- a/solution.py
+++ b/solution.py
@@ -61,8 +61,6 @@
     rows, width = psi_ref.shape[0], psi_ref.shape[2]
     lines = rows * per_row
     if pad > lines:
-        for y in range(nsec):
-            v_out_ref[y * pad + lines : (y + 1) * pad, :] = jnp.zeros((pad - lines, LANES), jnp.float32)
         d_out_ref[lines:pad, :] = jnp.ones((pad - lines, LANES), jnp.float32)
     row = lax.broadcasted_iota(jnp.int32, (rows, width), 0) + op_position() * rows
     col = lax.broadcasted_iota(jnp.int32, (rows, width), 1)
@@ -81,28 +79,29 @@
         v_ref[at, :] = v[:, part]
         d_out_ref[at, :] = d[:, part]
         for y in range(nsec):
-            v_out_ref[pl.ds(y * pad + k, rows, stride=per_row), :] = v[:, part]
+            v_out_ref[pl.ds(y * lines + k, rows, stride=per_row), :] = v[:, part]
 
 
 PIECES = 4
 
 
-def spread(table_ref, slots_ref, out_ref, lines, pitch, buf_ref, sems):
+def pick(table_ref, slots_ref, t, lines, pitch):
+    return table_ref[pl.ds(pl.multiple_of(slots_ref[t] * pitch, 8), lines), :]
+
+
+def select_kernel(lines, pad, nsec, slots_ref, v8_ref, out_ref, table_ref, buf_ref, sems):
+    for y in range(nsec):
+        table_ref[y * pad : y * pad + lines, :] = v8_ref[y * lines : (y + 1) * lines, :]
     terms = out_ref.shape[0] // lines
     copies = []
     for c in range(PIECES):
         for t in range(c * terms // PIECES, (c + 1) * terms // PIECES):
-            start = pl.multiple_of(slots_ref[t] * pitch, 8)
-            buf_ref[t * lines : (t + 1) * lines, :] = table_ref[pl.ds(start, lines), :]
+            buf_ref[t * lines : (t + 1) * lines, :] = pick(table_ref, slots_ref, t, lines, pad)
         at = pl.ds(c * (terms * lines // PIECES), terms * lines // PIECES)
         copies.append(pltpu.make_async_copy(buf_ref.at[at], out_ref.at[at], sems.at[c]))
         copies[-1].start()
     for c in copies:
         c.wait()
-
-
-def select_kernel(lines, pad, slots_ref, v8_ref, out_ref, buf_ref, sems):
-    spread(v8_ref, slots_ref, out_ref, lines, pad, buf_ref, sems)
 
 
 def halves(x):
@@ -148,16 +147,10 @@
             out_ref[pl.ds(m * step * per_row + k, step, stride=per_row), :] = y[:, k * LANES : (k + 1) * LANES]
 
 
-def inner_kernel(per_row, x_in, mats_ref, ih_ref, il_ref, out_ref, x_ref, sems):
+def inner_kernel(per_row, x_ref, mats_ref, ih_ref, il_ref, out_ref):
     width = mats_ref.shape[1]
-    step = width // PIECES
-    copies = []
-    for m in range(PIECES):
-        at = pl.ds(m * step * per_row, step * per_row)
-        copies.append(pltpu.make_async_copy(x_in.at[at], x_ref.at[at], sems.at[m]))
-        copies[-1].start()
-    for m in range(PIECES):
-        copies[m].wait()
+    step = 160
+    for m in range(width // step):
         x = jnp.concatenate(
             [x_ref[pl.ds(m * step * per_row + k, step, stride=per_row), :] for k in range(per_row)], axis=1
         )
@@ -180,38 +173,33 @@
     return jnp.where(keep, w, 0.0)
 
 
-def share_kernel(lines, pad, per_row, nsec, slots_ref, part_ref, w_ref, out_ref):
+def share_kernel(lines, per_row, nsec, slots_ref, part_ref, w_ref, out_ref):
     w = masked_sum(part_ref, slots_ref, lines, per_row)
     w_ref[...] = w
     for y in range(nsec):
-        out_ref[y * pad : y * pad + lines, :] = w
-        if pad > lines:
-            out_ref[y * pad + lines : (y + 1) * pad, :] = jnp.zeros((pad - lines, LANES), jnp.float32)
-
-
-def first_sums_kernel(pad, nsec, v8_ref, w8_ref, out_ref):
-    vv = jnp.zeros((pad, LANES), jnp.float32)
-    vw = jnp.zeros((pad, LANES), jnp.float32)
-    for y in range(nsec):
-        v = v8_ref[y * pad : (y + 1) * pad, :]
-        vv = vv + v * v
-        vw = vw + v * w8_ref[y * pad : (y + 1) * pad, :]
-    out_ref[...] = jnp.broadcast_to(lane_row([total(vv), total(vw)]), out_ref.shape)
-
-
-def update_kernel(lines, pad, nsec, count, slots_ref, sums_ref, v8_ref, d8_ref, w8_ref, out_ref, t_ref, scal_ref, t8_ref, buf_ref, sems):
+        out_ref[y * lines : (y + 1) * lines, :] = w
+
+
+def first_sums_kernel(v8_ref, w8_ref, out_ref):
+    v = v8_ref[...]
+    out_ref[...] = jnp.broadcast_to(lane_row([total(v * v), total(v * w8_ref[...])]), out_ref.shape)
+
+
+def update_kernel(lines, pad, nsec, count, slots_ref, sums_ref, v8_ref, d8_ref, w8_ref, out_ref, t_ref, scal_ref, t8_ref):
     sums = jnp.sum(sums_ref[...], axis=0, keepdims=True) / count
     norm, product = sums[:, 0:1], sums[:, 1:2]
     scale = 1.0 / jnp.sqrt(norm + EPS)
     rayleigh = product / (norm + EPS)
     me = lax.axis_index("sec")
-    for k in range(nsec):
-        slot = lax.rem(me + nsec - k, nsec)
-        at = pl.ds(pl.multiple_of(slot * pad, 8), pad)
-        t8_ref[at, :] = (scale * w8_ref[at, :] - rayleigh * (scale * v8_ref[at, :])) / d8_ref[k * pad : (k + 1) * pad, :]
+    for y in range(nsec):
+        k = lax.rem(me + nsec - y, nsec)
+        d = d8_ref[pl.ds(pl.multiple_of(k * pad, 8), lines), :]
+        at = slice(y * lines, (y + 1) * lines)
+        t8_ref[y * pad : y * pad + lines, :] = (scale * w8_ref[at, :] - rayleigh * (scale * v8_ref[at, :])) / d
     t_ref[...] = t8_ref[pl.ds(pl.multiple_of(me * pad, 8), lines), :]
     scal_ref[...] = jnp.broadcast_to(lane_row([norm, product]), scal_ref.shape)
-    spread(t8_ref, slots_ref, out_ref, lines, pad, buf_ref, sems)
+    for t in range(out_ref.shape[0] // lines):
+        out_ref[t * lines : (t + 1) * lines, :] = pick(t8_ref, slots_ref, t, lines, pad)
 
 
 def last_sums_kernel(lines, per_row, pad, slots_ref, part_ref, scal_ref, v_ref, w_ref, t_ref, d_ref, out_ref, keep_ref):
@@ -223,7 +211,12 @@
     for i, x in enumerate((v0, w0, t, h, d_ref[0:lines, :])):
         keep_ref[i * pad : i * pad + lines, :] = x
     keep_ref[5 * pad : 5 * pad + 8, :] = scal_ref[...]
-    out_ref[...] = lane_row([total(v0 * t), total(t * t), total(t * w0), total(t * h), total(v0 * h)])
+    sums = [total(v0 * t), total(t * t), total(t * w0), total(t * h), total(v0 * h)]
+    out_ref[...] = jnp.broadcast_to(lane_row(sums), out_ref.shape)
+
+
+def relay_kernel(in_ref, out_ref):
+    out_ref[...] = jnp.broadcast_to(jnp.sum(in_ref[...], axis=0, keepdims=True), out_ref.shape)
 
 
 def final_kernel(count, per_row, lines, pad, sums_ref, keep_ref, new_ref, corr_ref, new_lines, corr_lines):
@@ -311,7 +304,7 @@
         part(prep_kernel, per_row, nsec, pad),
         (
             f32(lines, LANES),
-            f32(nsec * pad, LANES),
+            f32(nsec * lines, LANES),
             f32(pad, LANES),
             jax.ShapeDtypeStruct((nop + 1,), jnp.int32),
         ),
@@ -340,22 +333,21 @@
         scratch=[pltpu.VMEM((width, width), jnp.float32)],
     )
 
+    table = pltpu.VMEM((nsec * pad, LANES), jnp.float32)
     whole = [pltpu.VMEM((nop * lines, LANES), jnp.float32), pltpu.SemaphoreType.DMA((PIECES,))]
 
     def products(x):
-        ih, il, other = call(
-            part(inner_kernel, per_row), (square, square, half), (), (mats,), anywhere=(x,), scratch=whole
-        )
+        ih, il, other = call(part(inner_kernel, per_row), (square, square, half), (), (x, mats))
         came = lax.ppermute(other, "op_2", swap)
         own = call(part(own_kernel, per_row), half, (), (mats, ih, il))
         return exchange(own + came, CHIP, nchip)
 
     chosen = call(
-        part(select_kernel, lines, pad),
+        part(select_kernel, lines, pad, nsec),
         f32(nop * lines, LANES),
         (slots,),
         (v8,),
-        scratch=whole,
+        scratch=[table, *whole],
         out_anywhere=1,
     )
     chosen, d8 = lax.optimization_barrier((chosen, d_out))
@@ -368,37 +360,37 @@
     chosen, d8 = lax.optimization_barrier((chosen, d8))
     parts = products(chosen)
     w, w_out = call(
-        part(share_kernel, lines, pad, per_row, nsec),
-        (f32(lines, LANES), f32(nsec * pad, LANES)),
+        part(share_kernel, lines, per_row, nsec),
+        (f32(lines, LANES), f32(nsec * lines, LANES)),
         (slots,),
         (parts,),
     )
     w8 = exchange(w_out, "sec", nsec)
-    sums = call(part(first_sums_kernel, pad, nsec), f32(nop, LANES), (), (v8, w8))
+    sums = call(first_sums_kernel, f32(nop, LANES), (), (v8, w8))
     sums = exchange(sums, OP, nop)
     chosen, t, scal = call(
         part(update_kernel, lines, pad, nsec, count),
         (f32(nop * lines, LANES), f32(lines, LANES), f32(8, LANES)),
         (slots,),
         (sums, v8, d8, w8),
-        scratch=[pltpu.VMEM((nsec * pad, LANES), jnp.float32), *whole],
-        out_anywhere=1,
+        scratch=[table],
     )
     parts = products(exchange(chosen, OP, nop))
+    near = ("op_0", "op_2", "sec")
     sums, keep = call(
         part(last_sums_kernel, lines, per_row, pad),
-        (f32(1, LANES), f32(5 * pad + 8, LANES)),
+        (f32(lax.axis_size(near), LANES), f32(5 * pad + 8, LANES)),
         (slots,),
         (parts, scal, v, w, t, d_out),
     )
-    chips = nchip * nsec
-    sums = jnp.broadcast_to(lax.psum(sums, "op_2"), (chips, LANES))
-    sums = exchange(sums, (*CHIP, "sec"), chips)
+    sums = exchange(sums, near, lax.axis_size(near))
+    far = lax.axis_size("op_1")
+    sums = call(relay_kernel, f32(far, LANES), (), (sums,))
     return call(
         part(final_kernel, count, per_row, lines, pad),
         (f32(*psi.shape), f32(*psi.shape)),
         (),
-        (sums, keep),
+        (exchange(sums, "op_1", far), keep),
         scratch=[pltpu.VMEM((lines, LANES), jnp.float32)] * 2,
     )
 

time: 259 us -> 255 us (0.985)
    psum x1 -> x0, blocking collectives: 6.75 us -> none  [per_device(): sums = jnp.broadcast_to(lax.psum(sums, 'op_2'), (chips, LANES))]
    all_to_all x7 -> x8, blocking collectives: 165 us -> 171 us  [exchange(): lax.all_to_all(x.reshape(parts, lines, 1, LANES), axis, 0, 0, tiled=True)]
    pallas_call x12 -> x13, Pallas kernels: 21.3 us -> 18.9 us  [call(): pl.pallas_call(kernel, out_shape=out, in_specs=[SMEM] * len(smem) + [ANY]...]
where the time goes in v4:
time: 255 us; the launch traced here: 254 us
  blocking collectives  171 us (67%)
  waiting for transfers between devices  32.2 us (13%)
  starting transfers between devices  26.5 us (10%)
  Pallas kernels  18.9 us (7%)
  local copies, waits for them, and re-layouts  3.53 us (1%)
    all_to_all x8, blocking collectives, exchange(): lax.all_to_all(x.reshape(parts, lines, 1, LANES), axis, 0, 0, tiled=True)  171 us
    pallas_call x13, Pallas kernels, call(): pl.pallas_call(kernel, out_shape=out, in_specs=[SMEM] * len(smem) + [ANY]...  18.9 us
    all_to_all x1, waiting for transfers between devices, exchange(): lax.all_to_all(x.reshape(parts, lines, 1, LANES), axis, 0, 0, tiled=True)  17.3 us
    all_to_all x1, starting transfers between devices, exchange(): lax.all_to_all(x.reshape(parts, lines, 1, LANES), axis, 0, 0, tiled=True)  16.3 us
    ppermute x3, waiting for transfers between devices, per_device(): lax.ppermute(d8, 'sec', [(i, (i + reach) % nsec) for i in range(nsec)])  13.1 us
    ppermute x3, starting transfers between devices, per_device(): lax.ppermute(d8, 'sec', [(i, (i + reach) % nsec) for i in range(nsec)])  6.22 us
  transfers between devices with their start and end apart: 6, of which 6 were waited for; matrix products, arithmetic and copies ran while one was open for 0% of the time, Pallas kernels for 1%

profile of v4, /device:TPU:1, one launch (start us, length us, event | category | flops | bytes accessed | tf_op | source)
XLA Modules:
  0.0 253.7 jit_solution(3165530916771838572)
XLA Ops:
  0.6 1.6 shard_map.86
  2.2 16.5 %all_to_all.45 = f32[8,50,1,128]{3,2,1,0:T(1,128)S(1)} all-to-all(f32[8,50,1,128]{3,2,1,0:T(1,128)} %bitcast.47), channel_id=1, replica_groups=mesh['op_0'=4,'op_1'=8,'op_2'=2,'sec'=8] {'sec'}, dimensions={0} | all-to-all | bytes 409600 | tf_op jit(solution)/shard_map/all_to_all | solution.py:283
  18.7 0.0 copy-start.5
  18.7 0.7 copy-done.5
  19.3 1.8 shard_map.88
  21.1 0.0 copy-start.3
  21.1 16.3 %all-to-all-start.1 = ((f32[64,50,1,128]{3,2,1,0:T(1,128)}), f32[64,50,1,128]{3,2,1,0:T(1,128)}, u32[]{:S(2)}, u32[]{:S(2)}) async-start(f32[64,50,1,128]{3,2,1,0:T(1,128)} %bitcast.5), calls=%async_computation.1 | async-start | bytes 3276800 | tf_op jit(solution)/shard_map/all_to_all | solution.py:283
  37.4 0.0 copy-done.3
  37.4 2.2 collective-permute-start
  39.6 4.0 %collective-permute-done = f32[56,128]{1,0:T(8,128)S(1)} collective-permute-done((f32[56,128]{1,0:T(8,128)S(1)}, f32[56,128]{1,0:T(8,128)S(1)}, u32[]{:S(2)}, u32[]{:S(2)}) %collective-permute-start) | collective-permute-done | bytes 28704 | tf_op jit(solution)/shard_map/ppermute | solution.py:357
  43.7 1.9 collective-permute-start.1
  45.6 5.4 %collective-permute-done.1 = f32[112,128]{1,0:T(8,128)S(1)} collective-permute-done((f32[112,128]{1,0:T(8,128)S(1)}, f32[112,128]{1,0:T(8,128)S(1)}, u32[]{:S(2)}, u32[]{:S(2)}) %collective-permute-start.1) | collective-permute-done | bytes 57376 | tf_op jit(solution)/shard_map/ppermute | solution.py:357
  51.0 2.1 collective-permute-start.2
  53.1 0.0 copy-start
  53.1 1.4 copy-done
  54.5 0.0 copy-start.1
  54.6 1.4 copy-done.1
  56.0 0.9 shard_map.87.mats_ref
  56.9 3.7 %collective-permute-done.2 = f32[224,128]{1,0:T(8,128)S(1)} collective-permute-done((f32[224,128]{1,0:T(8,128)S(1)}, f32[224,128]{1,0:T(8,128)S(1)}, u32[]{:S(2)}, u32[]{:S(2)}) %collective-permute-start.2) | collective-permute-done | bytes 114720 | tf_op jit(solution)/shard_map/ppermute | solution.py:357
  60.6 0.7 pad_maximum_fusion.d8_ref
  61.3 17.3 %all-to-all-done.1 = f32[64,50,1,128]{3,2,1,0:T(1,128)} async-done(((f32[64,50,1,128]{3,2,1,0:T(1,128)}), f32[64,50,1,128]{3,2,1,0:T(1,128)}, u32[]{:S(2)}, u32[]{:S(2)}) %all-to-all-start.1) | async-done | bytes 1638432 | tf_op jit(solution)/shard_map/all_to_all | solution.py:283
  78.5 5.0 %shard_map.89 = (bf16[640,640]{1,0:T(8,128)(2,1)S(1)}, bf16[640,640]{1,0:T(8,128)(2,1)S(1)}, f32[1600,128]{1,0:T(8,128)S(1)}) custom-call(f32[3200,128]{1,0:T(8,128)} %bitcast.6.x_ref, bf16[4,640,640]{2,1,0:T(8,128)(2,1)S(1)} %shard_map.87.mats_ref), custom_call_target="tpu_custom_call" | custom-call | tf_op jit(solution)/shard_map/pallas_call | solution.py:271
  83.5 1.9 collective-permute-start.3
  85.5 1.3 shard_map.90
  86.8 0.0 copy-start.6
  86.8 1.0 collective-permute-done.3
  87.7 0.1 add.6
  87.8 0.0 copy-start.2
  87.8 24.7 %all_to_all.46 = f32[32,50,1,128]{3,2,1,0:T(1,128)S(1)} all-to-all(f32[32,50,1,128]{3,2,1,0:T(1,128)S(1)} %bitcast.45), channel_id=1, replica_groups=mesh['op_0'=4,'op_1'=8,'op_2'=2,'sec'=8] {'op_0','op_1'}, dimensions={0} | all-to-all | bytes 1638400 | tf_op jit(solution)/shard_map/all_to_all | solution.py:283
  112.5 0.0 copy-done.6
  112.5 0.6 shard_map.91
  113.1 11.1 %all_to_all.47 = f32[8,50,1,128]{3,2,1,0:T(1,128)S(1)} all-to-all(f32[8,50,1,128]{3,2,1,0:T(1,128)S(1)} %bitcast.38), channel_id=1, replica_groups=mesh['op_0'=4,'op_1'=8,'op_2'=2,'sec'=8] {'sec'}, dimensions={0} | all-to-all | bytes 409600 | tf_op jit(solution)/shard_map/all_to_all | solution.py:283
  124.2 0.1 shard_map.92
  124.4 21.3 %all_to_all.48 = f32[64,1,1,128]{3,2,1,0:T(1,128)S(1)} all-to-all(f32[64,1,1,128]{3,2,1,0:T(1,128)S(1)} %bitcast.40), channel_id=1, replica_groups=mesh['op_0'=4,'op_1'=8,'op_2'=2,'sec'=8] {'op_0','op_1','op_2'}, dimensions={0} | all-to-all | bytes 65536 | tf_op jit(solution)/shard_map/all_to_all | solution.py:283
  145.7 0.0 copy-done.2
  145.7 0.9 shard_map.93
  146.6 45.2 %all_to_all.49 = f32[64,50,1,128]{3,2,1,0:T(1,128)S(1)} all-to-all(f32[64,50,1,128]{3,2,1,0:T(1,128)S(1)} %bitcast.37), channel_id=1, replica_groups=mesh['op_0'=4,'op_1'=8,'op_2'=2,'sec'=8] {'op_0','op_1','op_2'}, dimensions={0} | all-to-all | bytes 3276800 | tf_op jit(solution)/shard_map/all_to_all | solution.py:283
  191.8 3.6 %shard_map.94 = (bf16[640,640]{1,0:T(8,128)(2,1)S(1)}, bf16[640,640]{1,0:T(8,128)(2,1)S(1)}, f32[1600,128]{1,0:T(8,128)S(1)}) custom-call(f32[3200,128]{1,0:T(8,128)S(1)} %bitcast.27, bf16[4,640,640]{2,1,0:T(8,128)(2,1)S(1)} %shard_map.87.mats_ref), custom_call_target="tpu_custom_call" | custom-call | tf_op jit(solution)/shard_map/pallas_call | solution.py:271
  195.3 2.0 collective-permute-start.4
  197.4 1.3 shard_map.95
  198.7 0.0 copy-start.4
  198.7 0.9 collective-permute-done.4
  199.6 0.1 add.7
  199.7 24.6 %all_to_all.50 = f32[32,50,1,128]{3,2,1,0:T(1,128)S(1)} all-to-all(f32[32,50,1,128]{3,2,1,0:T(1,128)S(1)} %bitcast.46), channel_id=1, replica_groups=mesh['op_0'=4,'op_1'=8,'op_2'=2,'sec'=8] {'op_0','op_1'}, dimensions={0} | all-to-all | bytes 1638400 | tf_op jit(solution)/shard_map/all_to_all | solution.py:283
  224.3 0.0 copy-done.4
  224.3 0.7 shard_map.96
  225.0 17.2 %all_to_all.51 = f32[64,1,1,128]{3,2,1,0:T(1,128)S(1)} all-to-all(f32[64,1,1,128]{3,2,1,0:T(1,128)S(1)} %bitcast.42), channel_id=1, replica_groups=mesh['op_0'=4,'op_1'=8,'op_2'=2,'sec'=8] {'op_0','op_2','sec'}, dimensions={0} | all-to-all | bytes 65536 | tf_op jit(solution)/shard_map/all_to_all | solution.py:283
  242.2 10.4 %all_to_all.52 = f32[8,1,1,128]{3,2,1,0:T(1,128)S(1)} all-to-all(f32[8,1,1,128]{3,2,1,0:T(1,128)S(1)} %bitcast.44), channel_id=1, replica_groups=mesh['op_0'=4,'op_1'=8,'op_2'=2,'sec'=8] {'op_1'}, dimensions={0} | all-to-all | bytes 8192 | tf_op jit(solution)/shard_map/all_to_all | solution.py:283
  252.6 1.1 shard_map.98
  (3 shorter events, 0.0 us)
Async XLA Ops:
  18.7 0.7 copy-start.5
  21.1 16.3 %copy-start.3 = (f32[56,128]{1,0:T(8,128)S(1)}, f32[56,128]{1,0:T(8,128)}, u32[]{:S(2)}) copy-start(f32[56,128]{1,0:T(8,128)} %get-tuple-element.27.d_ref) | copy-start | bytes 86020
  21.1 57.4 %all-to-all-start.1 = ((f32[64,50,1,128]{3,2,1,0:T(1,128)}), f32[64,50,1,128]{3,2,1,0:T(1,128)}, u32[]{:S(2)}, u32[]{:S(2)}) async-start(f32[64,50,1,128]{3,2,1,0:T(1,128)} %bitcast.5), calls=%async_computation.1 | async-start | bytes 3276800 | tf_op jit(solution)/shard_map/all_to_all | solution.py:283
  37.4 6.2 %collective-permute-start = (f32[56,128]{1,0:T(8,128)S(1)}, f32[56,128]{1,0:T(8,128)S(1)}, u32[]{:S(2)}, u32[]{:S(2)}) collective-permute-start(f32[56,128]{1,0:T(8,128)S(1)} %copy-done.3), channel_id=1, source_target_pairs={{0,1},{1,2},{2,3},{3,4},{4,5},{5,6},{6,7},{7,0},{8,9},{9,10},{10,1... | collective-permute-start | bytes 86024 | tf_op jit(solution)/shard_map/ppermute | solution.py:357
  43.7 7.3 %collective-permute-start.1 = (f32[112,128]{1,0:T(8,128)S(1)}, f32[112,128]{1,0:T(8,128)S(1)}, u32[]{:S(2)}, u32[]{:S(2)}) collective-permute-start(f32[112,128]{1,0:T(8,128)S(1)} %pad_maximum_fusion.2), channel_id=1, source_target_pairs={{0,2},{1,3},{2,4},{3,5},{4,6},{5,7},{6,0},{7,1},{8,10},{9,11},{10,... | collective-permute-start | bytes 172040 | tf_op jit(solution)/shard_map/ppermute | solution.py:357
  51.0 9.6 %collective-permute-start.2 = (f32[224,128]{1,0:T(8,128)S(1)}, f32[224,128]{1,0:T(8,128)S(1)}, u32[]{:S(2)}, u32[]{:S(2)}) collective-permute-start(f32[224,128]{1,0:T(8,128)S(1)} %pad_maximum_fusion.1), channel_id=1, source_target_pairs={{0,4},{1,5},{2,6},{3,7},{4,0},{5,1},{6,2},{7,3},{8,12},{9,13},{10,... | collective-permute-start | bytes 344072 | tf_op jit(solution)/shard_map/ppermute | solution.py:357
  53.1 1.4 copy-start
  54.5 1.4 copy-start.1
  83.5 4.2 %collective-permute-start.3 = (f32[1600,128]{1,0:T(8,128)S(1)}, f32[1600,128]{1,0:T(8,128)S(1)}, u32[]{:S(2)}, u32[]{:S(2)}) collective-permute-start(f32[1600,128]{1,0:T(8,128)S(1)} %get-tuple-element.31), channel_id=1, source_target_pairs={{0,8},{8,0},{1,9},{9,1},{2,10},{10,2},{3,11},{11,3},{4,12},{12,4},... | collective-permute-start | bytes 2457608 | tf_op jit(solution)/shard_map/ppermute | solution.py:341
  86.8 25.7 %copy-start.6 = (s32[65]{0:T(128)S(1)}, s32[65]{0:T(128)}, u32[]{:S(2)}) copy-start(s32[65]{0:T(128)} %get-tuple-element.23.slots_ref) | copy-start | bytes 784
  87.8 57.9 %copy-start.2 = (f32[448,128]{1,0:T(8,128)S(1)}, f32[448,128]{1,0:T(8,128)}, u32[]{:S(2)}) copy-start(f32[448,128]{1,0:T(8,128)} %pad_maximum_fusion.d8_ref) | copy-start | bytes 688132
  195.3 4.2 %collective-permute-start.4 = (f32[1600,128]{1,0:T(8,128)S(1)}, f32[1600,128]{1,0:T(8,128)S(1)}, u32[]{:S(2)}, u32[]{:S(2)}) collective-permute-start(f32[1600,128]{1,0:T(8,128)S(1)} %get-tuple-element.37), channel_id=1, source_target_pairs={{0,8},{8,0},{1,9},{9,1},{2,10},{10,2},{3,11},{11,3},{4,12},{12,4},... | collective-permute-start | bytes 2457608 | tf_op jit(solution)/shard_map/ppermute | solution.py:341
  198.7 25.6 %copy-start.4 = (f32[50,128]{1,0:T(8,128)S(1)}, f32[50,128]{1,0:T(8,128)}, u32[]{:S(2)}) copy-start(f32[50,128]{1,0:T(8,128)} %get-tuple-element.39.v_ref) | copy-start | bytes 76804

commit v5 on v4

--- a/solution.py
+++ b/solution.py
@@ -139,24 +139,28 @@
 
 
 def left_product(mats_ref, ih_ref, il_ref, out_ref, first, per_row):
-    step = 160
+    step = 320
+    weights = jnp.concatenate([ih_ref[...], il_ref[...], ih_ref[...]], axis=0)
     for m in range(out_ref.shape[0] // per_row // step):
         at = pl.ds(first + m * step, step)
-        y = dot3(mats_ref[0, at, :], mats_ref[1, at, :], ih_ref[...], il_ref[...])
+        hi = mats_ref[0, at, :]
+        y = jnp.dot(jnp.concatenate([hi, hi, mats_ref[1, at, :]], axis=1), weights, preferred_element_type=jnp.float32)
         for k in range(per_row):
             out_ref[pl.ds(m * step * per_row + k, step, stride=per_row), :] = y[:, k * LANES : (k + 1) * LANES]
 
 
 def inner_kernel(per_row, x_ref, mats_ref, ih_ref, il_ref, out_ref):
     width = mats_ref.shape[1]
-    step = 160
+    step = 640
+    weights = jnp.concatenate([mats_ref[2], mats_ref[3], mats_ref[2]], axis=0)
     for m in range(width // step):
         x = jnp.concatenate(
             [x_ref[pl.ds(m * step * per_row + k, step, stride=per_row), :] for k in range(per_row)], axis=1
         )
         x_hi, x_lo = halves(x)
         at = pl.ds(m * step, step)
-        ih_ref[at, :], il_ref[at, :] = halves(dot3(x_hi, x_lo, mats_ref[2], mats_ref[3]))
+        y = jnp.dot(jnp.concatenate([x_hi, x_hi, x_lo], axis=1), weights, preferred_element_type=jnp.float32)
+        ih_ref[at, :], il_ref[at, :] = halves(y)
     left_product(mats_ref, ih_ref, il_ref, out_ref, 0, per_row)
 
 

time: 255 us -> 254 us (level)
  no operation moved by 1% of the time
where the time goes in v5:
time: 254 us; the launch traced here: 253 us
  blocking collectives  171 us (67%)
  waiting for transfers between devices  32.3 us (13%)
  starting transfers between devices  26.6 us (10%)
  Pallas kernels  17.9 us (7%)
  local copies, waits for them, and re-layouts  3.53 us (1%)
    all_to_all x8, blocking collectives, exchange(): lax.all_to_all(x.reshape(parts, lines, 1, LANES), axis, 0, 0, tiled=True)  171 us
    pallas_call x13, Pallas kernels, call(): pl.pallas_call(kernel, out_shape=out, in_specs=[SMEM] * len(smem) + [ANY]...  17.9 us
    all_to_all x1, waiting for transfers between devices, exchange(): lax.all_to_all(x.reshape(parts, lines, 1, LANES), axis, 0, 0, tiled=True)  17.3 us
    all_to_all x1, starting transfers between devices, exchange(): lax.all_to_all(x.reshape(parts, lines, 1, LANES), axis, 0, 0, tiled=True)  16.3 us
    ppermute x3, waiting for transfers between devices, per_device(): lax.ppermute(d8, 'sec', [(i, (i + reach) % nsec) for i in range(nsec)])  13.1 us
    ppermute x3, starting transfers between devices, per_device(): lax.ppermute(d8, 'sec', [(i, (i + reach) % nsec) for i in range(nsec)])  6.22 us
  transfers between devices with their start and end apart: 6, of which 6 were waited for; matrix products, arithmetic and copies ran while one was open for 0% of the time, Pallas kernels for 1%

profile of v5, /device:TPU:1, one launch (start us, length us, event | category | flops | bytes accessed | tf_op | source)
XLA Modules:
  0.0 253.0 jit_solution(15559128582335919332)
XLA Ops:
  0.6 1.6 shard_map.86
  2.2 16.5 %all_to_all.45 = f32[8,50,1,128]{3,2,1,0:T(1,128)S(1)} all-to-all(f32[8,50,1,128]{3,2,1,0:T(1,128)} %bitcast.47), channel_id=1, replica_groups=mesh['op_0'=4,'op_1'=8,'op_2'=2,'sec'=8] {'sec'}, dimensions={0} | all-to-all | bytes 409600 | tf_op jit(solution)/shard_map/all_to_all | solution.py:287
  18.7 0.0 copy-start.5
  18.7 0.7 copy-done.5
  19.3 1.8 shard_map.88
  21.1 0.0 copy-start.3
  21.1 16.3 %all-to-all-start.1 = ((f32[64,50,1,128]{3,2,1,0:T(1,128)}), f32[64,50,1,128]{3,2,1,0:T(1,128)}, u32[]{:S(2)}, u32[]{:S(2)}) async-start(f32[64,50,1,128]{3,2,1,0:T(1,128)} %bitcast.5), calls=%async_computation.1 | async-start | bytes 3276800 | tf_op jit(solution)/shard_map/all_to_all | solution.py:287
  37.4 0.0 copy-done.3
  37.4 2.2 collective-permute-start
  39.6 4.0 %collective-permute-done = f32[56,128]{1,0:T(8,128)S(1)} collective-permute-done((f32[56,128]{1,0:T(8,128)S(1)}, f32[56,128]{1,0:T(8,128)S(1)}, u32[]{:S(2)}, u32[]{:S(2)}) %collective-permute-start) | collective-permute-done | bytes 28704 | tf_op jit(solution)/shard_map/ppermute | solution.py:361
  43.7 1.9 collective-permute-start.1
  45.6 5.4 %collective-permute-done.1 = f32[112,128]{1,0:T(8,128)S(1)} collective-permute-done((f32[112,128]{1,0:T(8,128)S(1)}, f32[112,128]{1,0:T(8,128)S(1)}, u32[]{:S(2)}, u32[]{:S(2)}) %collective-permute-start.1) | collective-permute-done | bytes 57376 | tf_op jit(solution)/shard_map/ppermute | solution.py:361
  51.0 2.1 collective-permute-start.2
  53.1 0.0 copy-start
  53.1 1.4 copy-done
  54.5 0.0 copy-start.1
  54.6 1.4 copy-done.1
  56.0 0.9 shard_map.87.mats_ref
  56.9 3.7 %collective-permute-done.2 = f32[224,128]{1,0:T(8,128)S(1)} collective-permute-done((f32[224,128]{1,0:T(8,128)S(1)}, f32[224,128]{1,0:T(8,128)S(1)}, u32[]{:S(2)}, u32[]{:S(2)}) %collective-permute-start.2) | collective-permute-done | bytes 114720 | tf_op jit(solution)/shard_map/ppermute | solution.py:361
  60.6 0.7 pad_maximum_fusion.d8_ref
  61.3 17.3 %all-to-all-done.1 = f32[64,50,1,128]{3,2,1,0:T(1,128)} async-done(((f32[64,50,1,128]{3,2,1,0:T(1,128)}), f32[64,50,1,128]{3,2,1,0:T(1,128)}, u32[]{:S(2)}, u32[]{:S(2)}) %all-to-all-start.1) | async-done | bytes 1638432 | tf_op jit(solution)/shard_map/all_to_all | solution.py:287
  78.5 4.7 %shard_map.89 = (bf16[640,640]{1,0:T(8,128)(2,1)S(1)}, bf16[640,640]{1,0:T(8,128)(2,1)S(1)}, f32[1600,128]{1,0:T(8,128)S(1)}) custom-call(f32[3200,128]{1,0:T(8,128)} %bitcast.6.x_ref, bf16[4,640,640]{2,1,0:T(8,128)(2,1)S(1)} %shard_map.87.mats_ref), custom_call_target="tpu_custom_call" | custom-call | tf_op jit(solution)/shard_map/pallas_call | solution.py:275
  83.2 1.9 collective-permute-start.3
  85.1 1.2 shard_map.90
  86.3 0.0 copy-start.6
  86.3 1.1 collective-permute-done.3
  87.4 0.1 add.6
  87.5 0.0 copy-start.2
  87.5 24.7 %all_to_all.46 = f32[32,50,1,128]{3,2,1,0:T(1,128)S(1)} all-to-all(f32[32,50,1,128]{3,2,1,0:T(1,128)S(1)} %bitcast.45), channel_id=1, replica_groups=mesh['op_0'=4,'op_1'=8,'op_2'=2,'sec'=8] {'op_0','op_1'}, dimensions={0} | all-to-all | bytes 1638400 | tf_op jit(solution)/shard_map/all_to_all | solution.py:287
  112.2 0.0 copy-done.6
  112.2 0.6 shard_map.91
  112.8 11.1 %all_to_all.47 = f32[8,50,1,128]{3,2,1,0:T(1,128)S(1)} all-to-all(f32[8,50,1,128]{3,2,1,0:T(1,128)S(1)} %bitcast.38), channel_id=1, replica_groups=mesh['op_0'=4,'op_1'=8,'op_2'=2,'sec'=8] {'sec'}, dimensions={0} | all-to-all | bytes 409600 | tf_op jit(solution)/shard_map/all_to_all | solution.py:287
  123.9 0.1 shard_map.92
  124.1 21.3 %all_to_all.48 = f32[64,1,1,128]{3,2,1,0:T(1,128)S(1)} all-to-all(f32[64,1,1,128]{3,2,1,0:T(1,128)S(1)} %bitcast.40), channel_id=1, replica_groups=mesh['op_0'=4,'op_1'=8,'op_2'=2,'sec'=8] {'op_0','op_1','op_2'}, dimensions={0} | all-to-all | bytes 65536 | tf_op jit(solution)/shard_map/all_to_all | solution.py:287
  145.4 0.0 copy-done.2
  145.4 0.9 shard_map.93
  146.3 45.2 %all_to_all.49 = f32[64,50,1,128]{3,2,1,0:T(1,128)S(1)} all-to-all(f32[64,50,1,128]{3,2,1,0:T(1,128)S(1)} %bitcast.37), channel_id=1, replica_groups=mesh['op_0'=4,'op_1'=8,'op_2'=2,'sec'=8] {'op_0','op_1','op_2'}, dimensions={0} | all-to-all | bytes 3276800 | tf_op jit(solution)/shard_map/all_to_all | solution.py:287
  191.4 3.2 %shard_map.94 = (bf16[640,640]{1,0:T(8,128)(2,1)S(1)}, bf16[640,640]{1,0:T(8,128)(2,1)S(1)}, f32[1600,128]{1,0:T(8,128)S(1)}) custom-call(f32[3200,128]{1,0:T(8,128)S(1)} %bitcast.27, bf16[4,640,640]{2,1,0:T(8,128)(2,1)S(1)} %shard_map.87.mats_ref), custom_call_target="tpu_custom_call" | custom-call | tf_op jit(solution)/shard_map/pallas_call | solution.py:275
  194.7 2.2 collective-permute-start.4
  196.9 1.2 shard_map.95
  198.0 0.0 copy-start.4
  198.0 0.9 collective-permute-done.4
  198.9 0.1 add.7
  199.0 24.6 %all_to_all.50 = f32[32,50,1,128]{3,2,1,0:T(1,128)S(1)} all-to-all(f32[32,50,1,128]{3,2,1,0:T(1,128)S(1)} %bitcast.46), channel_id=1, replica_groups=mesh['op_0'=4,'op_1'=8,'op_2'=2,'sec'=8] {'op_0','op_1'}, dimensions={0} | all-to-all | bytes 1638400 | tf_op jit(solution)/shard_map/all_to_all | solution.py:287
  223.6 0.0 copy-done.4
  223.6 0.7 shard_map.96
  224.3 17.2 %all_to_all.51 = f32[64,1,1,128]{3,2,1,0:T(1,128)S(1)} all-to-all(f32[64,1,1,128]{3,2,1,0:T(1,128)S(1)} %bitcast.42), channel_id=1, replica_groups=mesh['op_0'=4,'op_1'=8,'op_2'=2,'sec'=8] {'op_0','op_2','sec'}, dimensions={0} | all-to-all | bytes 65536 | tf_op jit(solution)/shard_map/all_to_all | solution.py:287
  241.5 10.4 %all_to_all.52 = f32[8,1,1,128]{3,2,1,0:T(1,128)S(1)} all-to-all(f32[8,1,1,128]{3,2,1,0:T(1,128)S(1)} %bitcast.44), channel_id=1, replica_groups=mesh['op_0'=4,'op_1'=8,'op_2'=2,'sec'=8] {'op_1'}, dimensions={0} | all-to-all | bytes 8192 | tf_op jit(solution)/shard_map/all_to_all | solution.py:287
  251.9 1.1 shard_map.98
  (3 shorter events, 0.0 us)
Async XLA Ops:
  18.7 0.7 copy-start.5
  21.1 16.3 %copy-start.3 = (f32[56,128]{1,0:T(8,128)S(1)}, f32[56,128]{1,0:T(8,128)}, u32[]{:S(2)}) copy-start(f32[56,128]{1,0:T(8,128)} %get-tuple-element.27.d_ref) | copy-start | bytes 86020
  21.1 57.4 %all-to-all-start.1 = ((f32[64,50,1,128]{3,2,1,0:T(1,128)}), f32[64,50,1,128]{3,2,1,0:T(1,128)}, u32[]{:S(2)}, u32[]{:S(2)}) async-start(f32[64,50,1,128]{3,2,1,0:T(1,128)} %bitcast.5), calls=%async_computation.1 | async-start | bytes 3276800 | tf_op jit(solution)/shard_map/all_to_all | solution.py:287
  37.4 6.2 %collective-permute-start = (f32[56,128]{1,0:T(8,128)S(1)}, f32[56,128]{1,0:T(8,128)S(1)}, u32[]{:S(2)}, u32[]{:S(2)}) collective-permute-start(f32[56,128]{1,0:T(8,128)S(1)} %copy-done.3), channel_id=1, source_target_pairs={{0,1},{1,2},{2,3},{3,4},{4,5},{5,6},{6,7},{7,0},{8,9},{9,10},{10,1... | collective-permute-start | bytes 86024 | tf_op jit(solution)/shard_map/ppermute | solution.py:361
  43.7 7.3 %collective-permute-start.1 = (f32[112,128]{1,0:T(8,128)S(1)}, f32[112,128]{1,0:T(8,128)S(1)}, u32[]{:S(2)}, u32[]{:S(2)}) collective-permute-start(f32[112,128]{1,0:T(8,128)S(1)} %pad_maximum_fusion.2), channel_id=1, source_target_pairs={{0,2},{1,3},{2,4},{3,5},{4,6},{5,7},{6,0},{7,1},{8,10},{9,11},{10,... | collective-permute-start | bytes 172040 | tf_op jit(solution)/shard_map/ppermute | solution.py:361
  51.0 9.6 %collective-permute-start.2 = (f32[224,128]{1,0:T(8,128)S(1)}, f32[224,128]{1,0:T(8,128)S(1)}, u32[]{:S(2)}, u32[]{:S(2)}) collective-permute-start(f32[224,128]{1,0:T(8,128)S(1)} %pad_maximum_fusion.1), channel_id=1, source_target_pairs={{0,4},{1,5},{2,6},{3,7},{4,0},{5,1},{6,2},{7,3},{8,12},{9,13},{10,... | collective-permute-start | bytes 344072 | tf_op jit(solution)/shard_map/ppermute | solution.py:361
  53.1 1.4 copy-start
  54.5 1.4 copy-start.1
  83.2 4.2 %collective-permute-start.3 = (f32[1600,128]{1,0:T(8,128)S(1)}, f32[1600,128]{1,0:T(8,128)S(1)}, u32[]{:S(2)}, u32[]{:S(2)}) collective-permute-start(f32[1600,128]{1,0:T(8,128)S(1)} %get-tuple-element.31), channel_id=1, source_target_pairs={{0,8},{8,0},{1,9},{9,1},{2,10},{10,2},{3,11},{11,3},{4,12},{12,4},... | collective-permute-start | bytes 2457608 | tf_op jit(solution)/shard_map/ppermute | solution.py:345
  86.3 25.9 %copy-start.6 = (s32[65]{0:T(128)S(1)}, s32[65]{0:T(128)}, u32[]{:S(2)}) copy-start(s32[65]{0:T(128)} %get-tuple-element.23.slots_ref) | copy-start | bytes 784
  87.5 57.9 %copy-start.2 = (f32[448,128]{1,0:T(8,128)S(1)}, f32[448,128]{1,0:T(8,128)}, u32[]{:S(2)}) copy-start(f32[448,128]{1,0:T(8,128)} %pad_maximum_fusion.d8_ref) | copy-start | bytes 688132
  194.7 4.2 %collective-permute-start.4 = (f32[1600,128]{1,0:T(8,128)S(1)}, f32[1600,128]{1,0:T(8,128)S(1)}, u32[]{:S(2)}, u32[]{:S(2)}) collective-permute-start(f32[1600,128]{1,0:T(8,128)S(1)} %get-tuple-element.37), channel_id=1, source_target_pairs={{0,8},{8,0},{1,9},{9,1},{2,10},{10,2},{3,11},{11,3},{4,12},{12,4},... | collective-permute-start | bytes 2457608 | tf_op jit(solution)/shard_map/ppermute | solution.py:345
  198.0 25.6 %copy-start.4 = (f32[50,128]{1,0:T(8,128)S(1)}, f32[50,128]{1,0:T(8,128)}, u32[]{:S(2)}) copy-start(f32[50,128]{1,0:T(8,128)} %get-tuple-element.39.v_ref) | copy-start | bytes 76804

commit v6 on v5

--- a/solution.py
+++ b/solution.py
@@ -149,11 +149,20 @@
             out_ref[pl.ds(m * step * per_row + k, step, stride=per_row), :] = y[:, k * LANES : (k + 1) * LANES]
 
 
-def inner_kernel(per_row, x_ref, mats_ref, ih_ref, il_ref, out_ref):
+def inner_kernel(per_row, pieces, x_in, mats_ref, ih_ref, il_ref, out_ref, *scratch):
     width = mats_ref.shape[1]
-    step = 640
+    step = width // pieces
+    x_ref, copies = x_in, []
+    if scratch:
+        x_ref, sems = scratch
+        for m in range(pieces):
+            at = pl.ds(m * step * per_row, step * per_row)
+            copies.append(pltpu.make_async_copy(x_in.at[at], x_ref.at[at], sems.at[m]))
+            copies[-1].start()
     weights = jnp.concatenate([mats_ref[2], mats_ref[3], mats_ref[2]], axis=0)
-    for m in range(width // step):
+    for m in range(pieces):
+        if copies:
+            copies[m].wait()
         x = jnp.concatenate(
             [x_ref[pl.ds(m * step * per_row + k, step, stride=per_row), :] for k in range(per_row)], axis=1
         )
@@ -340,8 +349,15 @@
     table = pltpu.VMEM((nsec * pad, LANES), jnp.float32)
     whole = [pltpu.VMEM((nop * lines, LANES), jnp.float32), pltpu.SemaphoreType.DMA((PIECES,))]
 
-    def products(x):
-        ih, il, other = call(part(inner_kernel, per_row), (square, square, half), (), (x, mats))
+    def products(x, streamed):
+        if streamed:
+            scratch = [whole[0], pltpu.SemaphoreType.DMA((2,))]
+            made = call(
+                part(inner_kernel, per_row, 2), (square, square, half), (), (mats,), anywhere=(x,), scratch=scratch
+            )
+        else:
+            made = call(part(inner_kernel, per_row, 1), (square, square, half), (), (x, mats))
+        ih, il, other = made
         came = lax.ppermute(other, "op_2", swap)
         own = call(part(own_kernel, per_row), half, (), (mats, ih, il))
         return exchange(own + came, CHIP, nchip)
@@ -362,7 +378,7 @@
         d8 = jnp.concatenate([d8, came], axis=0)
         reach *= 2
     chosen, d8 = lax.optimization_barrier((chosen, d8))
-    parts = products(chosen)
+    parts = products(chosen, True)
     w, w_out = call(
         part(share_kernel, lines, per_row, nsec),
         (f32(lines, LANES), f32(nsec * lines, LANES)),
@@ -379,8 +395,8 @@
         (sums, v8, d8, w8),
         scratch=[table],
     )
-    parts = products(exchange(chosen, OP, nop))
-    near = ("op_0", "op_2", "sec")
+    parts = products(exchange(chosen, OP, nop), False)
+    near = ("op_0", "op_2")
     sums, keep = call(
         part(last_sums_kernel, lines, per_row, pad),
         (f32(lax.axis_size(near), LANES), f32(5 * pad + 8, LANES)),
@@ -388,13 +404,13 @@
         (parts, scal, v, w, t, d_out),
     )
     sums = exchange(sums, near, lax.axis_size(near))
-    far = lax.axis_size("op_1")
-    sums = call(relay_kernel, f32(far, LANES), (), (sums,))
+    far = ("op_1", "sec")
+    sums = call(relay_kernel, f32(lax.axis_size(far), LANES), (), (sums,))
     return call(
         part(final_kernel, count, per_row, lines, pad),
         (f32(*psi.shape), f32(*psi.shape)),
         (),
-        (exchange(sums, "op_1", far), keep),
+        (exchange(sums, far, lax.axis_size(far)), keep),
         scratch=[pltpu.VMEM((lines, LANES), jnp.float32)] * 2,
     )
 

time: 254 us -> 254 us (level)
  no operation moved by 1% of the time
where the time goes in v6:
time: 254 us; the launch traced here: 253 us
  blocking collectives  171 us (67%)
  waiting for transfers between devices  32.3 us (13%)
  starting transfers between devices  26.6 us (10%)
  Pallas kernels  17.8 us (7%)
  local copies, waits for them, and re-layouts  3.53 us (1%)
    all_to_all x8, blocking collectives, exchange(): lax.all_to_all(x.reshape(parts, lines, 1, LANES), axis, 0, 0, tiled=True)  171 us
    pallas_call x13, Pallas kernels, call(): pl.pallas_call(kernel, out_shape=out, in_specs=[SMEM] * len(smem) + [ANY]...  17.8 us
    all_to_all x1, waiting for transfers between devices, exchange(): lax.all_to_all(x.reshape(parts, lines, 1, LANES), axis, 0, 0, tiled=True)  17.3 us
    all_to_all x1, starting transfers between devices, exchange(): lax.all_to_all(x.reshape(parts, lines, 1, LANES), axis, 0, 0, tiled=True)  16.3 us
    ppermute x3, waiting for transfers between devices, per_device(): lax.ppermute(d8, 'sec', [(i, (i + reach) % nsec) for i in range(nsec)])  13.1 us
    ppermute x3, starting transfers between devices, per_device(): lax.ppermute(d8, 'sec', [(i, (i + reach) % nsec) for i in range(nsec)])  6.22 us
  transfers between devices with their start and end apart: 6, of which 6 were waited for; matrix products, arithmetic and copies ran while one was open for 0% of the time, Pallas kernels for 1%

profile of v6, /device:TPU:1, one launch (start us, length us, event | category | flops | bytes accessed | tf_op | source)
XLA Modules:
  0.0 252.8 jit_solution(34580670406311308)
XLA Ops:
  0.6 1.6 shard_map.86
  2.2 16.5 %all_to_all.45 = f32[8,50,1,128]{3,2,1,0:T(1,128)S(1)} all-to-all(f32[8,50,1,128]{3,2,1,0:T(1,128)} %bitcast.47), channel_id=1, replica_groups=mesh['op_0'=4,'op_1'=8,'op_2'=2,'sec'=8] {'sec'}, dimensions={0} | all-to-all | bytes 409600 | tf_op jit(solution)/shard_map/all_to_all | solution.py:296
  18.7 0.0 copy-start.5
  18.7 0.7 copy-done.5
  19.3 1.8 shard_map.88
  21.1 0.0 copy-start.3
  21.1 16.3 %all-to-all-start.1 = ((f32[64,50,1,128]{3,2,1,0:T(1,128)}), f32[64,50,1,128]{3,2,1,0:T(1,128)}, u32[]{:S(2)}, u32[]{:S(2)}) async-start(f32[64,50,1,128]{3,2,1,0:T(1,128)} %bitcast.5), calls=%async_computation.1 | async-start | bytes 3276800 | tf_op jit(solution)/shard_map/all_to_all | solution.py:296
  37.4 0.0 copy-done.3
  37.4 2.2 collective-permute-start
  39.6 4.0 %collective-permute-done = f32[56,128]{1,0:T(8,128)S(1)} collective-permute-done((f32[56,128]{1,0:T(8,128)S(1)}, f32[56,128]{1,0:T(8,128)S(1)}, u32[]{:S(2)}, u32[]{:S(2)}) %collective-permute-start) | collective-permute-done | bytes 28704 | tf_op jit(solution)/shard_map/ppermute | solution.py:377
  43.7 1.9 collective-permute-start.1
  45.6 5.4 %collective-permute-done.1 = f32[112,128]{1,0:T(8,128)S(1)} collective-permute-done((f32[112,128]{1,0:T(8,128)S(1)}, f32[112,128]{1,0:T(8,128)S(1)}, u32[]{:S(2)}, u32[]{:S(2)}) %collective-permute-start.1) | collective-permute-done | bytes 57376 | tf_op jit(solution)/shard_map/ppermute | solution.py:377
  51.0 2.1 collective-permute-start.2
  53.1 0.0 copy-start
  53.1 1.4 copy-done
  54.5 0.0 copy-start.1
  54.6 1.4 copy-done.1
  56.0 0.9 shard_map.87.mats_ref
  56.9 3.7 %collective-permute-done.2 = f32[224,128]{1,0:T(8,128)S(1)} collective-permute-done((f32[224,128]{1,0:T(8,128)S(1)}, f32[224,128]{1,0:T(8,128)S(1)}, u32[]{:S(2)}, u32[]{:S(2)}) %collective-permute-start.2) | collective-permute-done | bytes 114720 | tf_op jit(solution)/shard_map/ppermute | solution.py:377
  60.6 0.7 pad_maximum_fusion.d8_ref
  61.3 17.3 %all-to-all-done.1 = f32[64,50,1,128]{3,2,1,0:T(1,128)} async-done(((f32[64,50,1,128]{3,2,1,0:T(1,128)}), f32[64,50,1,128]{3,2,1,0:T(1,128)}, u32[]{:S(2)}, u32[]{:S(2)}) %all-to-all-start.1) | async-done | bytes 1638432 | tf_op jit(solution)/shard_map/all_to_all | solution.py:296
  78.5 4.5 %shard_map.89 = (bf16[640,640]{1,0:T(8,128)(2,1)S(1)}, bf16[640,640]{1,0:T(8,128)(2,1)S(1)}, f32[1600,128]{1,0:T(8,128)S(1)}) custom-call(f32[3200,128]{1,0:T(8,128)} %bitcast.6.x_in, bf16[4,640,640]{2,1,0:T(8,128)(2,1)S(1)} %shard_map.87.mats_ref), custom_call_target="tpu_custom_call" | custom-call | tf_op jit(solution)/shard_map/pallas_call | solution.py:284
  83.0 1.9 collective-permute-start.3
  85.0 1.2 shard_map.90
  86.2 0.0 copy-start.6
  86.2 1.1 collective-permute-done.3
  87.3 0.1 add.6
  87.3 0.0 copy-start.2
  87.4 24.7 %all_to_all.46 = f32[32,50,1,128]{3,2,1,0:T(1,128)S(1)} all-to-all(f32[32,50,1,128]{3,2,1,0:T(1,128)S(1)} %bitcast.45), channel_id=1, replica_groups=mesh['op_0'=4,'op_1'=8,'op_2'=2,'sec'=8] {'op_0','op_1'}, dimensions={0} | all-to-all | bytes 1638400 | tf_op jit(solution)/shard_map/all_to_all | solution.py:296
  112.0 0.0 copy-done.6
  112.0 0.6 shard_map.91
  112.6 11.1 %all_to_all.47 = f32[8,50,1,128]{3,2,1,0:T(1,128)S(1)} all-to-all(f32[8,50,1,128]{3,2,1,0:T(1,128)S(1)} %bitcast.38), channel_id=1, replica_groups=mesh['op_0'=4,'op_1'=8,'op_2'=2,'sec'=8] {'sec'}, dimensions={0} | all-to-all | bytes 409600 | tf_op jit(solution)/shard_map/all_to_all | solution.py:296
  123.8 0.1 shard_map.92
  123.9 21.3 %all_to_all.48 = f32[64,1,1,128]{3,2,1,0:T(1,128)S(1)} all-to-all(f32[64,1,1,128]{3,2,1,0:T(1,128)S(1)} %bitcast.40), channel_id=1, replica_groups=mesh['op_0'=4,'op_1'=8,'op_2'=2,'sec'=8] {'op_0','op_1','op_2'}, dimensions={0} | all-to-all | bytes 65536 | tf_op jit(solution)/shard_map/all_to_all | solution.py:296
  145.3 0.0 copy-done.2
  145.3 0.9 shard_map.93
  146.1 45.2 %all_to_all.49 = f32[64,50,1,128]{3,2,1,0:T(1,128)S(1)} all-to-all(f32[64,50,1,128]{3,2,1,0:T(1,128)S(1)} %bitcast.37), channel_id=1, replica_groups=mesh['op_0'=4,'op_1'=8,'op_2'=2,'sec'=8] {'op_0','op_1','op_2'}, dimensions={0} | all-to-all | bytes 3276800 | tf_op jit(solution)/shard_map/all_to_all | solution.py:296
  191.3 3.2 %shard_map.94 = (bf16[640,640]{1,0:T(8,128)(2,1)S(1)}, bf16[640,640]{1,0:T(8,128)(2,1)S(1)}, f32[1600,128]{1,0:T(8,128)S(1)}) custom-call(f32[3200,128]{1,0:T(8,128)S(1)} %bitcast.27, bf16[4,640,640]{2,1,0:T(8,128)(2,1)S(1)} %shard_map.87.mats_ref), custom_call_target="tpu_custom_call" | custom-call | tf_op jit(solution)/shard_map/pallas_call | solution.py:284
  194.5 2.2 collective-permute-start.4
  196.7 1.2 shard_map.95
  197.9 0.0 copy-start.4
  197.9 0.9 collective-permute-done.4
  198.8 0.1 add.7
  198.8 24.6 %all_to_all.50 = f32[32,50,1,128]{3,2,1,0:T(1,128)S(1)} all-to-all(f32[32,50,1,128]{3,2,1,0:T(1,128)S(1)} %bitcast.46), channel_id=1, replica_groups=mesh['op_0'=4,'op_1'=8,'op_2'=2,'sec'=8] {'op_0','op_1'}, dimensions={0} | all-to-all | bytes 1638400 | tf_op jit(solution)/shard_map/all_to_all | solution.py:296
  223.4 0.0 copy-done.4
  223.4 0.7 shard_map.96
  224.1 11.6 %all_to_all.51 = f32[8,1,1,128]{3,2,1,0:T(1,128)S(1)} all-to-all(f32[8,1,1,128]{3,2,1,0:T(1,128)S(1)} %bitcast.44), channel_id=1, replica_groups=mesh['op_0'=4,'op_1'=8,'op_2'=2,'sec'=8] {'op_0','op_2'}, dimensions={0} | all-to-all | bytes 8192 | tf_op jit(solution)/shard_map/all_to_all | solution.py:296
  235.7 15.9 %all_to_all.52 = f32[64,1,1,128]{3,2,1,0:T(1,128)S(1)} all-to-all(f32[64,1,1,128]{3,2,1,0:T(1,128)S(1)} %bitcast.41), channel_id=1, replica_groups=mesh['op_0'=4,'op_1'=8,'op_2'=2,'sec'=8] {'op_1','sec'}, dimensions={0} | all-to-all | bytes 65536 | tf_op jit(solution)/shard_map/all_to_all | solution.py:296
  251.7 1.1 shard_map.98
  (3 shorter events, 0.0 us)
Async XLA Ops:
  18.7 0.7 copy-start.5
  21.1 16.3 %copy-start.3 = (f32[56,128]{1,0:T(8,128)S(1)}, f32[56,128]{1,0:T(8,128)}, u32[]{:S(2)}) copy-start(f32[56,128]{1,0:T(8,128)} %get-tuple-element.27.d_ref) | copy-start | bytes 86020
  21.1 57.4 %all-to-all-start.1 = ((f32[64,50,1,128]{3,2,1,0:T(1,128)}), f32[64,50,1,128]{3,2,1,0:T(1,128)}, u32[]{:S(2)}, u32[]{:S(2)}) async-start(f32[64,50,1,128]{3,2,1,0:T(1,128)} %bitcast.5), calls=%async_computation.1 | async-start | bytes 3276800 | tf_op jit(solution)/shard_map/all_to_all | solution.py:296
  37.4 6.2 %collective-permute-start = (f32[56,128]{1,0:T(8,128)S(1)}, f32[56,128]{1,0:T(8,128)S(1)}, u32[]{:S(2)}, u32[]{:S(2)}) collective-permute-start(f32[56,128]{1,0:T(8,128)S(1)} %copy-done.3), channel_id=1, source_target_pairs={{0,1},{1,2},{2,3},{3,4},{4,5},{5,6},{6,7},{7,0},{8,9},{9,10},{10,1... | collective-permute-start | bytes 86024 | tf_op jit(solution)/shard_map/ppermute | solution.py:377
  43.7 7.3 %collective-permute-start.1 = (f32[112,128]{1,0:T(8,128)S(1)}, f32[112,128]{1,0:T(8,128)S(1)}, u32[]{:S(2)}, u32[]{:S(2)}) collective-permute-start(f32[112,128]{1,0:T(8,128)S(1)} %pad_maximum_fusion.2), channel_id=1, source_target_pairs={{0,2},{1,3},{2,4},{3,5},{4,6},{5,7},{6,0},{7,1},{8,10},{9,11},{10,... | collective-permute-start | bytes 172040 | tf_op jit(solution)/shard_map/ppermute | solution.py:377
  51.0 9.6 %collective-permute-start.2 = (f32[224,128]{1,0:T(8,128)S(1)}, f32[224,128]{1,0:T(8,128)S(1)}, u32[]{:S(2)}, u32[]{:S(2)}) collective-permute-start(f32[224,128]{1,0:T(8,128)S(1)} %pad_maximum_fusion.1), channel_id=1, source_target_pairs={{0,4},{1,5},{2,6},{3,7},{4,0},{5,1},{6,2},{7,3},{8,12},{9,13},{10,... | collective-permute-start | bytes 344072 | tf_op jit(solution)/shard_map/ppermute | solution.py:377
  53.1 1.4 copy-start
  54.5 1.4 copy-start.1
  83.0 4.2 %collective-permute-start.3 = (f32[1600,128]{1,0:T(8,128)S(1)}, f32[1600,128]{1,0:T(8,128)S(1)}, u32[]{:S(2)}, u32[]{:S(2)}) collective-permute-start(f32[1600,128]{1,0:T(8,128)S(1)} %get-tuple-element.31), channel_id=1, source_target_pairs={{0,8},{8,0},{1,9},{9,1},{2,10},{10,2},{3,11},{11,3},{4,12},{12,4},... | collective-permute-start | bytes 2457608 | tf_op jit(solution)/shard_map/ppermute | solution.py:361
  86.2 25.9 %copy-start.6 = (s32[65]{0:T(128)S(1)}, s32[65]{0:T(128)}, u32[]{:S(2)}) copy-start(s32[65]{0:T(128)} %get-tuple-element.23.slots_ref) | copy-start | bytes 784
  87.3 57.9 %copy-start.2 = (f32[448,128]{1,0:T(8,128)S(1)}, f32[448,128]{1,0:T(8,128)}, u32[]{:S(2)}) copy-start(f32[448,128]{1,0:T(8,128)} %pad_maximum_fusion.d8_ref) | copy-start | bytes 688132
  194.5 4.2 %collective-permute-start.4 = (f32[1600,128]{1,0:T(8,128)S(1)}, f32[1600,128]{1,0:T(8,128)S(1)}, u32[]{:S(2)}, u32[]{:S(2)}) collective-permute-start(f32[1600,128]{1,0:T(8,128)S(1)} %get-tuple-element.37), channel_id=1, source_target_pairs={{0,8},{8,0},{1,9},{9,1},{2,10},{10,2},{3,11},{11,3},{4,12},{12,4},... | collective-permute-start | bytes 2457608 | tf_op jit(solution)/shard_map/ppermute | solution.py:361
  197.9 25.5 %copy-start.4 = (f32[50,128]{1,0:T(8,128)S(1)}, f32[50,128]{1,0:T(8,128)}, u32[]{:S(2)}) copy-start(f32[50,128]{1,0:T(8,128)} %get-tuple-element.39.v_ref) | copy-start | bytes 76804

commit v7 on v6

--- a/solution.py
+++ b/solution.py
@@ -82,7 +82,7 @@
             v_out_ref[pl.ds(y * lines + k, rows, stride=per_row), :] = v[:, part]
 
 
-PIECES = 4
+PIECES = 8
 
 
 def pick(table_ref, slots_ref, t, lines, pitch):
@@ -396,7 +396,7 @@
         scratch=[table],
     )
     parts = products(exchange(chosen, OP, nop), False)
-    near = ("op_0", "op_2")
+    near = ("op_0", "op_2", "sec")
     sums, keep = call(
         part(last_sums_kernel, lines, per_row, pad),
         (f32(lax.axis_size(near), LANES), f32(5 * pad + 8, LANES)),
@@ -404,7 +404,7 @@
         (parts, scal, v, w, t, d_out),
     )
     sums = exchange(sums, near, lax.axis_size(near))
-    far = ("op_1", "sec")
+    far = ("op_1",)
     sums = call(relay_kernel, f32(lax.axis_size(far), LANES), (), (sums,))
     return call(
         part(final_kernel, count, per_row, lines, pad),

time: 254 us -> 254 us (level)
  no operation moved by 1% of the time
where the time goes in v7:
time: 254 us; the launch traced here: 253 us
  blocking collectives  171 us (67%)
  waiting for transfers between devices  32.3 us (13%)
  starting transfers between devices  26.6 us (10%)
  Pallas kernels  17.8 us (7%)
  local copies, waits for them, and re-layouts  3.53 us (1%)
    all_to_all x8, blocking collectives, exchange(): lax.all_to_all(x.reshape(parts, lines, 1, LANES), axis, 0, 0, tiled=True)  171 us
    pallas_call x13, Pallas kernels, call(): pl.pallas_call(kernel, out_shape=out, in_specs=[SMEM] * len(smem) + [ANY]...  17.8 us
    all_to_all x1, waiting for transfers between devices, exchange(): lax.all_to_all(x.reshape(parts, lines, 1, LANES), axis, 0, 0, tiled=True)  17.3 us
    all_to_all x1, starting transfers between devices, exchange(): lax.all_to_all(x.reshape(parts, lines, 1, LANES), axis, 0, 0, tiled=True)  16.3 us
    ppermute x3, waiting for transfers between devices, per_device(): lax.ppermute(d8, 'sec', [(i, (i + reach) % nsec) for i in range(nsec)])  13.1 us
    ppermute x3, starting transfers between devices, per_device(): lax.ppermute(d8, 'sec', [(i, (i + reach) % nsec) for i in range(nsec)])  6.22 us
  transfers between devices with their start and end apart: 6, of which 6 were waited for; matrix products, arithmetic and copies ran while one was open for 0% of the time, Pallas kernels for 1%

profile of v7, /device:TPU:1, one launch (start us, length us, event | category | flops | bytes accessed | tf_op | source)
XLA Modules:
  0.0 252.9 jit_solution(3388562910293730978)
XLA Ops:
  0.6 1.6 shard_map.86
  2.2 16.5 %all_to_all.45 = f32[8,50,1,128]{3,2,1,0:T(1,128)S(1)} all-to-all(f32[8,50,1,128]{3,2,1,0:T(1,128)} %bitcast.47), channel_id=1, replica_groups=mesh['op_0'=4,'op_1'=8,'op_2'=2,'sec'=8] {'sec'}, dimensions={0} | all-to-all | bytes 409600 | tf_op jit(solution)/shard_map/all_to_all | solution.py:296
  18.7 0.0 copy-start.5
  18.7 0.7 copy-done.5
  19.3 1.8 shard_map.88
  21.2 0.0 copy-start.3
  21.2 16.3 %all-to-all-start.1 = ((f32[64,50,1,128]{3,2,1,0:T(1,128)}), f32[64,50,1,128]{3,2,1,0:T(1,128)}, u32[]{:S(2)}, u32[]{:S(2)}) async-start(f32[64,50,1,128]{3,2,1,0:T(1,128)} %bitcast.5), calls=%async_computation.1 | async-start | bytes 3276800 | tf_op jit(solution)/shard_map/all_to_all | solution.py:296
  37.5 0.0 copy-done.3
  37.5 2.2 collective-permute-start
  39.7 4.0 %collective-permute-done = f32[56,128]{1,0:T(8,128)S(1)} collective-permute-done((f32[56,128]{1,0:T(8,128)S(1)}, f32[56,128]{1,0:T(8,128)S(1)}, u32[]{:S(2)}, u32[]{:S(2)}) %collective-permute-start) | collective-permute-done | bytes 28704 | tf_op jit(solution)/shard_map/ppermute | solution.py:377
  43.7 1.9 collective-permute-start.1
  45.6 5.4 %collective-permute-done.1 = f32[112,128]{1,0:T(8,128)S(1)} collective-permute-done((f32[112,128]{1,0:T(8,128)S(1)}, f32[112,128]{1,0:T(8,128)S(1)}, u32[]{:S(2)}, u32[]{:S(2)}) %collective-permute-start.1) | collective-permute-done | bytes 57376 | tf_op jit(solution)/shard_map/ppermute | solution.py:377
  51.0 2.1 collective-permute-start.2
  53.1 0.0 copy-start
  53.1 1.4 copy-done
  54.6 0.0 copy-start.1
  54.6 1.4 copy-done.1
  56.0 0.9 shard_map.87.mats_ref
  56.9 3.7 %collective-permute-done.2 = f32[224,128]{1,0:T(8,128)S(1)} collective-permute-done((f32[224,128]{1,0:T(8,128)S(1)}, f32[224,128]{1,0:T(8,128)S(1)}, u32[]{:S(2)}, u32[]{:S(2)}) %collective-permute-start.2) | collective-permute-done | bytes 114720 | tf_op jit(solution)/shard_map/ppermute | solution.py:377
  60.6 0.7 pad_maximum_fusion.d8_ref
  61.3 17.3 %all-to-all-done.1 = f32[64,50,1,128]{3,2,1,0:T(1,128)} async-done(((f32[64,50,1,128]{3,2,1,0:T(1,128)}), f32[64,50,1,128]{3,2,1,0:T(1,128)}, u32[]{:S(2)}, u32[]{:S(2)}) %all-to-all-start.1) | async-done | bytes 1638432 | tf_op jit(solution)/shard_map/all_to_all | solution.py:296
  78.6 4.5 %shard_map.89 = (bf16[640,640]{1,0:T(8,128)(2,1)S(1)}, bf16[640,640]{1,0:T(8,128)(2,1)S(1)}, f32[1600,128]{1,0:T(8,128)S(1)}) custom-call(f32[3200,128]{1,0:T(8,128)} %bitcast.6.x_in, bf16[4,640,640]{2,1,0:T(8,128)(2,1)S(1)} %shard_map.87.mats_ref), custom_call_target="tpu_custom_call" | custom-call | tf_op jit(solution)/shard_map/pallas_call | solution.py:284
  83.1 1.9 collective-permute-start.3
  85.0 1.2 shard_map.90
  86.2 0.0 copy-start.6
  86.2 1.1 collective-permute-done.3
  87.3 0.1 add.6
  87.4 0.0 copy-start.2
  87.4 24.7 %all_to_all.46 = f32[32,50,1,128]{3,2,1,0:T(1,128)S(1)} all-to-all(f32[32,50,1,128]{3,2,1,0:T(1,128)S(1)} %bitcast.45), channel_id=1, replica_groups=mesh['op_0'=4,'op_1'=8,'op_2'=2,'sec'=8] {'op_0','op_1'}, dimensions={0} | all-to-all | bytes 1638400 | tf_op jit(solution)/shard_map/all_to_all | solution.py:296
  112.0 0.0 copy-done.6
  112.0 0.6 shard_map.91
  112.7 11.1 %all_to_all.47 = f32[8,50,1,128]{3,2,1,0:T(1,128)S(1)} all-to-all(f32[8,50,1,128]{3,2,1,0:T(1,128)S(1)} %bitcast.38), channel_id=1, replica_groups=mesh['op_0'=4,'op_1'=8,'op_2'=2,'sec'=8] {'sec'}, dimensions={0} | all-to-all | bytes 409600 | tf_op jit(solution)/shard_map/all_to_all | solution.py:296
  123.8 0.1 shard_map.92
  123.9 21.3 %all_to_all.48 = f32[64,1,1,128]{3,2,1,0:T(1,128)S(1)} all-to-all(f32[64,1,1,128]{3,2,1,0:T(1,128)S(1)} %bitcast.40), channel_id=1, replica_groups=mesh['op_0'=4,'op_1'=8,'op_2'=2,'sec'=8] {'op_0','op_1','op_2'}, dimensions={0} | all-to-all | bytes 65536 | tf_op jit(solution)/shard_map/all_to_all | solution.py:296
  145.3 0.0 copy-done.2
  145.3 0.9 shard_map.93
  146.2 45.2 %all_to_all.49 = f32[64,50,1,128]{3,2,1,0:T(1,128)S(1)} all-to-all(f32[64,50,1,128]{3,2,1,0:T(1,128)S(1)} %bitcast.37), channel_id=1, replica_groups=mesh['op_0'=4,'op_1'=8,'op_2'=2,'sec'=8] {'op_0','op_1','op_2'}, dimensions={0} | all-to-all | bytes 3276800 | tf_op jit(solution)/shard_map/all_to_all | solution.py:296
  191.3 3.2 %shard_map.94 = (bf16[640,640]{1,0:T(8,128)(2,1)S(1)}, bf16[640,640]{1,0:T(8,128)(2,1)S(1)}, f32[1600,128]{1,0:T(8,128)S(1)}) custom-call(f32[3200,128]{1,0:T(8,128)S(1)} %bitcast.27, bf16[4,640,640]{2,1,0:T(8,128)(2,1)S(1)} %shard_map.87.mats_ref), custom_call_target="tpu_custom_call" | custom-call | tf_op jit(solution)/shard_map/pallas_call | solution.py:284
  194.5 2.2 collective-permute-start.4
  196.7 1.2 shard_map.95
  197.9 0.0 copy-start.4
  197.9 0.9 collective-permute-done.4
  198.8 0.1 add.7
  198.8 24.6 %all_to_all.50 = f32[32,50,1,128]{3,2,1,0:T(1,128)S(1)} all-to-all(f32[32,50,1,128]{3,2,1,0:T(1,128)S(1)} %bitcast.46), channel_id=1, replica_groups=mesh['op_0'=4,'op_1'=8,'op_2'=2,'sec'=8] {'op_0','op_1'}, dimensions={0} | all-to-all | bytes 1638400 | tf_op jit(solution)/shard_map/all_to_all | solution.py:296
  223.4 0.0 copy-done.4
  223.4 0.7 shard_map.96
  224.2 17.2 %all_to_all.51 = f32[64,1,1,128]{3,2,1,0:T(1,128)S(1)} all-to-all(f32[64,1,1,128]{3,2,1,0:T(1,128)S(1)} %bitcast.42), channel_id=1, replica_groups=mesh['op_0'=4,'op_1'=8,'op_2'=2,'sec'=8] {'op_0','op_2','sec'}, dimensions={0} | all-to-all | bytes 65536 | tf_op jit(solution)/shard_map/all_to_all | solution.py:296
  241.4 10.4 %all_to_all.52 = f32[8,1,1,128]{3,2,1,0:T(1,128)S(1)} all-to-all(f32[8,1,1,128]{3,2,1,0:T(1,128)S(1)} %bitcast.44), channel_id=1, replica_groups=mesh['op_0'=4,'op_1'=8,'op_2'=2,'sec'=8] {'op_1'}, dimensions={0} | all-to-all | bytes 8192 | tf_op jit(solution)/shard_map/all_to_all | solution.py:296
  251.8 1.1 shard_map.98
  (3 shorter events, 0.0 us)
Async XLA Ops:
  18.7 0.7 copy-start.5
  21.2 16.3 %copy-start.3 = (f32[56,128]{1,0:T(8,128)S(1)}, f32[56,128]{1,0:T(8,128)}, u32[]{:S(2)}) copy-start(f32[56,128]{1,0:T(8,128)} %get-tuple-element.27.d_ref) | copy-start | bytes 86020
  21.2 57.4 %all-to-all-start.1 = ((f32[64,50,1,128]{3,2,1,0:T(1,128)}), f32[64,50,1,128]{3,2,1,0:T(1,128)}, u32[]{:S(2)}, u32[]{:S(2)}) async-start(f32[64,50,1,128]{3,2,1,0:T(1,128)} %bitcast.5), calls=%async_computation.1 | async-start | bytes 3276800 | tf_op jit(solution)/shard_map/all_to_all | solution.py:296
  37.5 6.2 %collective-permute-start = (f32[56,128]{1,0:T(8,128)S(1)}, f32[56,128]{1,0:T(8,128)S(1)}, u32[]{:S(2)}, u32[]{:S(2)}) collective-permute-start(f32[56,128]{1,0:T(8,128)S(1)} %copy-done.3), channel_id=1, source_target_pairs={{0,1},{1,2},{2,3},{3,4},{4,5},{5,6},{6,7},{7,0},{8,9},{9,10},{10,1... | collective-permute-start | bytes 86024 | tf_op jit(solution)/shard_map/ppermute | solution.py:377
  43.7 7.3 %collective-permute-start.1 = (f32[112,128]{1,0:T(8,128)S(1)}, f32[112,128]{1,0:T(8,128)S(1)}, u32[]{:S(2)}, u32[]{:S(2)}) collective-permute-start(f32[112,128]{1,0:T(8,128)S(1)} %pad_maximum_fusion.2), channel_id=1, source_target_pairs={{0,2},{1,3},{2,4},{3,5},{4,6},{5,7},{6,0},{7,1},{8,10},{9,11},{10,... | collective-permute-start | bytes 172040 | tf_op jit(solution)/shard_map/ppermute | solution.py:377
  51.0 9.6 %collective-permute-start.2 = (f32[224,128]{1,0:T(8,128)S(1)}, f32[224,128]{1,0:T(8,128)S(1)}, u32[]{:S(2)}, u32[]{:S(2)}) collective-permute-start(f32[224,128]{1,0:T(8,128)S(1)} %pad_maximum_fusion.1), channel_id=1, source_target_pairs={{0,4},{1,5},{2,6},{3,7},{4,0},{5,1},{6,2},{7,3},{8,12},{9,13},{10,... | collective-permute-start | bytes 344072 | tf_op jit(solution)/shard_map/ppermute | solution.py:377
  53.1 1.4 copy-start
  54.6 1.4 copy-start.1
  83.1 4.2 %collective-permute-start.3 = (f32[1600,128]{1,0:T(8,128)S(1)}, f32[1600,128]{1,0:T(8,128)S(1)}, u32[]{:S(2)}, u32[]{:S(2)}) collective-permute-start(f32[1600,128]{1,0:T(8,128)S(1)} %get-tuple-element.31), channel_id=1, source_target_pairs={{0,8},{8,0},{1,9},{9,1},{2,10},{10,2},{3,11},{11,3},{4,12},{12,4},... | collective-permute-start | bytes 2457608 | tf_op jit(solution)/shard_map/ppermute | solution.py:361
  86.2 25.9 %copy-start.6 = (s32[65]{0:T(128)S(1)}, s32[65]{0:T(128)}, u32[]{:S(2)}) copy-start(s32[65]{0:T(128)} %get-tuple-element.23.slots_ref) | copy-start | bytes 784
  87.4 57.9 %copy-start.2 = (f32[448,128]{1,0:T(8,128)S(1)}, f32[448,128]{1,0:T(8,128)}, u32[]{:S(2)}) copy-start(f32[448,128]{1,0:T(8,128)} %pad_maximum_fusion.d8_ref) | copy-start | bytes 688132
  194.5 4.2 %collective-permute-start.4 = (f32[1600,128]{1,0:T(8,128)S(1)}, f32[1600,128]{1,0:T(8,128)S(1)}, u32[]{:S(2)}, u32[]{:S(2)}) collective-permute-start(f32[1600,128]{1,0:T(8,128)S(1)} %get-tuple-element.37), channel_id=1, source_target_pairs={{0,8},{8,0},{1,9},{9,1},{2,10},{10,2},{3,11},{11,3},{4,12},{12,4},... | collective-permute-start | bytes 2457608 | tf_op jit(solution)/shard_map/ppermute | solution.py:361
  197.9 25.6 %copy-start.4 = (f32[50,128]{1,0:T(8,128)S(1)}, f32[50,128]{1,0:T(8,128)}, u32[]{:S(2)}) copy-start(f32[50,128]{1,0:T(8,128)} %get-tuple-element.39.v_ref) | copy-start | bytes 76804
